TPU v7x, 256 devices: a whole 4x4x8 slice. The times are simulated.
256 devices in a mesh: context: 4 (over y), expert: 64 (over x, z, core).
Axes of the slice: x: 4, y: 4, z: 8, core: 2. Of those that a mesh axis runs over, the one named last changes fastest.
Arguments:
- queries: bfloat16 [512, 24576], P(None, 'expert'), may hold values from -14 to 14
- key_lift: bfloat16 [128, 128, 512], P('expert'), may hold values from -0.5 to 0.5
- value_lift: bfloat16 [128, 512, 128], P('expert'), may hold values from -0.25 to 0.25
- page_pool: bfloat16 [16, 64, 576], P('context'), may hold values from -6 to 6
- fresh_latents: bfloat16 [64, 8, 576], P('context'), may hold values from -6 to 6
- page_table: int32 [64, 12], replicated, may hold values from 0 to 15, as said below
- context_lengths: int32 [64], replicated, may hold values from 705 to 768, as said below
- tree_parents: int32 [64, 8], replicated, may hold values from -1 to 6, as said below
- out_weight: bfloat16 [16384, 7168], P('expert', 'context'), may hold values from -0.5 to 0.5
- residual: bfloat16 [512, 7168], P('expert', 'context'), may hold values from -6 to 6
- norm_gain: float32 [7168], replicated, may hold values from 0.5 to 2
- expert_ids: int32 [512, 8], P('expert'), may hold values from 0 to 63, all different within a row; in each aligned block of 8 rows (0 to 7, 8 to 15, ...) at most 3 rows name the same one
- route_weights: float32 [512, 8], P('expert'), may hold values from 0.1 to 0.6
- gate_matrix: bfloat16 [64, 7168, 1024], P('expert', None, 'context'), may hold values from -0.0625 to 0.0625
- up_matrix: bfloat16 [64, 7168, 1024], P('expert', None, 'context'), may hold values from -0.0625 to 0.0625
- down_matrix: bfloat16 [64, 1024, 7168], P('expert', 'context'), may hold values from -0.1875 to 0.1875
Outputs:
- layer_out: bfloat16 [512, 7168], P('expert', 'context')
Inputs may be any that keep to these rules, and one draw needn't show every extreme that they name: `page_table`: the 12 pages of a leaf are distinct. `context_lengths`: entry k of a leaf's page table holds its context tokens k * 64 to k * 64 + 63; some leaf fills all 12 pages. `tree_parents`: token 0 of a leaf has parent -1; token t > 0 has a parent among tokens 0 to t - 1 of the same leaf. `expert_ids`: within each aligned block of 8 rows, no expert is named by more than 3 rows, a bound that some block reaches.
All inputs are finite; a program needn't handle non-finite values.
Results may differ from a plain program's by a relative error of at most 0.011.
Values may be sent and summed in bfloat16 or wider, within the bound.
No kernel may reach another device: no remote copies, remote signals or barrier semaphores. Data moves between devices by JAX's collectives and lax.ppermute only.
A program may use at most 64 MiB of HBM per device.

v0:
```python
import jax
import jax.numpy as jnp
from jax import lax
from jax.sharding import PartitionSpec as P

LAT = 512
ROPE = 64
QK = 128


NEGATIVE_FILL = -1e30
NORM_EPSILON = 1e-06


def ancestry(tree_parents):
    advance = tree_parents.shape[1]
    positions = jnp.arange(advance, dtype=jnp.int32)
    current = jnp.broadcast_to(positions[None, :], tree_parents.shape)
    linked = current[:, :, None] == positions[None, None, :]
    for repeat in range(advance - 1):
        climbed = jnp.take_along_axis(tree_parents, jnp.maximum(current, 0), axis=1)
        current = jnp.where(current >= 0, climbed, -1)
        linked = linked | (current[:, :, None] == positions[None, None, :])
    return linked


def page_limits(page_table, context_lengths, first_page, page_count, page_len):
    page_ids = first_page + jnp.arange(page_count, dtype=jnp.int32)
    matches = page_table[:, :, None] == page_ids[None, None, :]
    offsets = jnp.arange(page_table.shape[1], dtype=jnp.int32) * page_len
    remain = context_lengths[:, None] - offsets[None, :]
    return jnp.sum(jnp.where(matches, remain[:, :, None], 0), axis=1)


def context_mask(limits, page_len, advance):
    within = jnp.arange(page_len, dtype=jnp.int32)
    visible = within[None, None, :] < limits[:, :, None]
    visible = visible.reshape(limits.shape[0], -1)
    return jnp.repeat(visible, advance, axis=0)


def normalize(values, norm_gain):
    floats = values.astype(jnp.float32)
    inverse = lax.rsqrt(jnp.mean(floats * floats, axis=-1, keepdims=True) + NORM_EPSILON)
    return (floats * inverse * norm_gain).astype(jnp.bfloat16)


def absorbed_queries(queries, key_lift):
    head_count = key_lift.shape[0]
    shaped = queries.reshape(queries.shape[0], head_count, QK + ROPE)
    latent = jnp.einsum(
        "rhq,hql->rhl", shaped[:, :, :QK], key_lift, preferred_element_type=jnp.float32
    ).astype(jnp.bfloat16)
    return jnp.concatenate([latent, shaped[:, :, QK:]], axis=2)


def score_parts(joined_query, pool_keys, row_mask, fresh_keys, fresh_mask, row_start):
    score_scale = (QK + ROPE) ** (-0.5)
    flat_keys = pool_keys.reshape(-1, pool_keys.shape[-1])
    page_scores = (
        jnp.einsum("rhc,kc->rhk", joined_query, flat_keys, preferred_element_type=jnp.float32)
        * score_scale
    )
    page_scores = jnp.where(row_mask[:, None, :], page_scores, NEGATIVE_FILL)
    leaf_count, advance = (fresh_keys.shape[0], fresh_keys.shape[1])
    own_rows = lax.dynamic_slice_in_dim(joined_query, row_start, leaf_count * advance, 0)
    own_rows = own_rows.reshape(leaf_count, advance, joined_query.shape[1], joined_query.shape[2])
    fresh_scores = (
        jnp.einsum("lthc,lsc->lths", own_rows, fresh_keys, preferred_element_type=jnp.float32)
        * score_scale
    )
    fresh_scores = jnp.where(fresh_mask[:, :, None, :], fresh_scores, NEGATIVE_FILL)
    return (page_scores, fresh_scores)


def local_maximum(page_scores, fresh_scores, row_start):
    page_best = jnp.max(page_scores, axis=2)
    fresh_best = jnp.max(fresh_scores, axis=3).reshape(-1, page_scores.shape[1])
    current = lax.dynamic_slice_in_dim(page_best, row_start, fresh_best.shape[0], 0)
    return lax.dynamic_update_slice_in_dim(
        page_best, jnp.maximum(current, fresh_best), row_start, 0
    )


def weighted_sums(page_scores, fresh_scores, row_max, pool_keys, fresh_keys, row_start):
    page_exp = jnp.exp(page_scores - row_max[:, :, None])
    flat_keys = pool_keys.reshape(-1, pool_keys.shape[-1])[:, :LAT]
    totals = jnp.sum(page_exp, axis=2)
    numerators = jnp.einsum(
        "rhk,kl->rhl", page_exp.astype(jnp.bfloat16), flat_keys, preferred_element_type=jnp.float32
    )
    leaf_count, advance = (fresh_keys.shape[0], fresh_keys.shape[1])
    count_rows = leaf_count * advance
    head_count = row_max.shape[1]
    own_max = lax.dynamic_slice_in_dim(row_max, row_start, count_rows, 0).reshape(
        leaf_count, advance, head_count
    )
    fresh_exp = jnp.exp(fresh_scores - own_max[:, :, :, None])
    fresh_totals = jnp.sum(fresh_exp, axis=3).reshape(count_rows, head_count)
    fresh_numer = jnp.einsum(
        "lths,lsc->lthc",
        fresh_exp.astype(jnp.bfloat16),
        fresh_keys[:, :, :LAT],
        preferred_element_type=jnp.float32,
    )
    fresh_numer = fresh_numer.reshape(count_rows, head_count, LAT)
    totals = lax.dynamic_update_slice_in_dim(
        totals,
        lax.dynamic_slice_in_dim(totals, row_start, count_rows, 0) + fresh_totals,
        row_start,
        0,
    )
    numerators = lax.dynamic_update_slice_in_dim(
        numerators,
        lax.dynamic_slice_in_dim(numerators, row_start, count_rows, 0) + fresh_numer,
        row_start,
        0,
    )
    return (totals, numerators)


def project_values(numerators, lift_float):
    return jnp.einsum("rhl,hlv->rhv", numerators, lift_float, precision=lax.Precision.HIGHEST)


def local(
    queries,
    key_lift,
    value_lift,
    page_pool,
    fresh_latents,
    page_table,
    context_lengths,
    tree_parents,
    out_weight,
    residual,
    norm_gain,
    expert_ids,
    route_weights,
    gate_matrix,
    up_matrix,
    down_matrix,
):
    row_total = queries.shape[0]
    advance = tree_parents.shape[1]
    page_len = page_pool.shape[1]
    joined_query = absorbed_queries(queries, key_lift)
    lift_float = value_lift.astype(jnp.float32)
    context_index = lax.axis_index("context")
    leaf_count = fresh_latents.shape[0]
    leaf_start = context_index * leaf_count
    row_start = leaf_start * advance
    own_parents = lax.dynamic_slice_in_dim(tree_parents, leaf_start, leaf_count, 0)
    fresh_mask = ancestry(own_parents)
    limits = page_limits(
        page_table,
        context_lengths,
        context_index * page_pool.shape[0],
        page_pool.shape[0],
        page_len,
    )
    row_mask = context_mask(limits, page_len, advance)
    page_scores, fresh_scores = score_parts(
        joined_query, page_pool, row_mask, fresh_latents, fresh_mask, row_start
    )
    row_max = lax.pmax(local_maximum(page_scores, fresh_scores, row_start), "context")
    totals, numerators = weighted_sums(
        page_scores, fresh_scores, row_max, page_pool, fresh_latents, row_start
    )
    totals, numerators = lax.psum((totals, numerators), "context")
    projected = project_values(numerators, lift_float)
    attention = (projected / totals[:, :, None]).astype(jnp.bfloat16).reshape(row_total, -1)
    row_dev = residual.shape[0]
    head_mix = lax.psum_scatter(
        jnp.dot(attention, out_weight, preferred_element_type=jnp.float32),
        "expert",
        scatter_dimension=0,
        tiled=True,
    )
    hidden_state = (residual.astype(jnp.float32) + head_mix).astype(jnp.bfloat16)
    expert_total = lax.axis_size("expert") * gate_matrix.shape[0]
    top_count = expert_ids.shape[1]
    capacity = max(3, (row_dev * top_count + expert_total - 1) // expert_total)
    flat_ids = expert_ids.reshape(-1)
    onehot = (flat_ids[:, None] == jnp.arange(expert_total, dtype=jnp.int32)[None, :]).astype(
        jnp.int32
    )
    earlier = jnp.cumsum(onehot, axis=0) - onehot
    slot_index = jnp.sum(earlier * onehot, axis=1)
    target = flat_ids * capacity + slot_index
    slot_ids = jnp.arange(expert_total * capacity, dtype=jnp.int32)
    slot_match = target.reshape(row_dev, top_count)[None, :, :] == slot_ids[:, None, None]
    dispatch = jnp.any(slot_match, axis=2).astype(jnp.bfloat16)
    full_rows = lax.all_gather(hidden_state, "context", axis=1, tiled=True)
    normed = normalize(full_rows, norm_gain)
    outgoing = jnp.dot(dispatch, normed, preferred_element_type=jnp.float32).astype(jnp.bfloat16)
    outgoing = outgoing.reshape(expert_total, capacity, -1)
    inputs = lax.all_to_all(outgoing, "expert", split_axis=0, concat_axis=0, tiled=True)
    sources, slots_here, feature_count = inputs.shape
    flat_rows = inputs.reshape(-1, feature_count)
    gate_part = jnp.dot(flat_rows, gate_matrix[0], preferred_element_type=jnp.float32)
    up_part = jnp.dot(flat_rows, up_matrix[0], preferred_element_type=jnp.float32)
    active = (jax.nn.silu(gate_part) * up_part).astype(jnp.bfloat16)
    partial_out = jnp.dot(active, down_matrix[0], preferred_element_type=jnp.float32)
    partial_out = partial_out.reshape(sources, slots_here, feature_count)
    summed = lax.psum_scatter(
        partial_out.astype(jnp.bfloat16), "context", scatter_dimension=2, tiled=True
    )
    returned = lax.all_to_all(summed, "expert", split_axis=0, concat_axis=0, tiled=True)
    slot_rows = returned.reshape(-1, returned.shape[2])
    picked = jnp.take(slot_rows, target, axis=0).reshape(row_dev, top_count, -1).astype(jnp.float32)
    mixed_sum = jnp.sum(route_weights[:, :, None] * picked, axis=1)
    return (hidden_state.astype(jnp.float32) + mixed_sum).astype(jnp.bfloat16)


def solution(mesh):
    return jax.shard_map(
        local,
        mesh=mesh,
        in_specs=(
            P(None, "expert"),
            P("expert", None, None),
            P("expert", None, None),
            P("context", None, None),
            P("context", None, None),
            P(),
            P(),
            P(),
            P("expert", "context"),
            P("expert", "context"),
            P(),
            P("expert", None),
            P("expert", None),
            P("expert", None, "context"),
            P("expert", None, "context"),
            P("expert", "context", None),
        ),
        out_specs=P("expert", "context"),
        check_vma=False,
    )
```

profile of v0, /device:TPU:24, one launch (start us, length us, event | category | flops | bytes accessed | tf_op | source)
XLA Modules:
  0.0 461.7 jit_solution(9158482918192379249)
XLA Ops:
  6.8 0.8 constant_dynamic-slice_fusion.2
  7.6 1.0 gather_fusion.1
  9.0 1.0 gather_fusion.2
  10.4 1.0 gather_fusion.3
  11.9 1.0 gather_fusion.4
  13.3 1.0 gather_fusion.5
  14.7 1.0 gather_fusion.6
  16.2 1.0 gather_fusion.7
  17.5 0.2 copy.123
  17.8 0.5 fusion.5
  18.3 0.2 copy.148
  18.6 1.0 fusion.57
  20.0 0.1 lt.64
  20.1 0.1 lt.65
  20.5 0.2 copy.122
  20.7 1.6 fusion.56
  22.3 8.4 %pmax.7 = f32[512,2]{0,1:T(2,128)S(1)} all-reduce(f32[512,2]{0,1:T(2,128)S(1)} %constant_dynamic-update-slice_fusion.1), channel_id=1, replica_groups=mesh['context'=4,'expert'=64] {'context'}, use_global_device_ids=true, to_apply=%region_3.5 | all-reduce | flops 1024 | bytes 8192 | tf_op jit(solution)/shard_map/pmax | solution.py:166
  30.9 1.7 fusion.21
  32.7 0.3 fusion.9
  33.0 1.3 copy-done.2
  34.4 1.4 fusion.19
  35.8 9.1 %psum.15 = f32[512,2]{0,1:T(2,128)S(1)} all-reduce(f32[512,2]{0,1:T(2,128)S(1)} %constant_dynamic-update-slice_fusion), channel_id=1, replica_groups=mesh['context'=4,'expert'=64] {'context'}, use_global_device_ids=true, to_apply=%region_7.9 | all-reduce | flops 1024 | bytes 8192 | tf_op jit(solution)/shard_map/psum | solution.py:170
  44.9 54.1 %all-reduce.2.cloned.1.call-done = f32[512,2,512]{2,0,1:T(8,128)} async-done(((f32[512,2,512]{2,0,1:T(8,128)}), f32[512,2,512]{2,0,1:T(8,128)}) %all-reduce.2.cloned.1.call-update) | async-done | bytes 2097168 | tf_op jit(solution)/shard_map/psum | solution.py:170
  99.0 2.9 fusion.10
  101.9 2.5 fusion.58
  104.5 0.6 copy-done.8
  105.3 0.2 select_reduce_fusion
  105.6 0.1 fusion.47
  105.7 144.2 %reduce-scatter.3.cloned.1.call-done = f32[8,1792]{1,0:T(8,128)} async-done(((f32[512,1792]{1,0:T(8,128)}), f32[8,1792]{1,0:T(8,128)}) %reduce-scatter.3.cloned.1.call-update) | async-done | bytes 57360 | tf_op jit(solution)/shard_map/reduce_scatter | solution.py:174
  249.9 0.8 add_convert_fusion.1
  250.7 11.9 %all_gather.3 = bf16[8,7168]{1,0:T(8,128)(2,1)S(1)} all-gather(bf16[8,1792]{1,0:T(8,128)(2,1)S(1)} %add_convert_fusion.1), channel_id=1, replica_groups=mesh['context'=4,'expert'=64] {'context'}, dimensions={1}, use_global_device_ids=true | all-gather | bytes 143360 | tf_op jit(solution)/shard_map/all_gather | solution.py:194
  262.6 0.2 fusion.27
  262.8 2.5 convolution_convert_fusion.1
  265.3 6.7 %reshape.197 = bf16[64,3,7168]{2,1,0:T(4,128)(2,1)} reshape(bf16[192,7168]{1,0:T(8,128)(2,1)} %convolution_convert_fusion.1) | data formatting | bytes 5505024 | tf_op jit(solution)/shard_map/reshape | solution.py:197
  272.0 91.9 %all_to_all.10 = bf16[64,3,7168]{2,1,0:T(4,128)(2,1)} all-to-all(bf16[64,3,7168]{2,1,0:T(4,128)(2,1)} %reshape.197), channel_id=1, replica_groups=mesh['context'=4,'expert'=64] {'expert'}, dimensions={0} | all-to-all | bytes 5505024 | tf_op jit(solution)/shard_map/all_to_all | solution.py:198
  363.9 7.1 %reshape.198 = bf16[192,7168]{1,0:T(8,128)(2,1)} reshape(bf16[64,3,7168]{2,1,0:T(4,128)(2,1)} %all_to_all.10) | data formatting | bytes 5505024 | tf_op jit(solution)/shard_map/reshape | solution.py:200
  371.0 3.9 fusion.3
  374.9 0.8 copy-done.14
  375.7 0.9 fusion.14
  376.7 4.5 convolution_convert_fusion
  381.2 32.9 %reduce-scatter.5.cloned.1.call-done = bf16[64,3,1792]{2,0,1:T(8,128)(2,1)} async-done(((bf16[64,3,7168]{2,0,1:T(8,128)(2,1)}), bf16[64,3,1792]{2,0,1:T(8,128)(2,1)}) %reduce-scatter.5.cloned.1.call-update) | async-done | bytes 688144 | tf_op jit(solution)/shard_map/reduce_scatter | solution.py:206
  414.1 2.6 copy.158
  416.8 10.6 %all-to-all-start.1 = ((bf16[64,3,1792]{2,1,0:T(4,128)(2,1)}), bf16[64,3,1792]{2,1,0:T(4,128)(2,1)S(1)}, u32[]{:S(2)}, u32[]{:S(2)}) async-start(bf16[64,3,1792]{2,1,0:T(4,128)(2,1)} %copy.158), calls=%async_computation.3 | async-start | bytes 1835008 | tf_op jit(solution)/shard_map/all_to_all | solution.py:209
  427.5 25.4 %all-to-all-done.1 = bf16[64,3,1792]{2,1,0:T(4,128)(2,1)S(1)} async-done(((bf16[64,3,1792]{2,1,0:T(4,128)(2,1)}), bf16[64,3,1792]{2,1,0:T(4,128)(2,1)S(1)}, u32[]{:S(2)}, u32[]{:S(2)}) %all-to-all-start.1) | async-done | bytes 688160 | tf_op jit(solution)/shard_map/all_to_all | solution.py:209
  452.9 0.6 reshape.199
  453.5 0.7 gather_fusion
  454.3 0.3 multiply_reduce_fusion
  454.6 0.6 add_convert_fusion
  (111 shorter events, 4.6 us)
Async XLA Ops:
  6.5 95.4 %copy-start = (bf16[256,1792]{1,0:T(8,128)(2,1)S(1)}, bf16[256,1792]{1,0:T(8,128)(2,1)}, u32[]{:S(2)}) copy-start(bf16[256,1792]{1,0:T(8,128)(2,1)} %param.26) | copy-start | bytes 2752516
  6.5 92.5 %all-reduce.2.cloned.1.call-start = ((), (), s32[]{:S(2)}) async-start(), calls=%async_computation.4 | async-start | bytes 4194304 | tf_op jit(solution)/shard_map/psum | solution.py:170
  16.2 1.4 copy-start.3
  16.2 1.6 copy-start.5
  17.2 1.4 copy-start.7
  17.5 2.2 copy-start.13
  17.5 2.3 copy-start.11
  17.8 2.9 copy-start.6
  32.7 66.3 %copy-start.4 = (bf16[2,512,128]{2,1,0:T(8,128)(2,1)S(1)}, bf16[2,512,128]{2,1,0:T(8,128)(2,1)}, u32[]{:S(2)}) copy-start(bf16[2,512,128]{2,1,0:T(8,128)(2,1)} %param.20) | copy-start | bytes 786436
  33.0 1.3 copy-start.2
  34.3 215.6 %reduce-scatter.3.cloned.1.call-start = ((), (), s32[]{:S(2)}) async-start(), calls=%async_computation.5 | async-start | bytes 3727360 | tf_op jit(solution)/shard_map/reduce_scatter | solution.py:174
  104.4 0.7 copy-start.8
  104.4 145.5 %copy-start.10 = (bf16[8,1792]{1,0:T(8,128)(2,1)S(1)}, bf16[8,1792]{1,0:T(8,128)(2,1)}, u32[]{:S(2)}) copy-start(bf16[8,1792]{1,0:T(8,128)(2,1)} %param.27) | copy-start | bytes 86020
  104.4 158.4 %copy-start.9 = (f32[7168]{0:T(1024)S(1)}, f32[7168]{0:T(1024)}, u32[]{:S(2)}) copy-start(f32[7168]{0:T(1024)} %param.28) | copy-start | bytes 86020
  104.4 309.7 %reduce-scatter.5.cloned.1.call-start = ((), (), s32[]{:S(2)}) async-start(), calls=%async_computation.6 | async-start | bytes 3440640 | tf_op jit(solution)/shard_map/reduce_scatter | solution.py:206
  371.0 3.9 copy-start.1
  371.0 4.8 %copy-start.14 = (bf16[1,7168,256]{2,1,0:T(8,128)(2,1)S(1)}, bf16[1,7168,256]{2,1,0:T(8,128)(2,1)}, u32[]{:S(2)}) copy-start(bf16[1,7168,256]{2,1,0:T(8,128)(2,1)} %param.32) | copy-start | bytes 11010052
  416.8 37.5 %copy-start.12 = (f32[8,8]{1,0:T(8,128)S(1)}, f32[8,8]{1,0:T(8,128)}, u32[]{:S(2)}) copy-start(f32[8,8]{1,0:T(8,128)} %param.30) | copy-start | bytes 772
  416.8 36.1 %all-to-all-start.1 = ((bf16[64,3,1792]{2,1,0:T(4,128)(2,1)}), bf16[64,3,1792]{2,1,0:T(4,128)(2,1)S(1)}, u32[]{:S(2)}, u32[]{:S(2)}) async-start(bf16[64,3,1792]{2,1,0:T(4,128)(2,1)} %copy.158), calls=%async_computation.3 | async-start | bytes 1835008 | tf_op jit(solution)/shard_map/all_to_all | solution.py:209
Sparse Core Ops, SparseCore 0:
  34.4 64.5 all-reduce.1
  104.5 145.2 reduce-scatter.2
  381.3 32.7 reduce-scatter.4
where the time goes:
time: 466 us; the launch traced here: 462 us
  waiting for transfers between devices  257 us (55%)
  blocking collectives  121 us (26%)
  local copies, waits for them, and re-layouts  32.8 us (7%)
  matrix products  22.2 us (5%)
  between operations  13.6 us (3%)
  starting transfers between devices  10.7 us (2%)
    reduce_scatter x1, waiting for transfers between devices, local(): lax.psum_scatter(jnp.dot(attention, out_weight, preferred_element_type=jn...  144 us
    all_to_all x1, blocking collectives, local(): lax.all_to_all(outgoing, 'expert', split_axis=0, concat_axis=0, tiled=True)  91.9 us
    psum x1, waiting for transfers between devices, local(): totals, numerators = lax.psum((totals, numerators), 'context')  54.1 us
    reduce_scatter x1, waiting for transfers between devices, local(): lax.psum_scatter(partial_out.astype(jnp.bfloat16), 'context', scatter_dim...  32.9 us
    all_to_all x1, waiting for transfers between devices, local(): lax.all_to_all(summed, 'expert', split_axis=0, concat_axis=0, tiled=True)  25.4 us
    all_gather x1, blocking collectives, local(): full_rows = lax.all_gather(hidden_state, 'context', axis=1, tiled=True)  11.9 us
    all_to_all x1, starting transfers between devices, local(): lax.all_to_all(summed, 'expert', split_axis=0, concat_axis=0, tiled=True)  10.6 us
  transfers between devices with their start and end apart: 4, of which 4 were waited for; matrix products, arithmetic and copies ran while one was open for 0% of the time, Pallas kernels for 0%

commit v1 on v0

v1 whole, which is shorter than its diff:
```python
import jax
import jax.numpy as jnp
from jax import lax
from jax.experimental import pallas as pl
from jax.experimental.pallas import tpu as pltpu
from jax.sharding import Mesh, PartitionSpec as P

LAT = 512
ROPE = 64
QK = 128
VD = 128
PAGE = 64
LOOK = 8
CAP = 3
NEGATIVE_FILL = -1e30
NORM_EPSILON = 1e-06
F32 = jnp.float32
BF16 = jnp.bfloat16
SMEM = pl.BlockSpec(memory_space=pltpu.SMEM)
VMEM = pl.BlockSpec(memory_space=pltpu.VMEM)
TAIL = 128

CONTEXT = "context"
ROW_AXES = ("x", "z")
CORE = "core"
EXPERT = ("x", "z", "core")


def iota(shape, axis):
    return lax.broadcasted_iota(jnp.int32, shape, axis)


def dot_nn(a, b):
    return jnp.dot(a, b, preferred_element_type=F32)


def dot_nt(a, b):
    return lax.dot_general(a, b, (((1,), (1,)), ((), ())), preferred_element_type=F32)


def dot_tn(a, b):
    return lax.dot_general(a, b, (((0,), (0,)), ((), ())), preferred_element_type=F32)


def split3(value):
    high = value.astype(BF16)
    rest = value - high.astype(F32)
    middle = rest.astype(BF16)
    low = (rest - middle.astype(F32)).astype(BF16)
    return high, middle, low


def attention_kernel(
    place, q_ref, kl_ref, vl_ref, pool_ref, fresh_ref, table_ref, length_ref, parent_ref, *outs
):
    context = place[0]
    pool_rows = pool_ref.shape[0]
    fresh_rows = fresh_ref.shape[0]
    rows = q_ref.shape[0]
    leaves, table_len = table_ref.shape
    pages = pool_rows // PAGE
    lengths = jnp.sum(
        jnp.where(
            iota((leaves, leaves), 0) == iota((leaves, leaves), 1),
            length_ref[...].astype(F32),
            0.0,
        ),
        axis=1,
        keepdims=True,
    )
    remain = lengths - (iota((leaves, table_len), 1) * PAGE).astype(F32)
    remain = jnp.clip(remain, 0.0, float(PAGE))
    table = table_ref[...]
    lane = iota((leaves, 128), 1)
    limits = jnp.zeros((leaves, 128), F32)
    for page in range(pages):
        seen = jnp.sum(
            jnp.where(table == context * pages + page, remain, 0.0), axis=1, keepdims=True
        )
        limits = jnp.where(lane == page, seen, limits)
    spread = (iota((leaves, rows), 0) == iota((leaves, rows), 1) // LOOK).astype(F32).astype(BF16)
    row_limits = dot_nn(limits.T.astype(BF16), spread)
    page_limit = jnp.concatenate(
        [jnp.broadcast_to(row_limits[p : p + 1, :], (PAGE, rows)) for p in range(pages)], axis=0
    )
    within = jnp.bitwise_and(iota((pool_rows, rows), 0), PAGE - 1).astype(F32)
    page_mask = jnp.where(within < page_limit, 1.0, 0.0)
    own_leaves = fresh_rows // LOOK
    pick_leaf = (
        (iota((fresh_rows, leaves), 1) == context * own_leaves + iota((fresh_rows, leaves), 0) // LOOK)
        .astype(F32)
        .astype(BF16)
    )
    parents = dot_nn(pick_leaf, parent_ref[...].astype(F32).astype(BF16))
    token = jnp.bitwise_and(iota((fresh_rows, LOOK), 0), LOOK - 1)
    parent = jnp.sum(
        jnp.where(iota((fresh_rows, LOOK), 1) == token, parents, 0.0), axis=1, keepdims=True
    )
    square = (fresh_rows, fresh_rows)
    first = (iota(square, 0) // LOOK) * LOOK
    step = (iota(square, 1) - first).astype(F32)
    linked = jnp.where((step == parent) & (parent >= 0.0), 1.0, 0.0)
    linked = jnp.where(iota(square, 0) == iota(square, 1), 1.0, linked)
    for repeat in range(3):
        half = linked.astype(BF16)
        linked = jnp.where(dot_nn(half, half) > 0.5, 1.0, 0.0)
    fresh_mask = jnp.concatenate([linked.T] * (rows // fresh_rows), axis=1)
    here = iota((fresh_rows, rows), 1) // fresh_rows == context
    fresh_mask = jnp.where(here, fresh_mask, 0.0)
    mask = jnp.concatenate([page_mask, fresh_mask], axis=0) > 0.5

    keys = jnp.concatenate([pool_ref[...], fresh_ref[...]], axis=0)
    latents = keys[:, :LAT]
    turned = keys[:, LAT:]
    scale = (QK + ROPE) ** (-0.5)
    for head, out in enumerate(outs):
        start = head * (QK + ROPE)
        plain = q_ref[:, start : start + QK]
        rotary = q_ref[:, start + QK : start + QK + ROPE]
        lifted = dot_nn(plain, kl_ref[head]).astype(BF16)
        scores = (dot_nt(latents, lifted) + dot_nt(turned, rotary)) * scale
        scores = jnp.where(mask, scores, NEGATIVE_FILL)
        best = jnp.max(scores, axis=0, keepdims=True)
        weights = jnp.exp(scores - best)
        total = jnp.sum(weights, axis=0, keepdims=True)
        values = dot_nn(latents, vl_ref[head]).T.astype(BF16)
        mixed = dot_nn(values, weights.astype(BF16)) / total
        out[:VD, :] = mixed.astype(BF16)
        high, middle, low = split3(best + jnp.log(total))
        line = iota((16, rows), 0)
        extra = jnp.where(
            line == 0,
            high.astype(F32),
            jnp.where(line == 1, middle.astype(F32), jnp.where(line == 2, low.astype(F32), 0.0)),
        )
        out[VD:, :] = extra.astype(BF16)


def merge_kernel(place, *refs):
    core = place[2]
    parts, (weight_ref, send_ref, keep_ref, scratch) = refs[:8], refs[8:]
    heads = []
    for head in range(2):
        own = parts[4 * head : 4 * head + 4]
        logs = []
        for part in own:
            extra = part[VD:, :].astype(F32)
            logs.append(extra[0:1, :] + extra[1:2, :] + extra[2:3, :])
        best = jnp.maximum(jnp.maximum(logs[0], logs[1]), jnp.maximum(logs[2], logs[3]))
        shares = [jnp.exp(log - best) for log in logs]
        inverse = 1.0 / (shares[0] + shares[1] + shares[2] + shares[3])
        mixed = 0.0
        for part, share in zip(own, shares):
            mixed = mixed + part[:VD, :].astype(F32) * (share * inverse)
        heads.append(mixed)
    attention = jnp.concatenate(heads, axis=0).T.astype(BF16)
    scratch[...] = dot_nn(attention, weight_ref[...]).reshape(scratch.shape)
    send_ref[...] = scratch[:, 1 - core].reshape(send_ref.shape).astype(BF16)
    keep_ref[...] = scratch[:, core].reshape(keep_ref.shape)


def add_kernel(keep_ref, got_ref, out_ref):
    total = keep_ref[...] + got_ref[...].astype(F32)
    out_ref[...] = total.astype(BF16).reshape(out_ref.shape)


def hidden_kernel(parts_ref, residual_ref, ids_ref, weights_ref, hidden_ref, payload_ref):
    total = residual_ref[...].astype(F32)
    mixed = parts_ref[0].astype(F32)
    for index in range(1, parts_ref.shape[0]):
        mixed = mixed + parts_ref[index].astype(F32)
    hidden = (total + mixed).astype(BF16)
    hidden_ref[...] = hidden
    floats = hidden.astype(F32)
    squares = jnp.sum(floats * floats, axis=1, keepdims=True)
    top = ids_ref.shape[1]
    row, lane = iota((top, TAIL), 0), iota((top, TAIL), 1)
    tail = dot_nn(
        ids_ref[...].astype(F32).astype(BF16), jnp.where(lane == row, 1.0, 0.0).astype(BF16)
    )
    for index, piece in enumerate(split3(weights_ref[...])):
        where = lane == row + (index + 1) * top
        tail = tail + dot_nn(piece, jnp.where(where, 1.0, 0.0).astype(BF16))
    lane = iota((hidden.shape[0], TAIL), 1)
    for index, piece in enumerate(split3(squares)):
        tail = jnp.where(lane == 4 * top + index, piece.astype(F32), tail)
    tail = tail.astype(BF16)
    width = hidden.shape[1]
    for index in range(payload_ref.shape[0]):
        payload_ref[index, :, :width] = hidden
        payload_ref[index, :, width:] = tail


def select_kernel(place, own_ref, other_ref, low_ref, high_ref, pick_ref):
    expert = place[1].astype(F32)
    half = own_ref.shape[0]
    rows = 2 * half
    slots = pick_ref.shape[1]
    width = own_ref.shape[1] - TAIL
    tails = jnp.concatenate([own_ref[:, width:], other_ref[:, width:]], axis=0).astype(F32)
    lane = iota((rows, TAIL), 1)
    named = jnp.max(
        jnp.where((tails == expert) & (lane < 8), 1.0, 0.0), axis=1, keepdims=True
    )
    ahead = (iota((rows, rows), 1) < iota((rows, rows), 0)) & (
        iota((rows, rows), 1) // 8 == iota((rows, rows), 0) // 8
    )
    before = dot_nn(
        jnp.where(ahead, 1.0, 0.0).astype(BF16),
        jnp.broadcast_to(named, (rows, TAIL)).astype(BF16),
    )[:, :1]
    place_of = (iota((rows, 1), 0) // 8 * CAP).astype(F32) + before
    slot = iota((rows, slots), 1).astype(F32)
    pick = jnp.where((slot == place_of) & (named > 0.5), 1.0, 0.0)
    pick_ref[...] = pick.astype(BF16)
    turned = pick.T.astype(BF16)
    chosen = dot_nn(turned[:, :half], own_ref[...]) + dot_nn(turned[:, half:], other_ref[...])
    chosen = chosen.astype(BF16)
    low_ref[...] = chosen[: slots // 2]
    high_ref[...] = chosen[slots // 2 :]


def expert_kernel(place, *refs):
    context, expert = place[0], place[1].astype(F32)
    parts = refs[:8]
    gain_ref, gate_ref, up_ref, down_ref, own_ref = refs[8:13]
    sends = refs[13:]
    slots = own_ref.shape[0]
    width = own_ref.shape[1]
    count = 4
    lane = iota((slots, TAIL), 1)
    squares = 0.0
    for index in range(count):
        tail = jnp.concatenate([parts[2 * index][:, width:], parts[2 * index + 1][:, width:]], axis=0)
        tail = tail.astype(F32)
        squares = squares + jnp.sum(
            jnp.where((lane >= 32) & (lane < 35), tail, 0.0), axis=1, keepdims=True
        )
        if index == 0:
            shares = (
                pltpu.roll(tail, TAIL - 8, 1)
                + pltpu.roll(tail, TAIL - 16, 1)
                + pltpu.roll(tail, TAIL - 24, 1)
            )
            share = jnp.sum(
                jnp.where((tail == expert) & (lane < 8), shares, 0.0), axis=1, keepdims=True
            )
    inverse = lax.rsqrt(squares * (1.0 / (count * width)) + NORM_EPSILON)
    gate_part = jnp.zeros((slots, gate_ref.shape[1]), F32)
    up_part = gate_part
    for index in range(count):
        source = lax.rem(context + (count - index), count)
        rows = jnp.concatenate(
            [parts[2 * index][:, :width], parts[2 * index + 1][:, :width]], axis=0
        )
        normed = (rows.astype(F32) * inverse * gain_ref[source]).astype(BF16)
        at = pl.ds(pl.multiple_of(source * width, width), width)
        gate_part = gate_part + dot_nn(normed, gate_ref[at, :])
        up_part = up_part + dot_nn(normed, up_ref[at, :])
    active = (gate_part / (1.0 + jnp.exp(-gate_part)) * up_part).astype(BF16)
    for index in (2, 1, 3, 0):
        target = lax.rem(context + index, count)
        at = pl.ds(pl.multiple_of(target * width, 128), width)
        made = dot_nn(active, down_ref[:, at]) * share
        if index == 0:
            own_ref[...] = made
        else:
            made = made.astype(BF16)
            sends[2 * index - 2][...] = made[: slots // 2]
            sends[2 * index - 1][...] = made[slots // 2 :]


def spread_kernel(own_ref, low1, high1, low3, high3, pick_ref, send_ref, keep_ref):
    slots = own_ref.shape[0]
    half = slots // 2
    low = own_ref[:half] + low1[...].astype(F32) + low3[...].astype(F32)
    high = own_ref[half:] + high1[...].astype(F32) + high3[...].astype(F32)
    total = jnp.concatenate([low, high], axis=0).astype(BF16)
    rows = keep_ref.shape[0]
    keep_ref[...] = dot_nn(pick_ref[:rows, :], total)
    send_ref[...] = dot_nn(pick_ref[rows:, :], total).astype(BF16)


def call(kernel, outs, inputs, scalars=0, scratch=()):
    return pl.pallas_call(
        kernel,
        out_shape=tuple(jax.ShapeDtypeStruct(shape, dtype) for shape, dtype in outs),
        in_specs=[SMEM] * scalars + [VMEM] * (len(inputs) - scalars),
        out_specs=tuple(VMEM for _ in outs),
        scratch_shapes=list(scratch),
        name=kernel.__name__,
    )(*inputs)


def shift(value, axis, count, step):
    return lax.ppermute(value, axis, [(i, (i + step) % count) for i in range(count)])


def local(
    queries,
    key_lift,
    value_lift,
    page_pool,
    fresh_latents,
    page_table,
    context_lengths,
    tree_parents,
    out_weight,
    residual,
    norm_gain,
    expert_ids,
    route_weights,
    gate_matrix,
    up_matrix,
    down_matrix,
):
    rows = queries.shape[0]
    row_dev, width = residual.shape
    ring = lax.axis_size(CONTEXT)
    chips = lax.axis_size(ROW_AXES)
    half = rows // 2
    slots = rows // row_dev * CAP
    context = lax.axis_index(CONTEXT)
    expert = lax.axis_index(EXPERT)
    core = lax.axis_index(CORE)
    number = jnp.arange(4, dtype=jnp.int32)
    place = jnp.where(number == 0, context, jnp.where(number == 1, expert, core)).astype(jnp.int32)

    low, high = call(
        attention_kernel,
        [((VD + 16, rows), BF16)] * 2,
        [
            place,
            queries,
            key_lift,
            value_lift,
            page_pool.reshape(-1, page_pool.shape[-1]),
            fresh_latents.reshape(-1, fresh_latents.shape[-1]),
            page_table,
            context_lengths.reshape(1, -1),
            tree_parents,
        ],
        scalars=1,
    )

    def around(low, high):
        low1, high1 = shift(low, CONTEXT, ring, 1), shift(high, CONTEXT, ring, 1)
        low3, high3 = shift(low, CONTEXT, ring, -1), shift(high, CONTEXT, ring, -1)
        low2, high2 = shift(low1, CONTEXT, ring, 1), shift(high3, CONTEXT, ring, -1)
        return (low, low1, low2, low3), (high, high1, high2, high3)

    lows, highs = around(low, high)
    send, keep = call(
        merge_kernel,
        [((half, width), BF16), ((half, width), F32)],
        [place, *lows, *highs, out_weight],
        scalars=1,
        scratch=[pltpu.VMEM((chips, 2, row_dev, width), F32)],
    )

    def return_rows(send, keep):
        got = shift(send, CORE, 2, 1)
        (summed,) = call(add_kernel, [((chips, row_dev, width), BF16)], [keep, got])
        return lax.all_to_all(summed, ROW_AXES, 0, 0, tiled=True)

    mixed = return_rows(send, keep)
    hidden, payload = call(
        hidden_kernel,
        [((row_dev, width), BF16), ((chips, row_dev, width + TAIL), BF16)],
        [mixed, residual, expert_ids, route_weights],
    )
    own = lax.all_to_all(payload, ROW_AXES, 0, 0, tiled=True).reshape(half, width + TAIL)
    other = shift(own, CORE, 2, 1)
    low, high, pick = call(
        select_kernel,
        [((slots // 2, width + TAIL), BF16)] * 2 + [((rows, slots), BF16)],
        [place, own, other],
        scalars=1,
    )
    lows, highs = around(low, high)
    parts = [part for pair in zip(lows, highs) for part in pair]
    made, low1, high1, low2, high2, low3, high3 = call(
        expert_kernel,
        [((slots, width), F32)] + [((slots // 2, width), BF16)] * 6,
        [
            place,
            *parts,
            norm_gain.reshape(ring, 1, width),
            gate_matrix[0],
            up_matrix[0],
            down_matrix[0],
        ],
        scalars=1,
    )
    passed_low = shift(low2, CONTEXT, ring, 1)
    passed_high = shift(high2, CONTEXT, ring, -1)
    got_high1 = shift(high1, CONTEXT, ring, 1)
    got_low3 = shift(low3, CONTEXT, ring, -1)
    got_low1 = shift((low1.astype(F32) + passed_low.astype(F32)).astype(BF16), CONTEXT, ring, 1)
    got_high3 = shift((high3.astype(F32) + passed_high.astype(F32)).astype(BF16), CONTEXT, ring, -1)
    send, keep = call(
        spread_kernel,
        [((half, width), BF16), ((half, width), F32)],
        [made, got_low1, got_high1, got_low3, got_high3, pick],
    )
    returned = return_rows(send, keep)
    total = jnp.sum(returned.astype(F32), axis=0)
    return (hidden.astype(F32) + total).astype(BF16)


def solution(mesh):
    fine = Mesh(mesh.devices.reshape(4, 4, 8, 2), (CONTEXT, "x", "z", CORE))
    return jax.shard_map(
        local,
        mesh=fine,
        in_specs=(
            P(None, EXPERT),
            P(EXPERT, None, None),
            P(EXPERT, None, None),
            P(CONTEXT, None, None),
            P(CONTEXT, None, None),
            P(),
            P(),
            P(),
            P(EXPERT, CONTEXT),
            P(EXPERT, CONTEXT),
            P(),
            P(EXPERT, None),
            P(EXPERT, None),
            P(EXPERT, None, CONTEXT),
            P(EXPERT, None, CONTEXT),
            P(EXPERT, CONTEXT, None),
        ),
        out_specs=P(EXPERT, CONTEXT),
        check_vma=False,
    )
```

time: 466 us -> 224 us (0.48)
  waiting for transfers between devices: 257 us -> 57 us
  Pallas kernels: 0 us -> 33.3 us
  local copies, waits for them, and re-layouts: 32.8 us -> 7.73 us
  matrix products: 22.2 us -> 0 us
  blocking collectives: 121 us -> 100 us
  between operations: 13.6 us -> 0.12 us
  starting transfers between devices: 10.7 us -> 20.8 us
    reduce_scatter x2 -> x0, waiting for transfers between devices: 177 us -> none  [the longest x1 144 us: local(): lax.psum_scatter(jnp.dot(attention, out_weight, preferred_element_type=jn...]
    ppermute x0 -> x21, waiting for transfers between devices: none -> 57 us  [shift(): lax.ppermute(value, axis, [(i, (i + step) % count) for i in range(count)])]
    psum x1 -> x0, waiting for transfers between devices: 54.1 us -> none  [local(): totals, numerators = lax.psum((totals, numerators), 'context')]
    pallas_call x0 -> x8, Pallas kernels: none -> 33.3 us  [call(): pl.pallas_call(kernel, out_shape=tuple((jax.ShapeDtypeStruct(shape, dtype...]
    all_to_all x1 -> x0, waiting for transfers between devices: 25.4 us -> none  [local(): lax.all_to_all(summed, 'expert', split_axis=0, concat_axis=0, tiled=True)]
    dot_general x11 -> x0, matrix products: 22.2 us -> none  [the longest x1 4.49 us: local(): jnp.dot(active, down_matrix[0], preferred_element_type=jnp.float32)]
    ppermute x0 -> x21, starting transfers between devices: none -> 20.8 us  [shift(): lax.ppermute(value, axis, [(i, (i + step) % count) for i in range(count)])]
    reshape x6 -> x0, local copies, waits for them, and re-layouts: 14.6 us -> none  [the longest x1 7.06 us: local(): flat_rows = inputs.reshape(-1, feature_count)]
  transfers between devices with their start and end apart: 4 -> 21, of which waited for: 4 -> 15; matrix products, arithmetic and copies ran while one was open for 0% -> 1% of each run, Pallas kernels for 0% -> 0%
where the time goes in v1:
time: 224 us; the launch traced here: 223 us
  blocking collectives  100 us (45%)
  waiting for transfers between devices  57 us (25%)
  Pallas kernels  33.3 us (15%)
  starting transfers between devices  20.8 us (9%)
  local copies, waits for them, and re-layouts  7.73 us (3%)
  other arithmetic  3.45 us (2%)
    all_to_all x2, blocking collectives, return_rows(): return lax.all_to_all(summed, ROW_AXES, 0, 0, tiled=True)  68.4 us
    ppermute x21, waiting for transfers between devices, shift(): lax.ppermute(value, axis, [(i, (i + step) % count) for i in range(count)])  57 us
    pallas_call x8, Pallas kernels, call(): pl.pallas_call(kernel, out_shape=tuple((jax.ShapeDtypeStruct(shape, dtype...  33.3 us
    all_to_all x1, blocking collectives, local(): lax.all_to_all(payload, ROW_AXES, 0, 0, tiled=True)  32 us
    ppermute x21, starting transfers between devices, shift(): lax.ppermute(value, axis, [(i, (i + step) % count) for i in range(count)])  20.8 us
    unnamed x44, local copies, waits for them, and re-layouts  7.73 us
  transfers between devices with their start and end apart: 21, of which 15 were waited for; matrix products, arithmetic and copies ran while one was open for 1% of the time, Pallas kernels for 0%

profile of v1, /device:TPU:24, one launch (start us, length us, event | category | flops | bytes accessed | tf_op | source)
XLA Modules:
  0.0 222.9 jit_solution(16069444050184583070)
XLA Ops:
  0.0 1.4 copy.17.table_ref
  1.4 1.4 copy.18.parent_ref
  3.3 4.7 %attention_kernel.1 = (bf16[144,512]{1,0:T(8,128)(2,1)}, bf16[144,512]{1,0:T(8,128)(2,1)}) custom-call(s32[4]{0:T(128)} %compare_select_fusion.1.place, bf16[512,384]{1,0:T(8,128)(2,1)} %q_ref.1, bf16[2,128,512]{2,1,0:T(8,128)(2,1)} %kl_ref.1, bf16[2,512,128]{2,1,0:T(8,128)(2,1)} %vl_ref.1, bf16[256,576]{1,0:T(8,128)(2,1)} %bitcast.13, ...), custom_call_target="tpu_custom_call" | custom-call | tf_op jit(solution)/shard_map/attention_kernel/pallas_call | solution.py:285
  8.1 1.9 collective-permute-start
  10.1 0.7 collective-permute-start.2
  10.8 2.5 %collective-permute-start.3 = (bf16[144,512]{1,0:T(8,128)(2,1)}, bf16[144,512]{1,0:T(8,128)(2,1)S(1)}, u32[]{:S(2)}, u32[]{:S(2)}) collective-permute-start(bf16[144,512]{1,0:T(8,128)(2,1)} %get-tuple-element.24.refs_4_), channel_id=1, source_target_pairs={{0,64},{64,128},{128,192},{192,0},{1,65},{65,129},{129,193},{193,1... | collective-permute-start | bytes 442376 | tf_op jit(solution)/shard_map/ppermute | solution.py:296
  13.3 1.7 collective-permute-done.refs_1_
  15.0 1.8 collective-permute-start.1
  17.0 2.3 %collective-permute-done.2.refs_3_ = bf16[144,512]{1,0:T(8,128)(2,1)S(1)} collective-permute-done((bf16[144,512]{1,0:T(8,128)(2,1)}, bf16[144,512]{1,0:T(8,128)(2,1)S(1)}, u32[]{:S(2)}, u32[]{:S(2)}) %collective-permute-start.2) | collective-permute-done | bytes 147488 | tf_op jit(solution)/shard_map/ppermute | solution.py:296
  19.3 0.8 collective-permute-done.1.refs_2_
  20.2 3.0 %collective-permute-done.5.refs_6_ = bf16[144,512]{1,0:T(8,128)(2,1)S(1)} collective-permute-done((bf16[144,512]{1,0:T(8,128)(2,1)S(1)}, bf16[144,512]{1,0:T(8,128)(2,1)S(1)}, u32[]{:S(2)}, u32[]{:S(2)}) %collective-permute-start.5) | collective-permute-done | bytes 147488 | tf_op jit(solution)/shard_map/ppermute | solution.py:296
  23.2 0.6 copy-done.19
  23.8 4.2 %merge_kernel.1 = (bf16[256,1792]{1,0:T(8,128)(2,1)}, f32[256,1792]{1,0:T(8,128)}) custom-call(s32[4]{0:T(128)} %compare_select_fusion.1.place, bf16[144,512]{1,0:T(8,128)(2,1)} %get-tuple-element.23.refs_0_, bf16[144,512]{1,0:T(8,128)(2,1)} %copy-done.14, bf16[144,512]{1,0:T(8,128)(2,1)} %copy-done.18, bf16[144,512]{1,0:T(8,128)(2,1)} %copy-done.16, ...), custom_call_target="tpu_custom_call" | custom-call | tf_op jit(solution)/shard_map/merge_kernel/pallas_call | solution.py:285
  28.0 2.7 %collective-permute-done.6.got_ref = bf16[256,1792]{1,0:T(8,128)(2,1)S(1)} collective-permute-done((bf16[256,1792]{1,0:T(8,128)(2,1)}, bf16[256,1792]{1,0:T(8,128)(2,1)S(1)}, u32[]{:S(2)}, u32[]{:S(2)}) %collective-permute-start.6) | collective-permute-done | bytes 917536 | tf_op jit(solution)/shard_map/ppermute | solution.py:296
  30.7 0.9 copy-done.2
  31.6 2.8 %add_kernel.2 = bf16[32,8,1792]{2,1,0:T(8,128)(2,1)} custom-call(f32[256,1792]{1,0:T(8,128)} %get-tuple-element.25.keep_ref, bf16[256,1792]{1,0:T(8,128)(2,1)} %copy-done.2), custom_call_target="tpu_custom_call" | custom-call | tf_op jit(solution)/shard_map/add_kernel/pallas_call | solution.py:285
  34.5 37.3 %all_to_all.15.parts_ref = bf16[32,8,1792]{2,1,0:T(8,128)(2,1)} all-to-all(bf16[32,8,1792]{2,1,0:T(8,128)(2,1)} %add_kernel.2), channel_id=1, replica_groups=mesh['context'=4,'x'=4,'z'=8,'core'=2] {'x','z'}, dimensions={0} | all-to-all | bytes 1835008 | tf_op jit(solution)/shard_map/all_to_all | solution.py:364
  71.7 2.4 %hidden_kernel.1 = (bf16[8,1792]{1,0:T(8,128)(2,1)}, bf16[32,8,1920]{2,1,0:T(8,128)(2,1)}) custom-call(bf16[32,8,1792]{2,1,0:T(8,128)(2,1)} %all_to_all.15.parts_ref, bf16[8,1792]{1,0:T(8,128)(2,1)} %residual_ref.1, s32[8,8]{1,0:T(8,128)} %ids_ref.1, f32[8,8]{1,0:T(8,128)} %weights_ref.1), custom_call_target="tpu_custom_call" | custom-call | tf_op jit(solution)/shard_map/hidden_kernel/pallas_call | solution.py:285
  74.1 32.0 %all_to_all.16 = bf16[32,8,1920]{2,1,0:T(8,128)(2,1)S(1)} all-to-all(bf16[32,8,1920]{2,1,0:T(8,128)(2,1)} %get-tuple-element.28), channel_id=1, replica_groups=mesh['context'=4,'x'=4,'z'=8,'core'=2] {'x','z'}, dimensions={0} | all-to-all | bytes 1966080 | tf_op jit(solution)/shard_map/all_to_all | solution.py:372
  106.1 2.6 %collective-permute-done.7.other_ref = bf16[256,1920]{1,0:T(8,128)(2,1)S(1)} collective-permute-done((bf16[256,1920]{1,0:T(8,128)(2,1)S(1)}, bf16[256,1920]{1,0:T(8,128)(2,1)S(1)}, u32[]{:S(2)}, u32[]{:S(2)}) %collective-permute-start.7) | collective-permute-done | bytes 983072 | tf_op jit(solution)/shard_map/ppermute | solution.py:296
  108.7 1.0 copy-done.1
  109.6 3.6 %select_kernel.1 = (bf16[96,1920]{1,0:T(8,128)(2,1)}, bf16[96,1920]{1,0:T(8,128)(2,1)}, bf16[512,192]{1,0:T(8,128)(2,1)}) custom-call(s32[4]{0:T(128)} %compare_select_fusion.1.place, bf16[256,1920]{1,0:T(8,128)(2,1)} %bitcast.9, bf16[256,1920]{1,0:T(8,128)(2,1)} %copy-done.1), custom_call_target="tpu_custom_call" | custom-call | tf_op jit(solution)/shard_map/select_kernel/pallas_call | solution.py:285
  113.2 0.8 collective-permute-start.8
  114.0 1.2 collective-permute-start.11
  115.3 3.2 %collective-permute-start.9 = (bf16[96,1920]{1,0:T(8,128)(2,1)}, bf16[96,1920]{1,0:T(8,128)(2,1)S(1)}, u32[]{:S(2)}, u32[]{:S(2)}) collective-permute-start(bf16[96,1920]{1,0:T(8,128)(2,1)} %get-tuple-element.30.refs_1_), channel_id=1, source_target_pairs={{0,64},{64,128},{128,192},{192,0},{1,65},{65,129},{129,193},{193,1... | collective-permute-start | bytes 1105928 | tf_op jit(solution)/shard_map/ppermute | solution.py:296
  118.5 6.4 %collective-permute-done.8.refs_2_ = bf16[96,1920]{1,0:T(8,128)(2,1)S(1)} collective-permute-done((bf16[96,1920]{1,0:T(8,128)(2,1)}, bf16[96,1920]{1,0:T(8,128)(2,1)S(1)}, u32[]{:S(2)}, u32[]{:S(2)}) %collective-permute-start.8) | collective-permute-done | bytes 368672 | tf_op jit(solution)/shard_map/ppermute | solution.py:296
  124.9 2.0 collective-permute-start.10
  126.9 7.9 %collective-permute-done.13.refs_6_ = bf16[96,1920]{1,0:T(8,128)(2,1)S(1)} collective-permute-done((bf16[96,1920]{1,0:T(8,128)(2,1)}, bf16[96,1920]{1,0:T(8,128)(2,1)S(1)}, u32[]{:S(2)}, u32[]{:S(2)}) %collective-permute-start.13) | collective-permute-done | bytes 368672 | tf_op jit(solution)/shard_map/ppermute | solution.py:296
  134.8 5.1 %collective-permute-done.10.refs_4_ = bf16[96,1920]{1,0:T(8,128)(2,1)S(1)} collective-permute-done((bf16[96,1920]{1,0:T(8,128)(2,1)S(1)}, bf16[96,1920]{1,0:T(8,128)(2,1)S(1)}, u32[]{:S(2)}, u32[]{:S(2)}) %collective-permute-start.10) | collective-permute-done | bytes 368672 | tf_op jit(solution)/shard_map/ppermute | solution.py:296
  139.9 1.7 collective-permute-done.12.refs_5_
  141.6 0.7 copy-done.9
  142.3 9.0 %expert_kernel.1 = (f32[192,1792]{1,0:T(8,128)}, bf16[96,1792]{1,0:T(8,128)(2,1)}, bf16[96,1792]{1,0:T(8,128)(2,1)}, bf16[96,1792]{1,0:T(8,128)(2,1)}, bf16[96,1...) custom-call(s32[4]{0:T(128)} %compare_select_fusion.1.place, ...), custom_call_target="tpu_custom_call" | custom-call | tf_op jit(solution)/shard_map/expert_kernel/pallas_call | solution.py:285
  152.3 1.5 collective-permute-start.17
  153.8 1.6 collective-permute-start.18
  155.4 7.1 %collective-permute-done.14 = bf16[96,1792]{1,0:T(8,128)(2,1)S(1)} collective-permute-done((bf16[96,1792]{1,0:T(8,128)(2,1)}, bf16[96,1792]{1,0:T(8,128)(2,1)S(1)}, u32[]{:S(2)}, u32[]{:S(2)}) %collective-permute-start.14) | collective-permute-done | bytes 344096 | tf_op jit(solution)/shard_map/ppermute | solution.py:296
  162.5 1.1 add_convert_fusion.1
  163.6 1.7 collective-permute-start.15
  165.3 4.5 %collective-permute-done.18 = bf16[96,1792]{1,0:T(8,128)(2,1)S(1)} collective-permute-done((bf16[96,1792]{1,0:T(8,128)(2,1)}, bf16[96,1792]{1,0:T(8,128)(2,1)S(1)}, u32[]{:S(2)}, u32[]{:S(2)}) %collective-permute-start.18) | collective-permute-done | bytes 344096 | tf_op jit(solution)/shard_map/ppermute | solution.py:296
  169.8 1.1 add_convert_fusion
  171.2 4.1 %collective-permute-done.15.low1 = bf16[96,1792]{1,0:T(8,128)(2,1)S(1)} collective-permute-done((bf16[96,1792]{1,0:T(8,128)(2,1)S(1)}, bf16[96,1792]{1,0:T(8,128)(2,1)S(1)}, u32[]{:S(2)}, u32[]{:S(2)}) %collective-permute-start.15) | collective-permute-done | bytes 344096 | tf_op jit(solution)/shard_map/ppermute | solution.py:296
  175.3 4.6 %collective-permute-done.19.high3 = bf16[96,1792]{1,0:T(8,128)(2,1)S(1)} collective-permute-done((bf16[96,1792]{1,0:T(8,128)(2,1)S(1)}, bf16[96,1792]{1,0:T(8,128)(2,1)S(1)}, u32[]{:S(2)}, u32[]{:S(2)}) %collective-permute-start.19) | collective-permute-done | bytes 344096 | tf_op jit(solution)/shard_map/ppermute | solution.py:296
  179.9 0.7 copy-done.13
  180.7 3.8 %spread_kernel.1 = (bf16[256,1792]{1,0:T(8,128)(2,1)}, f32[256,1792]{1,0:T(8,128)}) custom-call(f32[192,1792]{1,0:T(8,128)} %get-tuple-element.31.own_ref, bf16[96,1792]{1,0:T(8,128)(2,1)} %copy-done.12, bf16[96,1792]{1,0:T(8,128)(2,1)} %copy-done.10, bf16[96,1792]{1,0:T(8,128)(2,1)} %copy-done.11, bf16[96,1792]{1,0:T(8,128)(2,1)} %copy-done.13, ...), custom_call_target="tpu_custom_call" | custom-call | tf_op jit(solution)/shard_map/spread_kernel/pallas_call | solution.py:285
  184.5 2.7 %collective-permute-done.20.got_ref = bf16[256,1792]{1,0:T(8,128)(2,1)S(1)} collective-permute-done((bf16[256,1792]{1,0:T(8,128)(2,1)}, bf16[256,1792]{1,0:T(8,128)(2,1)S(1)}, u32[]{:S(2)}, u32[]{:S(2)}) %collective-permute-start.20) | collective-permute-done | bytes 917536 | tf_op jit(solution)/shard_map/ppermute | solution.py:296
  187.2 0.9 copy-done.3
  188.1 2.8 %add_kernel.3 = bf16[32,8,1792]{2,1,0:T(8,128)(2,1)} custom-call(f32[256,1792]{1,0:T(8,128)} %get-tuple-element.39.keep_ref, bf16[256,1792]{1,0:T(8,128)(2,1)} %copy-done.3), custom_call_target="tpu_custom_call" | custom-call | tf_op jit(solution)/shard_map/add_kernel/pallas_call | solution.py:285
  190.9 31.2 %all_to_all.17 = bf16[32,8,1792]{2,1,0:T(8,128)(2,1)S(1)} all-to-all(bf16[32,8,1792]{2,1,0:T(8,128)(2,1)} %add_kernel.3), channel_id=1, replica_groups=mesh['context'=4,'x'=4,'z'=8,'core'=2] {'x','z'}, dimensions={0} | all-to-all | bytes 1835008 | tf_op jit(solution)/shard_map/all_to_all | solution.py:364
  222.2 0.6 add_convert_fusion.2
  (54 shorter events, 2.6 us)
Async XLA Ops:
  8.1 6.9 %collective-permute-start = (bf16[144,512]{1,0:T(8,128)(2,1)}, bf16[144,512]{1,0:T(8,128)(2,1)S(1)}, u32[]{:S(2)}, u32[]{:S(2)}) collective-permute-start(bf16[144,512]{1,0:T(8,128)(2,1)} %get-tuple-element.23.refs_0_), channel_id=1, source_target_pairs={{0,64},{64,128},{128,192},{192,0},{1,65},{65,129},{129,193},{193,1... | collective-permute-start | bytes 442376 | tf_op jit(solution)/shard_map/ppermute | solution.py:296
  10.0 6.8 %collective-permute-start.4 = (bf16[144,512]{1,0:T(8,128)(2,1)}, bf16[144,512]{1,0:T(8,128)(2,1)S(1)}, u32[]{:S(2)}, u32[]{:S(2)}) collective-permute-start(bf16[144,512]{1,0:T(8,128)(2,1)} %get-tuple-element.24.refs_4_), channel_id=1, source_target_pairs={{0,192},{64,0},{128,64},{192,128},{1,193},{65,1},{129,65},{193,129... | collective-permute-start | bytes 442376 | tf_op jit(solution)/shard_map/ppermute | solution.py:296
  10.1 9.2 %collective-permute-start.2 = (bf16[144,512]{1,0:T(8,128)(2,1)}, bf16[144,512]{1,0:T(8,128)(2,1)S(1)}, u32[]{:S(2)}, u32[]{:S(2)}) collective-permute-start(bf16[144,512]{1,0:T(8,128)(2,1)} %get-tuple-element.23.refs_0_), channel_id=1, source_target_pairs={{0,192},{64,0},{128,64},{192,128},{1,193},{65,1},{129,65},{193,129... | collective-permute-start | bytes 442376 | tf_op jit(solution)/shard_map/ppermute | solution.py:296
  10.8 8.5 %collective-permute-start.3 = (bf16[144,512]{1,0:T(8,128)(2,1)}, bf16[144,512]{1,0:T(8,128)(2,1)S(1)}, u32[]{:S(2)}, u32[]{:S(2)}) collective-permute-start(bf16[144,512]{1,0:T(8,128)(2,1)} %get-tuple-element.24.refs_4_), channel_id=1, source_target_pairs={{0,64},{64,128},{128,192},{192,0},{1,65},{65,129},{129,193},{193,1... | collective-permute-start | bytes 442376 | tf_op jit(solution)/shard_map/ppermute | solution.py:296
  15.0 8.1 %copy-start.14 = (bf16[144,512]{1,0:T(8,128)(2,1)}, bf16[144,512]{1,0:T(8,128)(2,1)S(1)}, u32[]{:S(2)}) copy-start(bf16[144,512]{1,0:T(8,128)(2,1)S(1)} %collective-permute-done.refs_1_) | copy-start | bytes 442372
  15.0 5.2 %collective-permute-start.1 = (bf16[144,512]{1,0:T(8,128)(2,1)S(1)}, bf16[144,512]{1,0:T(8,128)(2,1)S(1)}, u32[]{:S(2)}, u32[]{:S(2)}) collective-permute-start(bf16[144,512]{1,0:T(8,128)(2,1)S(1)} %collective-permute-done.refs_1_), channel_id=1, source_target_pairs={{0,64},{64,128},{128,192},{192,0},{1,65},{65,129},{129,193},{193,1... | collective-permute-start | bytes 442376 | tf_op jit(solution)/shard_map/ppermute | solution.py:296
  16.8 6.4 %copy-start.15 = (bf16[144,512]{1,0:T(8,128)(2,1)}, bf16[144,512]{1,0:T(8,128)(2,1)S(1)}, u32[]{:S(2)}) copy-start(bf16[144,512]{1,0:T(8,128)(2,1)S(1)} %collective-permute-done.4.refs_7_) | copy-start | bytes 442372
  16.8 6.4 %collective-permute-start.5 = (bf16[144,512]{1,0:T(8,128)(2,1)S(1)}, bf16[144,512]{1,0:T(8,128)(2,1)S(1)}, u32[]{:S(2)}, u32[]{:S(2)}) collective-permute-start(bf16[144,512]{1,0:T(8,128)(2,1)S(1)} %collective-permute-done.4.refs_7_), channel_id=1, source_target_pairs={{0,192},{64,0},{128,64},{192,128},{1,193},{65,1},{129,65},{193,129... | collective-permute-start | bytes 442376 | tf_op jit(solution)/shard_map/ppermute | solution.py:296
  19.3 3.8 %copy-start.16 = (bf16[144,512]{1,0:T(8,128)(2,1)}, bf16[144,512]{1,0:T(8,128)(2,1)S(1)}, u32[]{:S(2)}) copy-start(bf16[144,512]{1,0:T(8,128)(2,1)S(1)} %collective-permute-done.2.refs_3_) | copy-start | bytes 442372
  19.3 3.8 %copy-start.17 = (bf16[144,512]{1,0:T(8,128)(2,1)}, bf16[144,512]{1,0:T(8,128)(2,1)S(1)}, u32[]{:S(2)}) copy-start(bf16[144,512]{1,0:T(8,128)(2,1)S(1)} %collective-permute-done.3.refs_5_) | copy-start | bytes 442372
  20.2 3.0 %copy-start.18 = (bf16[144,512]{1,0:T(8,128)(2,1)}, bf16[144,512]{1,0:T(8,128)(2,1)S(1)}, u32[]{:S(2)}) copy-start(bf16[144,512]{1,0:T(8,128)(2,1)S(1)} %collective-permute-done.1.refs_2_) | copy-start | bytes 442372
  23.2 0.7 copy-start.19
  28.0 2.7 %collective-permute-start.6 = (bf16[256,1792]{1,0:T(8,128)(2,1)}, bf16[256,1792]{1,0:T(8,128)(2,1)S(1)}, u32[]{:S(2)}, u32[]{:S(2)}) collective-permute-start(bf16[256,1792]{1,0:T(8,128)(2,1)} %get-tuple-element.26), channel_id=1, source_target_pairs={{0,1},{1,0},{2,3},{3,2},{4,5},{5,4},{6,7},{7,6},{8,9},{9,8},{10,11... | collective-permute-start | bytes 2752520 | tf_op jit(solution)/shard_map/ppermute | solution.py:296
  30.7 0.9 copy-start.2
  106.1 2.6 %copy-start = (bf16[32,8,1920]{2,1,0:T(8,128)(2,1)}, bf16[32,8,1920]{2,1,0:T(8,128)(2,1)S(1)}, u32[]{:S(2)}) copy-start(bf16[32,8,1920]{2,1,0:T(8,128)(2,1)S(1)} %all_to_all.16) | copy-start | bytes 2949124
  106.1 2.6 %collective-permute-start.7 = (bf16[256,1920]{1,0:T(8,128)(2,1)S(1)}, bf16[256,1920]{1,0:T(8,128)(2,1)S(1)}, u32[]{:S(2)}, u32[]{:S(2)}) collective-permute-start(bf16[256,1920]{1,0:T(8,128)(2,1)S(1)} %bitcast.8), channel_id=1, source_target_pairs={{0,1},{1,0},{2,3},{3,2},{4,5},{5,4},{6,7},{7,6},{8,9},{9,8},{10,11... | collective-permute-start | bytes 2949128 | tf_op jit(solution)/shard_map/ppermute | solution.py:296
  108.7 1.0 copy-start.1
  113.2 11.7 %collective-permute-start.8 = (bf16[96,1920]{1,0:T(8,128)(2,1)}, bf16[96,1920]{1,0:T(8,128)(2,1)S(1)}, u32[]{:S(2)}, u32[]{:S(2)}) collective-permute-start(bf16[96,1920]{1,0:T(8,128)(2,1)} %get-tuple-element.29.refs_0_), channel_id=1, source_target_pairs={{0,64},{64,128},{128,192},{192,0},{1,65},{65,129},{129,193},{193,1... | collective-permute-start | bytes 1105928 | tf_op jit(solution)/shard_map/ppermute | solution.py:296
  114.0 12.9 %collective-permute-start.11 = (bf16[96,1920]{1,0:T(8,128)(2,1)}, bf16[96,1920]{1,0:T(8,128)(2,1)S(1)}, u32[]{:S(2)}, u32[]{:S(2)}) collective-permute-start(bf16[96,1920]{1,0:T(8,128)(2,1)} %get-tuple-element.30.refs_1_), channel_id=1, source_target_pairs={{0,192},{64,0},{128,64},{192,128},{1,193},{65,1},{129,65},{193,129... | collective-permute-start | bytes 1105928 | tf_op jit(solution)/shard_map/ppermute | solution.py:296
  115.2 19.5 %collective-permute-start.13 = (bf16[96,1920]{1,0:T(8,128)(2,1)}, bf16[96,1920]{1,0:T(8,128)(2,1)S(1)}, u32[]{:S(2)}, u32[]{:S(2)}) collective-permute-start(bf16[96,1920]{1,0:T(8,128)(2,1)} %get-tuple-element.29.refs_0_), channel_id=1, source_target_pairs={{0,192},{64,0},{128,64},{192,128},{1,193},{65,1},{129,65},{193,129... | collective-permute-start | bytes 1105928 | tf_op jit(solution)/shard_map/ppermute | solution.py:296
  115.3 19.5 %collective-permute-start.9 = (bf16[96,1920]{1,0:T(8,128)(2,1)}, bf16[96,1920]{1,0:T(8,128)(2,1)S(1)}, u32[]{:S(2)}, u32[]{:S(2)}) collective-permute-start(bf16[96,1920]{1,0:T(8,128)(2,1)} %get-tuple-element.30.refs_1_), channel_id=1, source_target_pairs={{0,64},{64,128},{128,192},{192,0},{1,65},{65,129},{129,193},{193,1... | collective-permute-start | bytes 1105928 | tf_op jit(solution)/shard_map/ppermute | solution.py:296
  124.9 16.7 %copy-start.4 = (bf16[96,1920]{1,0:T(8,128)(2,1)}, bf16[96,1920]{1,0:T(8,128)(2,1)S(1)}, u32[]{:S(2)}) copy-start(bf16[96,1920]{1,0:T(8,128)(2,1)S(1)} %collective-permute-done.8.refs_2_) | copy-start | bytes 1105924
  124.9 15.0 %collective-permute-start.10 = (bf16[96,1920]{1,0:T(8,128)(2,1)S(1)}, bf16[96,1920]{1,0:T(8,128)(2,1)S(1)}, u32[]{:S(2)}, u32[]{:S(2)}) collective-permute-start(bf16[96,1920]{1,0:T(8,128)(2,1)S(1)} %collective-permute-done.8.refs_2_), channel_id=1, source_target_pairs={{0,64},{64,128},{128,192},{192,0},{1,65},{65,129},{129,193},{193,1... | collective-permute-start | bytes 1105928 | tf_op jit(solution)/shard_map/ppermute | solution.py:296
  126.9 14.7 %copy-start.5 = (bf16[96,1920]{1,0:T(8,128)(2,1)}, bf16[96,1920]{1,0:T(8,128)(2,1)S(1)}, u32[]{:S(2)}) copy-start(bf16[96,1920]{1,0:T(8,128)(2,1)S(1)} %collective-permute-done.11.refs_7_) | copy-start | bytes 1105924
  126.9 14.7 %collective-permute-start.12 = (bf16[96,1920]{1,0:T(8,128)(2,1)S(1)}, bf16[96,1920]{1,0:T(8,128)(2,1)S(1)}, u32[]{:S(2)}, u32[]{:S(2)}) collective-permute-start(bf16[96,1920]{1,0:T(8,128)(2,1)S(1)} %collective-permute-done.11.refs_7_), channel_id=1, source_target_pairs={{0,192},{64,0},{128,64},{192,128},{1,193},{65,1},{129,65},{193,129... | collective-permute-start | bytes 1105928 | tf_op jit(solution)/shard_map/ppermute | solution.py:296
  134.8 6.8 %copy-start.6 = (bf16[96,1920]{1,0:T(8,128)(2,1)}, bf16[96,1920]{1,0:T(8,128)(2,1)S(1)}, u32[]{:S(2)}) copy-start(bf16[96,1920]{1,0:T(8,128)(2,1)S(1)} %collective-permute-done.13.refs_6_) | copy-start | bytes 1105924
  134.8 6.8 %copy-start.7 = (bf16[96,1920]{1,0:T(8,128)(2,1)}, bf16[96,1920]{1,0:T(8,128)(2,1)S(1)}, u32[]{:S(2)}) copy-start(bf16[96,1920]{1,0:T(8,128)(2,1)S(1)} %collective-permute-done.9.refs_3_) | copy-start | bytes 1105924
  139.9 1.7 copy-start.8
  141.6 0.7 copy-start.9
  151.3 11.2 %collective-permute-start.14 = (bf16[96,1792]{1,0:T(8,128)(2,1)}, bf16[96,1792]{1,0:T(8,128)(2,1)S(1)}, u32[]{:S(2)}, u32[]{:S(2)}) collective-permute-start(bf16[96,1792]{1,0:T(8,128)(2,1)} %get-tuple-element.33), channel_id=1, source_target_pairs={{0,64},{64,128},{128,192},{192,0},{1,65},{65,129},{129,193},{193,1... | collective-permute-start | bytes 1032200 | tf_op jit(solution)/shard_map/ppermute | solution.py:296
  151.8 19.4 %collective-permute-start.16 = (bf16[96,1792]{1,0:T(8,128)(2,1)}, bf16[96,1792]{1,0:T(8,128)(2,1)S(1)}, u32[]{:S(2)}, u32[]{:S(2)}) collective-permute-start(bf16[96,1792]{1,0:T(8,128)(2,1)} %get-tuple-element.34), channel_id=1, source_target_pairs={{0,64},{64,128},{128,192},{192,0},{1,65},{65,129},{129,193},{193,1... | collective-permute-start | bytes 1032200 | tf_op jit(solution)/shard_map/ppermute | solution.py:296
  152.3 19.0 %collective-permute-start.17 = (bf16[96,1792]{1,0:T(8,128)(2,1)}, bf16[96,1792]{1,0:T(8,128)(2,1)S(1)}, u32[]{:S(2)}, u32[]{:S(2)}) collective-permute-start(bf16[96,1792]{1,0:T(8,128)(2,1)} %get-tuple-element.35), channel_id=1, source_target_pairs={{0,192},{64,0},{128,64},{192,128},{1,193},{65,1},{129,65},{193,129... | collective-permute-start | bytes 1032200 | tf_op jit(solution)/shard_map/ppermute | solution.py:296
  153.8 15.9 %collective-permute-start.18 = (bf16[96,1792]{1,0:T(8,128)(2,1)}, bf16[96,1792]{1,0:T(8,128)(2,1)S(1)}, u32[]{:S(2)}, u32[]{:S(2)}) collective-permute-start(bf16[96,1792]{1,0:T(8,128)(2,1)} %get-tuple-element.37), channel_id=1, source_target_pairs={{0,192},{64,0},{128,64},{192,128},{1,193},{65,1},{129,65},{193,129... | collective-permute-start | bytes 1032200 | tf_op jit(solution)/shard_map/ppermute | solution.py:296
  163.6 11.7 %collective-permute-start.15 = (bf16[96,1792]{1,0:T(8,128)(2,1)S(1)}, bf16[96,1792]{1,0:T(8,128)(2,1)S(1)}, u32[]{:S(2)}, u32[]{:S(2)}) collective-permute-start(bf16[96,1792]{1,0:T(8,128)(2,1)S(1)} %add_convert_fusion.1), channel_id=1, source_target_pairs={{0,64},{64,128},{128,192},{192,0},{1,65},{65,129},{129,193},{193,1... | collective-permute-start | bytes 1032200 | tf_op jit(solution)/shard_map/ppermute | solution.py:296
  170.8 9.1 %collective-permute-start.19 = (bf16[96,1792]{1,0:T(8,128)(2,1)S(1)}, bf16[96,1792]{1,0:T(8,128)(2,1)S(1)}, u32[]{:S(2)}, u32[]{:S(2)}) collective-permute-start(bf16[96,1792]{1,0:T(8,128)(2,1)S(1)} %add_convert_fusion), channel_id=1, source_target_pairs={{0,192},{64,0},{128,64},{192,128},{1,193},{65,1},{129,65},{193,129... | collective-permute-start | bytes 1032200 | tf_op jit(solution)/shard_map/ppermute | solution.py:296
  171.2 8.7 %copy-start.10 = (bf16[96,1792]{1,0:T(8,128)(2,1)}, bf16[96,1792]{1,0:T(8,128)(2,1)S(1)}, u32[]{:S(2)}) copy-start(bf16[96,1792]{1,0:T(8,128)(2,1)S(1)} %collective-permute-done.16.high1) | copy-start | bytes 1032196
  171.2 8.7 %copy-start.11 = (bf16[96,1792]{1,0:T(8,128)(2,1)}, bf16[96,1792]{1,0:T(8,128)(2,1)S(1)}, u32[]{:S(2)}) copy-start(bf16[96,1792]{1,0:T(8,128)(2,1)S(1)} %collective-permute-done.17.low3) | copy-start | bytes 1032196
  175.3 4.7 %copy-start.12 = (bf16[96,1792]{1,0:T(8,128)(2,1)}, bf16[96,1792]{1,0:T(8,128)(2,1)S(1)}, u32[]{:S(2)}) copy-start(bf16[96,1792]{1,0:T(8,128)(2,1)S(1)} %collective-permute-done.15.low1) | copy-start | bytes 1032196
  179.9 0.7 copy-start.13
  184.5 2.7 %collective-permute-start.20 = (bf16[256,1792]{1,0:T(8,128)(2,1)}, bf16[256,1792]{1,0:T(8,128)(2,1)S(1)}, u32[]{:S(2)}, u32[]{:S(2)}) collective-permute-start(bf16[256,1792]{1,0:T(8,128)(2,1)} %get-tuple-element.40), channel_id=1, source_target_pairs={{0,1},{1,0},{2,3},{3,2},{4,5},{5,4},{6,7},{7,6},{8,9},{9,8},{10,11... | collective-permute-start | bytes 2752520 | tf_op jit(solution)/shard_map/ppermute | solution.py:296
  187.2 0.9 copy-start.3
  190.9 31.3 %copy-start.20 = (bf16[8,1792]{1,0:T(8,128)(2,1)S(1)}, bf16[8,1792]{1,0:T(8,128)(2,1)}, u32[]{:S(2)}) copy-start(bf16[8,1792]{1,0:T(8,128)(2,1)} %get-tuple-element.27) | copy-start | bytes 86020

commit v2 on v1

--- a/solution.py
+++ b/solution.py
@@ -281,15 +281,19 @@
     send_ref[...] = dot_nn(pick_ref[rows:, :], total).astype(BF16)
 
 
-def call(kernel, outs, inputs, scalars=0, scratch=()):
+def call(kernel, outs, inputs, scalars=0, scratch=(), limit=16, hold=True):
+    held = inputs[scalars:]
+    if hold:
+        held = [pltpu.with_memory_space_constraint(value, pltpu.VMEM) for value in held]
     return pl.pallas_call(
         kernel,
-        out_shape=tuple(jax.ShapeDtypeStruct(shape, dtype) for shape, dtype in outs),
-        in_specs=[SMEM] * scalars + [VMEM] * (len(inputs) - scalars),
+        out_shape=tuple(pltpu.VMEM(shape, dtype) for shape, dtype in outs),
+        in_specs=[SMEM] * scalars + [VMEM] * len(held),
         out_specs=tuple(VMEM for _ in outs),
         scratch_shapes=list(scratch),
+        compiler_params=pltpu.CompilerParams(vmem_limit_bytes=limit << 20),
         name=kernel.__name__,
-    )(*inputs)
+    )(*inputs[:scalars], *held)
 
 
 def shift(value, axis, count, step):
@@ -341,6 +345,7 @@
             tree_parents,
         ],
         scalars=1,
+        hold=False,
     )
 
     def around(low, high):

time: 224 us -> 198 us (0.88)
  Pallas kernels: 33.3 us -> 11.1 us
  other arithmetic: 3.45 us -> 0.92 us
    pallas_call x8, Pallas kernels: 33.3 us -> 11.1 us  [call(): pl.pallas_call(kernel, out_shape=tuple((pltpu.VMEM(shape, dtype) for shap...]
    unnamed x44 -> x30, local copies, waits for them, and re-layouts: 7.73 us -> 7.1 us
  transfers between devices with their start and end apart: 21 -> 21, of which waited for: 15 -> 16; matrix products, arithmetic and copies ran while one was open for 1% -> 0% of each run, Pallas kernels for 0% -> 0%
where the time goes in v2:
time: 198 us; the launch traced here: 197 us
  blocking collectives  100 us (51%)
  waiting for transfers between devices  57.7 us (29%)
  starting transfers between devices  20.4 us (10%)
  Pallas kernels  11.1 us (6%)
  local copies, waits for them, and re-layouts  7.1 us (4%)
    all_to_all x2, blocking collectives, return_rows(): return lax.all_to_all(summed, ROW_AXES, 0, 0, tiled=True)  68.1 us
    ppermute x21, waiting for transfers between devices, shift(): lax.ppermute(value, axis, [(i, (i + step) % count) for i in range(count)])  57.7 us
    all_to_all x1, blocking collectives, local(): lax.all_to_all(payload, ROW_AXES, 0, 0, tiled=True)  32.1 us
    ppermute x21, starting transfers between devices, shift(): lax.ppermute(value, axis, [(i, (i + step) % count) for i in range(count)])  20.4 us
    pallas_call x8, Pallas kernels, call(): pl.pallas_call(kernel, out_shape=tuple((pltpu.VMEM(shape, dtype) for shap...  11.1 us
    unnamed x30, local copies, waits for them, and re-layouts  7.1 us
  transfers between devices with their start and end apart: 21, of which 16 were waited for; matrix products, arithmetic and copies ran while one was open for 0% of the time, Pallas kernels for 0%

profile of v2, /device:TPU:24, one launch (start us, length us, event | category | flops | bytes accessed | tf_op | source)
XLA Modules:
  0.0 197.5 jit_solution(3877724260652170722)
XLA Ops:
  0.0 0.9 copy.17.table_ref
  0.9 0.8 copy.18.parent_ref
  1.7 1.0 copy-done.4
  2.6 1.0 copy-done.5
  3.6 0.9 copy-done.6
  4.6 0.9 copy-done.7
  5.5 0.9 copy-done.8
  6.4 0.7 copy-done.13
  7.1 3.3 %attention_kernel.1 = (bf16[144,512]{1,0:T(8,128)(2,1)S(1)}, bf16[144,512]{1,0:T(8,128)(2,1)S(1)}) custom-call(s32[4]{0:T(128)S(1)} %compare_select_fusion.1.place, bf16[512,384]{1,0:T(8,128)(2,1)S(1)} %copy-done.4, bf16[2,128,512]{2,1,0:T(8,128)(2,1)S(1)} %copy-done.6, bf16[2,512,128]{2,1,0:T(8,128)(2,1)S(1)} %copy-done.7, bf16[256,576]{1,0:T(8,128)(2,1)S(1)} %bitcast.13, ...), custom_call_target="tpu_custom_call" | custom-call | tf_op jit(solution)/shard_map/attention_kernel/pallas_call | solution.py:288
  10.4 2.0 %collective-permute-start = (bf16[144,512]{1,0:T(8,128)(2,1)S(1)}, bf16[144,512]{1,0:T(8,128)(2,1)S(1)}, u32[]{:S(2)}, u32[]{:S(2)}) collective-permute-start(bf16[144,512]{1,0:T(8,128)(2,1)S(1)} %get-tuple-element.23.refs_0_), channel_id=1, source_target_pairs={{0,64},{64,128},{128,192},{192,0},{1,65},{65,129},{129,193},{193,1... | collective-permute-start | bytes 442376 | tf_op jit(solution)/shard_map/ppermute | solution.py:300
  12.5 0.7 collective-permute-start.2
  13.2 2.5 %collective-permute-start.3 = (bf16[144,512]{1,0:T(8,128)(2,1)S(1)}, bf16[144,512]{1,0:T(8,128)(2,1)S(1)}, u32[]{:S(2)}, u32[]{:S(2)}) collective-permute-start(bf16[144,512]{1,0:T(8,128)(2,1)S(1)} %get-tuple-element.24.refs_4_), channel_id=1, source_target_pairs={{0,64},{64,128},{128,192},{192,0},{1,65},{65,129},{129,193},{193,1... | collective-permute-start | bytes 442376 | tf_op jit(solution)/shard_map/ppermute | solution.py:300
  15.7 1.5 collective-permute-done.refs_1_
  17.2 1.8 collective-permute-start.1
  19.0 0.2 collective-permute-start.5
  19.2 2.4 %collective-permute-done.2.refs_3_ = bf16[144,512]{1,0:T(8,128)(2,1)S(1)} collective-permute-done((bf16[144,512]{1,0:T(8,128)(2,1)S(1)}, bf16[144,512]{1,0:T(8,128)(2,1)S(1)}, u32[]{:S(2)}, u32[]{:S(2)}) %collective-permute-start.2) | collective-permute-done | bytes 147488 | tf_op jit(solution)/shard_map/ppermute | solution.py:300
  21.6 0.7 collective-permute-done.1.refs_2_
  22.4 3.0 %collective-permute-done.5.refs_6_ = bf16[144,512]{1,0:T(8,128)(2,1)S(1)} collective-permute-done((bf16[144,512]{1,0:T(8,128)(2,1)S(1)}, bf16[144,512]{1,0:T(8,128)(2,1)S(1)}, u32[]{:S(2)}, u32[]{:S(2)}) %collective-permute-start.5) | collective-permute-done | bytes 147488 | tf_op jit(solution)/shard_map/ppermute | solution.py:300
  25.3 1.7 merge_kernel.1
  27.1 2.5 %collective-permute-done.6.got_ref = bf16[256,1792]{1,0:T(8,128)(2,1)S(1)} collective-permute-done((bf16[256,1792]{1,0:T(8,128)(2,1)S(1)}, bf16[256,1792]{1,0:T(8,128)(2,1)S(1)}, u32[]{:S(2)}, u32[]{:S(2)}) %collective-permute-start.6) | collective-permute-done | bytes 917536 | tf_op jit(solution)/shard_map/ppermute | solution.py:300
  29.6 0.2 add_kernel.2
  29.8 37.2 %all_to_all.15.parts_ref = bf16[32,8,1792]{2,1,0:T(8,128)(2,1)S(1)} all-to-all(bf16[32,8,1792]{2,1,0:T(8,128)(2,1)S(1)} %add_kernel.2), channel_id=1, replica_groups=mesh['context'=4,'x'=4,'z'=8,'core'=2] {'x','z'}, dimensions={0} | all-to-all | bytes 1835008 | tf_op jit(solution)/shard_map/all_to_all | solution.py:369
  67.0 0.2 hidden_kernel.1
  67.3 32.1 %all_to_all.16 = bf16[32,8,1920]{2,1,0:T(8,128)(2,1)S(1)} all-to-all(bf16[32,8,1920]{2,1,0:T(8,128)(2,1)S(1)} %get-tuple-element.28), channel_id=1, replica_groups=mesh['context'=4,'x'=4,'z'=8,'core'=2] {'x','z'}, dimensions={0} | all-to-all | bytes 1966080 | tf_op jit(solution)/shard_map/all_to_all | solution.py:377
  99.3 2.6 %collective-permute-done.7.other_ref = bf16[256,1920]{1,0:T(8,128)(2,1)S(1)} collective-permute-done((bf16[256,1920]{1,0:T(8,128)(2,1)S(1)}, bf16[256,1920]{1,0:T(8,128)(2,1)S(1)}, u32[]{:S(2)}, u32[]{:S(2)}) %collective-permute-start.7) | collective-permute-done | bytes 983072 | tf_op jit(solution)/shard_map/ppermute | solution.py:300
  101.9 1.7 select_kernel.1
  103.6 0.2 collective-permute-start.8
  103.8 1.9 collective-permute-start.11
  105.7 3.2 %collective-permute-start.9 = (bf16[96,1920]{1,0:T(8,128)(2,1)S(1)}, bf16[96,1920]{1,0:T(8,128)(2,1)S(1)}, u32[]{:S(2)}, u32[]{:S(2)}) collective-permute-start(bf16[96,1920]{1,0:T(8,128)(2,1)S(1)} %get-tuple-element.30.refs_1_), channel_id=1, source_target_pairs={{0,64},{64,128},{128,192},{192,0},{1,65},{65,129},{129,193},{193,1... | collective-permute-start | bytes 1105928 | tf_op jit(solution)/shard_map/ppermute | solution.py:300
  108.9 6.2 %collective-permute-done.8.refs_2_ = bf16[96,1920]{1,0:T(8,128)(2,1)S(1)} collective-permute-done((bf16[96,1920]{1,0:T(8,128)(2,1)S(1)}, bf16[96,1920]{1,0:T(8,128)(2,1)S(1)}, u32[]{:S(2)}, u32[]{:S(2)}) %collective-permute-start.8) | collective-permute-done | bytes 368672 | tf_op jit(solution)/shard_map/ppermute | solution.py:300
  115.1 1.4 collective-permute-start.10
  116.6 0.5 collective-permute-start.12
  117.1 7.4 %collective-permute-done.13.refs_6_ = bf16[96,1920]{1,0:T(8,128)(2,1)S(1)} collective-permute-done((bf16[96,1920]{1,0:T(8,128)(2,1)S(1)}, bf16[96,1920]{1,0:T(8,128)(2,1)S(1)}, u32[]{:S(2)}, u32[]{:S(2)}) %collective-permute-start.13) | collective-permute-done | bytes 368672 | tf_op jit(solution)/shard_map/ppermute | solution.py:300
  124.5 5.6 %collective-permute-done.10.refs_4_ = bf16[96,1920]{1,0:T(8,128)(2,1)S(1)} collective-permute-done((bf16[96,1920]{1,0:T(8,128)(2,1)S(1)}, bf16[96,1920]{1,0:T(8,128)(2,1)S(1)}, u32[]{:S(2)}, u32[]{:S(2)}) %collective-permute-start.10) | collective-permute-done | bytes 368672 | tf_op jit(solution)/shard_map/ppermute | solution.py:300
  130.1 1.5 collective-permute-done.12.refs_5_
  131.6 3.2 %expert_kernel.1 = (f32[192,1792]{1,0:T(8,128)S(1)}, bf16[96,1792]{1,0:T(8,128)(2,1)S(1)}, bf16[96,1792]{1,0:T(8,128)(2,1)S(1)}, bf16[96,1792]{1,0:T(8,128)(2,1)...) custom-call(s32[4]{0:T(128)S(1)} %compare_select_fusion.1.place, ...), custom_call_target="tpu_custom_call" | custom-call | tf_op jit(solution)/shard_map/expert_kernel/pallas_call | solution.py:288
  134.9 1.1 collective-permute-start.16
  136.0 1.0 collective-permute-start.17
  136.9 1.9 collective-permute-start.18
  138.9 6.9 %collective-permute-done.14 = bf16[96,1792]{1,0:T(8,128)(2,1)S(1)} collective-permute-done((bf16[96,1792]{1,0:T(8,128)(2,1)S(1)}, bf16[96,1792]{1,0:T(8,128)(2,1)S(1)}, u32[]{:S(2)}, u32[]{:S(2)}) %collective-permute-start.14) | collective-permute-done | bytes 344096 | tf_op jit(solution)/shard_map/ppermute | solution.py:300
  145.8 1.3 collective-permute-start.15
  147.2 6.1 %collective-permute-done.18 = bf16[96,1792]{1,0:T(8,128)(2,1)S(1)} collective-permute-done((bf16[96,1792]{1,0:T(8,128)(2,1)S(1)}, bf16[96,1792]{1,0:T(8,128)(2,1)S(1)}, u32[]{:S(2)}, u32[]{:S(2)}) %collective-permute-start.18) | collective-permute-done | bytes 344096 | tf_op jit(solution)/shard_map/ppermute | solution.py:300
  153.4 5.4 %collective-permute-done.15.low1 = bf16[96,1792]{1,0:T(8,128)(2,1)S(1)} collective-permute-done((bf16[96,1792]{1,0:T(8,128)(2,1)S(1)}, bf16[96,1792]{1,0:T(8,128)(2,1)S(1)}, u32[]{:S(2)}, u32[]{:S(2)}) %collective-permute-start.15) | collective-permute-done | bytes 344096 | tf_op jit(solution)/shard_map/ppermute | solution.py:300
  158.8 3.6 %collective-permute-done.19.high3 = bf16[96,1792]{1,0:T(8,128)(2,1)S(1)} collective-permute-done((bf16[96,1792]{1,0:T(8,128)(2,1)S(1)}, bf16[96,1792]{1,0:T(8,128)(2,1)S(1)}, u32[]{:S(2)}, u32[]{:S(2)}) %collective-permute-start.19) | collective-permute-done | bytes 344096 | tf_op jit(solution)/shard_map/ppermute | solution.py:300
  162.4 0.7 spread_kernel.1
  163.2 2.5 %collective-permute-done.20.got_ref = bf16[256,1792]{1,0:T(8,128)(2,1)S(1)} collective-permute-done((bf16[256,1792]{1,0:T(8,128)(2,1)S(1)}, bf16[256,1792]{1,0:T(8,128)(2,1)S(1)}, u32[]{:S(2)}, u32[]{:S(2)}) %collective-permute-start.20) | collective-permute-done | bytes 917536 | tf_op jit(solution)/shard_map/ppermute | solution.py:300
  165.8 30.9 %all_to_all.17 = bf16[32,8,1792]{2,1,0:T(8,128)(2,1)S(1)} all-to-all(bf16[32,8,1792]{2,1,0:T(8,128)(2,1)S(1)} %add_kernel.3), channel_id=1, replica_groups=mesh['context'=4,'x'=4,'z'=8,'core'=2] {'x','z'}, dimensions={0} | all-to-all | bytes 1835008 | tf_op jit(solution)/shard_map/all_to_all | solution.py:369
  196.9 0.6 add_convert_fusion.2
  (40 shorter events, 1.2 us)
Async XLA Ops:
  0.0 25.3 %copy-start.3 = (bf16[256,1792]{1,0:T(8,128)(2,1)S(1)}, bf16[256,1792]{1,0:T(8,128)(2,1)}, u32[]{:S(2)}) copy-start(bf16[256,1792]{1,0:T(8,128)(2,1)} %refs_8_.1) | copy-start | bytes 2752516
  1.6 1.0 copy-start.4
  2.6 1.0 copy-start.5
  3.6 0.9 copy-start.6
  4.6 0.9 copy-start.7
  5.5 0.9 copy-start.8
  6.4 0.7 copy-start.13
  10.4 6.8 %collective-permute-start = (bf16[144,512]{1,0:T(8,128)(2,1)S(1)}, bf16[144,512]{1,0:T(8,128)(2,1)S(1)}, u32[]{:S(2)}, u32[]{:S(2)}) collective-permute-start(bf16[144,512]{1,0:T(8,128)(2,1)S(1)} %get-tuple-element.23.refs_0_), channel_id=1, source_target_pairs={{0,64},{64,128},{128,192},{192,0},{1,65},{65,129},{129,193},{193,1... | collective-permute-start | bytes 442376 | tf_op jit(solution)/shard_map/ppermute | solution.py:300
  12.4 6.6 %collective-permute-start.4 = (bf16[144,512]{1,0:T(8,128)(2,1)S(1)}, bf16[144,512]{1,0:T(8,128)(2,1)S(1)}, u32[]{:S(2)}, u32[]{:S(2)}) collective-permute-start(bf16[144,512]{1,0:T(8,128)(2,1)S(1)} %get-tuple-element.24.refs_4_), channel_id=1, source_target_pairs={{0,192},{64,0},{128,64},{192,128},{1,193},{65,1},{129,65},{193,129... | collective-permute-start | bytes 442376 | tf_op jit(solution)/shard_map/ppermute | solution.py:300
  12.5 9.1 %collective-permute-start.2 = (bf16[144,512]{1,0:T(8,128)(2,1)S(1)}, bf16[144,512]{1,0:T(8,128)(2,1)S(1)}, u32[]{:S(2)}, u32[]{:S(2)}) collective-permute-start(bf16[144,512]{1,0:T(8,128)(2,1)S(1)} %get-tuple-element.23.refs_0_), channel_id=1, source_target_pairs={{0,192},{64,0},{128,64},{192,128},{1,193},{65,1},{129,65},{193,129... | collective-permute-start | bytes 442376 | tf_op jit(solution)/shard_map/ppermute | solution.py:300
  13.2 8.4 %collective-permute-start.3 = (bf16[144,512]{1,0:T(8,128)(2,1)S(1)}, bf16[144,512]{1,0:T(8,128)(2,1)S(1)}, u32[]{:S(2)}, u32[]{:S(2)}) collective-permute-start(bf16[144,512]{1,0:T(8,128)(2,1)S(1)} %get-tuple-element.24.refs_4_), channel_id=1, source_target_pairs={{0,64},{64,128},{128,192},{192,0},{1,65},{65,129},{129,193},{193,1... | collective-permute-start | bytes 442376 | tf_op jit(solution)/shard_map/ppermute | solution.py:300
  17.2 5.2 %collective-permute-start.1 = (bf16[144,512]{1,0:T(8,128)(2,1)S(1)}, bf16[144,512]{1,0:T(8,128)(2,1)S(1)}, u32[]{:S(2)}, u32[]{:S(2)}) collective-permute-start(bf16[144,512]{1,0:T(8,128)(2,1)S(1)} %collective-permute-done.refs_1_), channel_id=1, source_target_pairs={{0,64},{64,128},{128,192},{192,0},{1,65},{65,129},{129,193},{193,1... | collective-permute-start | bytes 442376 | tf_op jit(solution)/shard_map/ppermute | solution.py:300
  19.0 6.4 %collective-permute-start.5 = (bf16[144,512]{1,0:T(8,128)(2,1)S(1)}, bf16[144,512]{1,0:T(8,128)(2,1)S(1)}, u32[]{:S(2)}, u32[]{:S(2)}) collective-permute-start(bf16[144,512]{1,0:T(8,128)(2,1)S(1)} %collective-permute-done.4.refs_7_), channel_id=1, source_target_pairs={{0,192},{64,0},{128,64},{192,128},{1,193},{65,1},{129,65},{193,129... | collective-permute-start | bytes 442376 | tf_op jit(solution)/shard_map/ppermute | solution.py:300
  25.3 106.2 %copy-start.2 = (bf16[1,256,7168]{2,1,0:T(8,128)(2,1)S(1)}, bf16[1,256,7168]{2,1,0:T(8,128)(2,1)}, u32[]{:S(2)}) copy-start(bf16[1,256,7168]{2,1,0:T(8,128)(2,1)} %param.31) | copy-start | bytes 11010052
  27.0 2.6 %collective-permute-start.6 = (bf16[256,1792]{1,0:T(8,128)(2,1)S(1)}, bf16[256,1792]{1,0:T(8,128)(2,1)S(1)}, u32[]{:S(2)}, u32[]{:S(2)}) collective-permute-start(bf16[256,1792]{1,0:T(8,128)(2,1)S(1)} %get-tuple-element.26), channel_id=1, source_target_pairs={{0,1},{1,0},{2,3},{3,2},{4,5},{5,4},{6,7},{7,6},{8,9},{9,8},{10,11... | collective-permute-start | bytes 2752520 | tf_op jit(solution)/shard_map/ppermute | solution.py:300
  29.6 37.4 %copy-start.10 = (bf16[8,1792]{1,0:T(8,128)(2,1)S(1)}, bf16[8,1792]{1,0:T(8,128)(2,1)}, u32[]{:S(2)}) copy-start(bf16[8,1792]{1,0:T(8,128)(2,1)} %residual_ref.1) | copy-start | bytes 86020
  29.6 37.4 %copy-start.11 = (s32[8,8]{1,0:T(8,128)S(1)}, s32[8,8]{1,0:T(8,128)}, u32[]{:S(2)}) copy-start(s32[8,8]{1,0:T(8,128)} %ids_ref.1) | copy-start | bytes 772
  29.6 37.4 %copy-start.12 = (f32[8,8]{1,0:T(8,128)S(1)}, f32[8,8]{1,0:T(8,128)}, u32[]{:S(2)}) copy-start(f32[8,8]{1,0:T(8,128)} %weights_ref.1) | copy-start | bytes 772
  29.6 102.0 %copy-start.1 = (bf16[1,7168,256]{2,1,0:T(8,128)(2,1)S(1)}, bf16[1,7168,256]{2,1,0:T(8,128)(2,1)}, u32[]{:S(2)}) copy-start(bf16[1,7168,256]{2,1,0:T(8,128)(2,1)} %param.30) | copy-start | bytes 11010052
  67.2 64.3 %copy-start = (bf16[1,7168,256]{2,1,0:T(8,128)(2,1)S(1)}, bf16[1,7168,256]{2,1,0:T(8,128)(2,1)}, u32[]{:S(2)}) copy-start(bf16[1,7168,256]{2,1,0:T(8,128)(2,1)} %param.29) | copy-start | bytes 11010052
  67.3 64.3 %copy-start.9 = (f32[7168]{0:T(1024)S(1)}, f32[7168]{0:T(1024)}, u32[]{:S(2)}) copy-start(f32[7168]{0:T(1024)} %param.26) | copy-start | bytes 86020
  99.3 2.6 %collective-permute-start.7 = (bf16[256,1920]{1,0:T(8,128)(2,1)S(1)}, bf16[256,1920]{1,0:T(8,128)(2,1)S(1)}, u32[]{:S(2)}, u32[]{:S(2)}) collective-permute-start(bf16[256,1920]{1,0:T(8,128)(2,1)S(1)} %bitcast.8), channel_id=1, source_target_pairs={{0,1},{1,0},{2,3},{3,2},{4,5},{5,4},{6,7},{7,6},{8,9},{9,8},{10,11... | collective-permute-start | bytes 2949128 | tf_op jit(solution)/shard_map/ppermute | solution.py:300
  103.6 11.5 %collective-permute-start.8 = (bf16[96,1920]{1,0:T(8,128)(2,1)S(1)}, bf16[96,1920]{1,0:T(8,128)(2,1)S(1)}, u32[]{:S(2)}, u32[]{:S(2)}) collective-permute-start(bf16[96,1920]{1,0:T(8,128)(2,1)S(1)} %get-tuple-element.29.refs_0_), channel_id=1, source_target_pairs={{0,64},{64,128},{128,192},{192,0},{1,65},{65,129},{129,193},{193,1... | collective-permute-start | bytes 1105928 | tf_op jit(solution)/shard_map/ppermute | solution.py:300
  103.8 12.8 %collective-permute-start.11 = (bf16[96,1920]{1,0:T(8,128)(2,1)S(1)}, bf16[96,1920]{1,0:T(8,128)(2,1)S(1)}, u32[]{:S(2)}, u32[]{:S(2)}) collective-permute-start(bf16[96,1920]{1,0:T(8,128)(2,1)S(1)} %get-tuple-element.30.refs_1_), channel_id=1, source_target_pairs={{0,192},{64,0},{128,64},{192,128},{1,193},{65,1},{129,65},{193,129... | collective-permute-start | bytes 1105928 | tf_op jit(solution)/shard_map/ppermute | solution.py:300
  105.7 18.8 %collective-permute-start.13 = (bf16[96,1920]{1,0:T(8,128)(2,1)S(1)}, bf16[96,1920]{1,0:T(8,128)(2,1)S(1)}, u32[]{:S(2)}, u32[]{:S(2)}) collective-permute-start(bf16[96,1920]{1,0:T(8,128)(2,1)S(1)} %get-tuple-element.29.refs_0_), channel_id=1, source_target_pairs={{0,192},{64,0},{128,64},{192,128},{1,193},{65,1},{129,65},{193,129... | collective-permute-start | bytes 1105928 | tf_op jit(solution)/shard_map/ppermute | solution.py:300
  105.7 18.8 %collective-permute-start.9 = (bf16[96,1920]{1,0:T(8,128)(2,1)S(1)}, bf16[96,1920]{1,0:T(8,128)(2,1)S(1)}, u32[]{:S(2)}, u32[]{:S(2)}) collective-permute-start(bf16[96,1920]{1,0:T(8,128)(2,1)S(1)} %get-tuple-element.30.refs_1_), channel_id=1, source_target_pairs={{0,64},{64,128},{128,192},{192,0},{1,65},{65,129},{129,193},{193,1... | collective-permute-start | bytes 1105928 | tf_op jit(solution)/shard_map/ppermute | solution.py:300
  115.1 15.0 %collective-permute-start.10 = (bf16[96,1920]{1,0:T(8,128)(2,1)S(1)}, bf16[96,1920]{1,0:T(8,128)(2,1)S(1)}, u32[]{:S(2)}, u32[]{:S(2)}) collective-permute-start(bf16[96,1920]{1,0:T(8,128)(2,1)S(1)} %collective-permute-done.8.refs_2_), channel_id=1, source_target_pairs={{0,64},{64,128},{128,192},{192,0},{1,65},{65,129},{129,193},{193,1... | collective-permute-start | bytes 1105928 | tf_op jit(solution)/shard_map/ppermute | solution.py:300
  116.6 15.0 %collective-permute-start.12 = (bf16[96,1920]{1,0:T(8,128)(2,1)S(1)}, bf16[96,1920]{1,0:T(8,128)(2,1)S(1)}, u32[]{:S(2)}, u32[]{:S(2)}) collective-permute-start(bf16[96,1920]{1,0:T(8,128)(2,1)S(1)} %collective-permute-done.11.refs_7_), channel_id=1, source_target_pairs={{0,192},{64,0},{128,64},{192,128},{1,193},{65,1},{129,65},{193,129... | collective-permute-start | bytes 1105928 | tf_op jit(solution)/shard_map/ppermute | solution.py:300
  134.7 11.0 %collective-permute-start.14 = (bf16[96,1792]{1,0:T(8,128)(2,1)S(1)}, bf16[96,1792]{1,0:T(8,128)(2,1)S(1)}, u32[]{:S(2)}, u32[]{:S(2)}) collective-permute-start(bf16[96,1792]{1,0:T(8,128)(2,1)S(1)} %get-tuple-element.33), channel_id=1, source_target_pairs={{0,64},{64,128},{128,192},{192,0},{1,65},{65,129},{129,193},{193,1... | collective-permute-start | bytes 1032200 | tf_op jit(solution)/shard_map/ppermute | solution.py:300
  134.9 18.6 %collective-permute-start.16 = (bf16[96,1792]{1,0:T(8,128)(2,1)S(1)}, bf16[96,1792]{1,0:T(8,128)(2,1)S(1)}, u32[]{:S(2)}, u32[]{:S(2)}) collective-permute-start(bf16[96,1792]{1,0:T(8,128)(2,1)S(1)} %get-tuple-element.34), channel_id=1, source_target_pairs={{0,64},{64,128},{128,192},{192,0},{1,65},{65,129},{129,193},{193,1... | collective-permute-start | bytes 1032200 | tf_op jit(solution)/shard_map/ppermute | solution.py:300
  136.0 17.5 %collective-permute-start.17 = (bf16[96,1792]{1,0:T(8,128)(2,1)S(1)}, bf16[96,1792]{1,0:T(8,128)(2,1)S(1)}, u32[]{:S(2)}, u32[]{:S(2)}) collective-permute-start(bf16[96,1792]{1,0:T(8,128)(2,1)S(1)} %get-tuple-element.35), channel_id=1, source_target_pairs={{0,192},{64,0},{128,64},{192,128},{1,193},{65,1},{129,65},{193,129... | collective-permute-start | bytes 1032200 | tf_op jit(solution)/shard_map/ppermute | solution.py:300
  136.9 16.3 %collective-permute-start.18 = (bf16[96,1792]{1,0:T(8,128)(2,1)S(1)}, bf16[96,1792]{1,0:T(8,128)(2,1)S(1)}, u32[]{:S(2)}, u32[]{:S(2)}) collective-permute-start(bf16[96,1792]{1,0:T(8,128)(2,1)S(1)} %get-tuple-element.37), channel_id=1, source_target_pairs={{0,192},{64,0},{128,64},{192,128},{1,193},{65,1},{129,65},{193,129... | collective-permute-start | bytes 1032200 | tf_op jit(solution)/shard_map/ppermute | solution.py:300
  145.8 13.0 %collective-permute-start.15 = (bf16[96,1792]{1,0:T(8,128)(2,1)S(1)}, bf16[96,1792]{1,0:T(8,128)(2,1)S(1)}, u32[]{:S(2)}, u32[]{:S(2)}) collective-permute-start(bf16[96,1792]{1,0:T(8,128)(2,1)S(1)} %add_convert_fusion.1), channel_id=1, source_target_pairs={{0,64},{64,128},{128,192},{192,0},{1,65},{65,129},{129,193},{193,1... | collective-permute-start | bytes 1032200 | tf_op jit(solution)/shard_map/ppermute | solution.py:300
  153.3 9.1 %collective-permute-start.19 = (bf16[96,1792]{1,0:T(8,128)(2,1)S(1)}, bf16[96,1792]{1,0:T(8,128)(2,1)S(1)}, u32[]{:S(2)}, u32[]{:S(2)}) collective-permute-start(bf16[96,1792]{1,0:T(8,128)(2,1)S(1)} %add_convert_fusion), channel_id=1, source_target_pairs={{0,192},{64,0},{128,64},{192,128},{1,193},{65,1},{129,65},{193,129... | collective-permute-start | bytes 1032200 | tf_op jit(solution)/shard_map/ppermute | solution.py:300
  163.1 2.6 %collective-permute-start.20 = (bf16[256,1792]{1,0:T(8,128)(2,1)S(1)}, bf16[256,1792]{1,0:T(8,128)(2,1)S(1)}, u32[]{:S(2)}, u32[]{:S(2)}) collective-permute-start(bf16[256,1792]{1,0:T(8,128)(2,1)S(1)} %get-tuple-element.40), channel_id=1, source_target_pairs={{0,1},{1,0},{2,3},{3,2},{4,5},{5,4},{6,7},{7,6},{8,9},{9,8},{10,11... | collective-permute-start | bytes 2752520 | tf_op jit(solution)/shard_map/ppermute | solution.py:300

commit v3 on v2

--- a/solution.py
+++ b/solution.py
@@ -4,6 +4,7 @@
 from jax.experimental import pallas as pl
 from jax.experimental.pallas import tpu as pltpu
 from jax.sharding import Mesh, PartitionSpec as P
+
 
 LAT = 512
 ROPE = 64
@@ -20,10 +21,12 @@
 VMEM = pl.BlockSpec(memory_space=pltpu.VMEM)
 TAIL = 128
 
+
 CONTEXT = "context"
-ROW_AXES = ("x", "z")
+WIDE = "x"
+DEEP = "z"
 CORE = "core"
-EXPERT = ("x", "z", "core")
+EXPERT = (WIDE, DEEP, CORE)
 
 
 def iota(shape, axis):
@@ -36,10 +39,6 @@
 
 def dot_nt(a, b):
     return lax.dot_general(a, b, (((1,), (1,)), ((), ())), preferred_element_type=F32)
-
-
-def dot_tn(a, b):
-    return lax.dot_general(a, b, (((0,), (0,)), ((), ())), preferred_element_type=F32)
 
 
 def split3(value):
@@ -57,29 +56,20 @@
     pool_rows = pool_ref.shape[0]
     fresh_rows = fresh_ref.shape[0]
     rows = q_ref.shape[0]
-    leaves, table_len = table_ref.shape
+    table_len, leaves = table_ref.shape
     pages = pool_rows // PAGE
-    lengths = jnp.sum(
-        jnp.where(
-            iota((leaves, leaves), 0) == iota((leaves, leaves), 1),
-            length_ref[...].astype(F32),
-            0.0,
-        ),
-        axis=1,
-        keepdims=True,
-    )
-    remain = lengths - (iota((leaves, table_len), 1) * PAGE).astype(F32)
-    remain = jnp.clip(remain, 0.0, float(PAGE))
+    passed = (iota((table_len, leaves), 0) * PAGE).astype(F32)
+    remain = jnp.clip(length_ref[...].astype(F32) - passed, 0.0, float(PAGE))
     table = table_ref[...]
-    lane = iota((leaves, 128), 1)
-    limits = jnp.zeros((leaves, 128), F32)
+    line = iota((16, leaves), 0)
+    limits = jnp.zeros((16, leaves), F32)
     for page in range(pages):
         seen = jnp.sum(
-            jnp.where(table == context * pages + page, remain, 0.0), axis=1, keepdims=True
+            jnp.where(table == context * pages + page, remain, 0.0), axis=0, keepdims=True
         )
-        limits = jnp.where(lane == page, seen, limits)
+        limits = jnp.where(line == page, seen, limits)
     spread = (iota((leaves, rows), 0) == iota((leaves, rows), 1) // LOOK).astype(F32).astype(BF16)
-    row_limits = dot_nn(limits.T.astype(BF16), spread)
+    row_limits = dot_nn(limits.astype(BF16), spread)
     page_limit = jnp.concatenate(
         [jnp.broadcast_to(row_limits[p : p + 1, :], (PAGE, rows)) for p in range(pages)], axis=0
     )
@@ -91,7 +81,7 @@
         .astype(F32)
         .astype(BF16)
     )
-    parents = dot_nn(pick_leaf, parent_ref[...].astype(F32).astype(BF16))
+    parents = dot_nt(pick_leaf, parent_ref[...].astype(F32).astype(BF16))
     token = jnp.bitwise_and(iota((fresh_rows, LOOK), 0), LOOK - 1)
     parent = jnp.sum(
         jnp.where(iota((fresh_rows, LOOK), 1) == token, parents, 0.0), axis=1, keepdims=True
@@ -101,7 +91,7 @@
     step = (iota(square, 1) - first).astype(F32)
     linked = jnp.where((step == parent) & (parent >= 0.0), 1.0, 0.0)
     linked = jnp.where(iota(square, 0) == iota(square, 1), 1.0, linked)
-    for repeat in range(3):
+    for _ in range(3):
         half = linked.astype(BF16)
         linked = jnp.where(dot_nn(half, half) > 0.5, 1.0, 0.0)
     fresh_mask = jnp.concatenate([linked.T] * (rows // fresh_rows), axis=1)
@@ -159,9 +149,32 @@
     keep_ref[...] = scratch[:, core].reshape(keep_ref.shape)
 
 
-def add_kernel(keep_ref, got_ref, out_ref):
-    total = keep_ref[...] + got_ref[...].astype(F32)
-    out_ref[...] = total.astype(BF16).reshape(out_ref.shape)
+def add_kernel(place, keep_ref, got_ref, own_ref, *sends):
+    rows = own_ref.shape[0]
+    count = len(sends) + 1
+    for step in range(count):
+        target = lax.rem(place[3] + step, count)
+        at = pl.ds(pl.multiple_of(target * rows, rows), rows)
+        total = keep_ref[at, :] + got_ref[at, :].astype(F32)
+        if step == 0:
+            own_ref[...] = total
+        else:
+            sends[step - 1][...] = total.astype(BF16)
+
+
+def sum_kernel(own_ref, *refs):
+    total = own_ref[...]
+    for ref in refs[:-1]:
+        total = total + ref[...].astype(F32)
+    refs[-1][...] = total.astype(BF16).reshape(refs[-1].shape)
+
+
+def cut_kernel(place, down_ref, after_ref, *outs):
+    width = outs[0].shape[1]
+    count = len(outs) + 1
+    for step, out in enumerate(outs, 1):
+        target = lax.rem(place[0] + step, count)
+        out[...] = down_ref[:, pl.ds(pl.multiple_of(target * width, 128), width)]
 
 
 def hidden_kernel(parts_ref, residual_ref, ids_ref, weights_ref, hidden_ref, payload_ref):
@@ -191,42 +204,36 @@
         payload_ref[index, :, width:] = tail
 
 
-def select_kernel(place, own_ref, other_ref, low_ref, high_ref, pick_ref):
-    expert = place[1].astype(F32)
-    half = own_ref.shape[0]
-    rows = 2 * half
-    slots = pick_ref.shape[1]
-    width = own_ref.shape[1] - TAIL
-    tails = jnp.concatenate([own_ref[:, width:], other_ref[:, width:]], axis=0).astype(F32)
+def select_kernel(place, *refs):
+    parts, (low_ref, send_ref, pick_ref, other_ref) = refs[:4], refs[4:]
+    rows, slots = pick_ref.shape
+    values = jnp.concatenate([part[...] for part in parts], axis=0)
+    width = values.shape[1] - TAIL
+    tails = values[:, width:].astype(F32)
     lane = iota((rows, TAIL), 1)
-    named = jnp.max(
-        jnp.where((tails == expert) & (lane < 8), 1.0, 0.0), axis=1, keepdims=True
-    )
     ahead = (iota((rows, rows), 1) < iota((rows, rows), 0)) & (
         iota((rows, rows), 1) // 8 == iota((rows, rows), 0) // 8
     )
-    before = dot_nn(
-        jnp.where(ahead, 1.0, 0.0).astype(BF16),
-        jnp.broadcast_to(named, (rows, TAIL)).astype(BF16),
-    )[:, :1]
-    place_of = (iota((rows, 1), 0) // 8 * CAP).astype(F32) + before
+    ahead = jnp.where(ahead, 1.0, 0.0).astype(BF16)
+    first = (iota((rows, 1), 0) // 8 * CAP).astype(F32)
     slot = iota((rows, slots), 1).astype(F32)
-    pick = jnp.where((slot == place_of) & (named > 0.5), 1.0, 0.0)
-    pick_ref[...] = pick.astype(BF16)
-    turned = pick.T.astype(BF16)
-    chosen = dot_nn(turned[:, :half], own_ref[...]) + dot_nn(turned[:, half:], other_ref[...])
-    chosen = chosen.astype(BF16)
-    low_ref[...] = chosen[: slots // 2]
-    high_ref[...] = chosen[slots // 2 :]
+    partner = place[1] + 1 - 2 * place[2]
+    for expert, out, keep in ((place[1], low_ref, pick_ref), (partner, send_ref, other_ref)):
+        named = jnp.max(
+            jnp.where((tails == expert.astype(F32)) & (lane < 8), 1.0, 0.0), axis=1, keepdims=True
+        )
+        before = dot_nn(ahead, jnp.broadcast_to(named, (rows, TAIL)).astype(BF16))[:, :1]
+        pick = jnp.where((slot == first + before) & (named > 0.5), 1.0, 0.0)
+        keep[...] = pick.astype(BF16)
+        out[...] = dot_nn(pick.T.astype(BF16), values).astype(BF16)
 
 
 def expert_kernel(place, *refs):
     context, expert = place[0], place[1].astype(F32)
     parts = refs[:8]
-    gain_ref, gate_ref, up_ref, down_ref, own_ref = refs[8:13]
-    sends = refs[13:]
-    slots = own_ref.shape[0]
-    width = own_ref.shape[1]
+    gain_ref, gate_ref, up_ref, active_ref, share_ref = refs[8:]
+    slots = active_ref.shape[0]
+    width = gain_ref.shape[2]
     count = 4
     lane = iota((slots, TAIL), 1)
     squares = 0.0
@@ -245,6 +252,7 @@
             share = jnp.sum(
                 jnp.where((tail == expert) & (lane < 8), shares, 0.0), axis=1, keepdims=True
             )
+            share_ref[...] = jnp.broadcast_to(share, share_ref.shape)
     inverse = lax.rsqrt(squares * (1.0 / (count * width)) + NORM_EPSILON)
     gate_part = jnp.zeros((slots, gate_ref.shape[1]), F32)
     up_part = gate_part
@@ -257,28 +265,28 @@
         at = pl.ds(pl.multiple_of(source * width, width), width)
         gate_part = gate_part + dot_nn(normed, gate_ref[at, :])
         up_part = up_part + dot_nn(normed, up_ref[at, :])
-    active = (gate_part / (1.0 + jnp.exp(-gate_part)) * up_part).astype(BF16)
-    for index in (2, 1, 3, 0):
-        target = lax.rem(context + index, count)
-        at = pl.ds(pl.multiple_of(target * width, 128), width)
-        made = dot_nn(active, down_ref[:, at]) * share
-        if index == 0:
-            own_ref[...] = made
-        else:
-            made = made.astype(BF16)
-            sends[2 * index - 2][...] = made[: slots // 2]
-            sends[2 * index - 1][...] = made[slots // 2 :]
-
-
-def spread_kernel(own_ref, low1, high1, low3, high3, pick_ref, send_ref, keep_ref):
-    slots = own_ref.shape[0]
-    half = slots // 2
-    low = own_ref[:half] + low1[...].astype(F32) + low3[...].astype(F32)
-    high = own_ref[half:] + high1[...].astype(F32) + high3[...].astype(F32)
-    total = jnp.concatenate([low, high], axis=0).astype(BF16)
-    rows = keep_ref.shape[0]
-    keep_ref[...] = dot_nn(pick_ref[:rows, :], total)
-    send_ref[...] = dot_nn(pick_ref[rows:, :], total).astype(BF16)
+    active_ref[...] = (gate_part / (1.0 + jnp.exp(-gate_part)) * up_part).astype(BF16)
+
+
+def down_kernel(place, *refs):
+    actives, others, (down_ref, share_ref, low_ref, high_ref) = refs[:4], refs[4:7], refs[7:]
+    width = low_ref.shape[1]
+    half = low_ref.shape[0]
+    at = pl.ds(pl.multiple_of(place[0] * width, 128), width)
+    made = dot_nn(actives[0][...], down_ref[:, at])
+    for active, other in zip(actives[1:], others):
+        made = made + dot_nn(active[...], other[...])
+    made = (made * share_ref[:, :1]).astype(BF16)
+    low_ref[...] = made[:half]
+    high_ref[...] = made[half:]
+
+
+def spread_kernel(low_ref, got_ref, pick_ref, other_ref, own_ref, *sends):
+    rows = own_ref.shape[0]
+    total = dot_nn(pick_ref[...], low_ref[...]) + dot_nn(other_ref[...], got_ref[...])
+    own_ref[...] = total[:rows]
+    for step, send in enumerate(sends, 1):
+        send[...] = total[step * rows : (step + 1) * rows].astype(BF16)
 
 
 def call(kernel, outs, inputs, scalars=0, scratch=(), limit=16, hold=True):
@@ -292,7 +300,6 @@
         out_specs=tuple(VMEM for _ in outs),
         scratch_shapes=list(scratch),
         compiler_params=pltpu.CompilerParams(vmem_limit_bytes=limit << 20),
-        name=kernel.__name__,
     )(*inputs[:scalars], *held)
 
 
@@ -320,15 +327,17 @@
 ):
     rows = queries.shape[0]
     row_dev, width = residual.shape
-    ring = lax.axis_size(CONTEXT)
-    chips = lax.axis_size(ROW_AXES)
+    ring, wide, deep = lax.axis_size(CONTEXT), lax.axis_size(WIDE), lax.axis_size(DEEP)
     half = rows // 2
     slots = rows // row_dev * CAP
-    context = lax.axis_index(CONTEXT)
+    full = width + TAIL
+    hidden_units = gate_matrix.shape[2]
     expert = lax.axis_index(EXPERT)
-    core = lax.axis_index(CORE)
+    places = (lax.axis_index(CONTEXT), expert, lax.axis_index(CORE), lax.axis_index(WIDE))
     number = jnp.arange(4, dtype=jnp.int32)
-    place = jnp.where(number == 0, context, jnp.where(number == 1, expert, core)).astype(jnp.int32)
+    place = jnp.zeros((4,), jnp.int32)
+    for index, value in enumerate(places):
+        place = jnp.where(number == index, value, place)
 
     low, high = call(
         attention_kernel,
@@ -340,12 +349,13 @@
             value_lift,
             page_pool.reshape(-1, page_pool.shape[-1]),
             fresh_latents.reshape(-1, fresh_latents.shape[-1]),
-            page_table,
+            page_table.T,
             context_lengths.reshape(1, -1),
-            tree_parents,
+            tree_parents.T,
         ],
         scalars=1,
         hold=False,
+        limit=56,
     )
 
     def around(low, high):
@@ -354,67 +364,75 @@
         low2, high2 = shift(low1, CONTEXT, ring, 1), shift(high3, CONTEXT, ring, -1)
         return (low, low1, low2, low3), (high, high1, high2, high3)
 
+    def gather(own, sends):
+        chunk = [((deep, row_dev, width), BF16)]
+        (summed,) = call(sum_kernel, chunk, [own, *sends])
+        return lax.all_to_all(summed, DEEP, 0, 0, tiled=True)
+
     lows, highs = around(low, high)
     send, keep = call(
         merge_kernel,
         [((half, width), BF16), ((half, width), F32)],
         [place, *lows, *highs, out_weight],
         scalars=1,
-        scratch=[pltpu.VMEM((chips, 2, row_dev, width), F32)],
-    )
-
-    def return_rows(send, keep):
-        got = shift(send, CORE, 2, 1)
-        (summed,) = call(add_kernel, [((chips, row_dev, width), BF16)], [keep, got])
-        return lax.all_to_all(summed, ROW_AXES, 0, 0, tiled=True)
-
-    mixed = return_rows(send, keep)
+        scratch=[pltpu.VMEM((wide * deep, 2, row_dev, width), F32)],
+    )
+    cuts = call(
+        cut_kernel,
+        [((hidden_units, width), BF16)] * (ring - 1),
+        [place, down_matrix[0], send],
+        scalars=1,
+    )
+    others = []
+    for step, cut in enumerate(cuts, 1):
+        others.append(shift(cut, CONTEXT, ring, step))
+    split = [((half // wide, width), F32)] + [((half // wide, width), BF16)] * (wide - 1)
+    got = shift(send, CORE, 2, 1)
+    own, *sends = call(add_kernel, split, [place, keep, got], scalars=1)
+    mixed = gather(own, [shift(part, WIDE, wide, step) for step, part in enumerate(sends, 1)])
     hidden, payload = call(
         hidden_kernel,
-        [((row_dev, width), BF16), ((chips, row_dev, width + TAIL), BF16)],
+        [((row_dev, width), BF16), ((deep, row_dev, full), BF16)],
         [mixed, residual, expert_ids, route_weights],
     )
-    own = lax.all_to_all(payload, ROW_AXES, 0, 0, tiled=True).reshape(half, width + TAIL)
-    other = shift(own, CORE, 2, 1)
-    low, high, pick = call(
+    near = lax.all_to_all(payload, DEEP, 0, 0, tiled=True).reshape(deep * row_dev, full)
+    parts = [near] + [shift(near, WIDE, wide, step) for step in range(1, wide)]
+    low, send, pick, pick_other = call(
         select_kernel,
-        [((slots // 2, width + TAIL), BF16)] * 2 + [((rows, slots), BF16)],
-        [place, own, other],
-        scalars=1,
-    )
-    lows, highs = around(low, high)
-    parts = [part for pair in zip(lows, highs) for part in pair]
-    made, low1, high1, low2, high2, low3, high3 = call(
+        [((slots // 2, full), BF16)] * 2 + [((half, slots // 2), BF16)] * 2,
+        [place, *parts],
+        scalars=1,
+    )
+    lows, highs = around(low, shift(send, CORE, 2, 1))
+    active, share = call(
         expert_kernel,
-        [((slots, width), F32)] + [((slots // 2, width), BF16)] * 6,
+        [((slots, hidden_units), BF16), ((slots, TAIL), F32)],
         [
             place,
-            *parts,
+            *[part for pair in zip(lows, highs) for part in pair],
             norm_gain.reshape(ring, 1, width),
             gate_matrix[0],
             up_matrix[0],
-            down_matrix[0],
         ],
         scalars=1,
     )
-    passed_low = shift(low2, CONTEXT, ring, 1)
-    passed_high = shift(high2, CONTEXT, ring, -1)
-    got_high1 = shift(high1, CONTEXT, ring, 1)
-    got_low3 = shift(low3, CONTEXT, ring, -1)
-    got_low1 = shift((low1.astype(F32) + passed_low.astype(F32)).astype(BF16), CONTEXT, ring, 1)
-    got_high3 = shift((high3.astype(F32) + passed_high.astype(F32)).astype(BF16), CONTEXT, ring, -1)
-    send, keep = call(
-        spread_kernel,
-        [((half, width), BF16), ((half, width), F32)],
-        [made, got_low1, got_high1, got_low3, got_high3, pick],
-    )
-    returned = return_rows(send, keep)
+    actives = [active] + [shift(active, CONTEXT, ring, step) for step in range(1, ring)]
+    low, high = call(
+        down_kernel,
+        [((slots // 2, width), BF16)] * 2,
+        [place, *actives, *others, down_matrix[0], share],
+        scalars=1,
+    )
+    own, *sends = call(
+        spread_kernel, split, [low, shift(high, CORE, 2, 1), pick, pick_other]
+    )
+    returned = gather(own, [shift(part, WIDE, wide, -step) for step, part in enumerate(sends, 1)])
     total = jnp.sum(returned.astype(F32), axis=0)
     return (hidden.astype(F32) + total).astype(BF16)
 
 
 def solution(mesh):
-    fine = Mesh(mesh.devices.reshape(4, 4, 8, 2), (CONTEXT, "x", "z", CORE))
+    fine = Mesh(mesh.devices.reshape(4, 4, 8, 2), (CONTEXT, WIDE, DEEP, CORE))
     return jax.shard_map(
         local,
         mesh=fine,

time: 198 us -> 206 us (1.040); the launches traced: 197 us -> 203 us
  blocking collectives: 100 us -> 45.9 us
  waiting for transfers between devices: 57.7 us -> 108 us
  starting transfers between devices: 20.4 us -> 33.3 us
  local copies, waits for them, and re-layouts: 7.1 us -> 1.87 us
  Pallas kernels: 11.1 us -> 13.3 us
    all_to_all x3, blocking collectives: 100 us -> 45.9 us  [the longest x2 33.2 us: gather(): return lax.all_to_all(summed, DEEP, 0, 0, tiled=True)]
    ppermute x21 -> x30, waiting for transfers between devices: 57.7 us -> 108 us  [shift(): lax.ppermute(value, axis, [(i, (i + step) % count) for i in range(count)])]
    ppermute x21 -> x30, starting transfers between devices: 20.4 us -> 33.3 us  [shift(): lax.ppermute(value, axis, [(i, (i + step) % count) for i in range(count)])]
    unnamed x30 -> x20, local copies, waits for them, and re-layouts: 7.1 us -> 1.87 us
    pallas_call x8 -> x11, Pallas kernels: 11.1 us -> 13.3 us  [call(): pl.pallas_call(kernel, out_shape=tuple((pltpu.VMEM(shape, dtype) for shap...]
  transfers between devices with their start and end apart: 21 -> 30, of which waited for: 16 -> 20; matrix products, arithmetic and copies ran while one was open for 0% -> 0% of each run, Pallas kernels for 0% -> 1%
where the time goes in v3:
time: 206 us; the launch traced here: 203 us
  waiting for transfers between devices  108 us (52%)
  blocking collectives  45.9 us (22%)
  starting transfers between devices  33.3 us (16%)
  Pallas kernels  13.3 us (6%)
    ppermute x30, waiting for transfers between devices, shift(): lax.ppermute(value, axis, [(i, (i + step) % count) for i in range(count)])  108 us
    ppermute x30, starting transfers between devices, shift(): lax.ppermute(value, axis, [(i, (i + step) % count) for i in range(count)])  33.3 us
    all_to_all x2, blocking collectives, gather(): return lax.all_to_all(summed, DEEP, 0, 0, tiled=True)  33.2 us
    pallas_call x11, Pallas kernels, call(): pl.pallas_call(kernel, out_shape=tuple((pltpu.VMEM(shape, dtype) for shap...  13.3 us
    all_to_all x1, blocking collectives, local(): lax.all_to_all(payload, DEEP, 0, 0, tiled=True)  12.7 us
  transfers between devices with their start and end apart: 30, of which 20 were waited for; matrix products, arithmetic and copies ran while one was open for 0% of the time, Pallas kernels for 1%

profile of v3, /device:TPU:24, one launch (start us, length us, event | category | flops | bytes accessed | tf_op | source)
XLA Modules:
  0.0 203.2 jit_solution(3221998588537733462)
XLA Ops:
  0.5 3.8 %shard_map.154 = (bf16[144,512]{1,0:T(8,128)(2,1)S(1)}, bf16[144,512]{1,0:T(8,128)(2,1)S(1)}) custom-call(s32[4]{0:T(128)} %compare_select_fusion.3.place, bf16[512,384]{1,0:T(8,128)(2,1)} %q_ref.1, bf16[2,128,512]{2,1,0:T(8,128)(2,1)} %kl_ref.1, bf16[2,512,128]{2,1,0:T(8,128)(2,1)} %vl_ref.1, bf16[256,576]{1,0:T(8,128)(2,1)} %bitcast.19, ...), custom_call_target="tpu_custom_call" | custom-call | tf_op jit(solution)/shard_map/pallas_call | solution.py:296
  4.3 2.0 collective-permute-start
  6.4 0.7 collective-permute-start.2
  7.2 2.5 %collective-permute-start.3 = (bf16[144,512]{1,0:T(8,128)(2,1)S(1)}, bf16[144,512]{1,0:T(8,128)(2,1)S(1)}, u32[]{:S(2)}, u32[]{:S(2)}) collective-permute-start(bf16[144,512]{1,0:T(8,128)(2,1)S(1)} %get-tuple-element.31.refs_4_), channel_id=1, source_target_pairs={{0,64},{64,128},{128,192},{192,0},{1,65},{65,129},{129,193},{193,1... | collective-permute-start | bytes 442376 | tf_op jit(solution)/shard_map/ppermute | solution.py:307
  9.7 1.5 collective-permute-done.refs_1_
  11.1 1.8 collective-permute-start.1
  13.2 2.4 %collective-permute-done.2.refs_3_ = bf16[144,512]{1,0:T(8,128)(2,1)S(1)} collective-permute-done((bf16[144,512]{1,0:T(8,128)(2,1)S(1)}, bf16[144,512]{1,0:T(8,128)(2,1)S(1)}, u32[]{:S(2)}, u32[]{:S(2)}) %collective-permute-start.2) | collective-permute-done | bytes 147488 | tf_op jit(solution)/shard_map/ppermute | solution.py:307
  15.6 0.7 collective-permute-done.1.refs_2_
  16.3 2.9 %collective-permute-done.5.refs_6_ = bf16[144,512]{1,0:T(8,128)(2,1)S(1)} collective-permute-done((bf16[144,512]{1,0:T(8,128)(2,1)S(1)}, bf16[144,512]{1,0:T(8,128)(2,1)S(1)}, u32[]{:S(2)}, u32[]{:S(2)}) %collective-permute-start.5) | collective-permute-done | bytes 147488 | tf_op jit(solution)/shard_map/ppermute | solution.py:307
  19.3 1.2 copy-done.3
  20.4 0.7 copy-done.4
  21.1 1.7 shard_map.155
  22.9 2.5 %collective-permute-done.6.got_ref = bf16[256,1792]{1,0:T(8,128)(2,1)S(1)} collective-permute-done((bf16[256,1792]{1,0:T(8,128)(2,1)S(1)}, bf16[256,1792]{1,0:T(8,128)(2,1)S(1)}, u32[]{:S(2)}, u32[]{:S(2)}) %collective-permute-start.6) | collective-permute-done | bytes 917536 | tf_op jit(solution)/shard_map/ppermute | solution.py:307
  25.3 0.7 shard_map.156
  26.1 1.2 collective-permute-start.7
  27.3 2.7 %collective-permute-start.8 = (bf16[64,1792]{1,0:T(8,128)(2,1)S(1)}, bf16[64,1792]{1,0:T(8,128)(2,1)S(1)}, u32[]{:S(2)}, u32[]{:S(2)}) collective-permute-start(bf16[64,1792]{1,0:T(8,128)(2,1)S(1)} %get-tuple-element.36), channel_id=1, source_target_pairs={{0,32},{16,48},{32,0},{48,16},{1,33},{17,49},{33,1},{49,17},{2,34}... | collective-permute-start | bytes 688136 | tf_op jit(solution)/shard_map/ppermute | solution.py:307
  30.0 1.4 collective-permute-start.9
  31.5 3.7 %collective-permute-done.7.refs_0_ = bf16[64,1792]{1,0:T(8,128)(2,1)S(1)} collective-permute-done((bf16[64,1792]{1,0:T(8,128)(2,1)S(1)}, bf16[64,1792]{1,0:T(8,128)(2,1)S(1)}, u32[]{:S(2)}, u32[]{:S(2)}) %collective-permute-start.7) | collective-permute-done | bytes 229408 | tf_op jit(solution)/shard_map/ppermute | solution.py:307
  35.2 5.4 %collective-permute-done.8.refs_1_ = bf16[64,1792]{1,0:T(8,128)(2,1)S(1)} collective-permute-done((bf16[64,1792]{1,0:T(8,128)(2,1)S(1)}, bf16[64,1792]{1,0:T(8,128)(2,1)S(1)}, u32[]{:S(2)}, u32[]{:S(2)}) %collective-permute-start.8) | collective-permute-done | bytes 229408 | tf_op jit(solution)/shard_map/ppermute | solution.py:307
  40.7 19.1 %all_to_all.15.parts_ref = bf16[8,8,1792]{2,1,0:T(8,128)(2,1)S(1)} all-to-all(bf16[8,8,1792]{2,1,0:T(8,128)(2,1)S(1)} %shard_map.157), channel_id=1, replica_groups=mesh['context'=4,'x'=4,'z'=8,'core'=2] {'z'}, dimensions={0} | all-to-all | bytes 458752 | tf_op jit(solution)/shard_map/all_to_all | solution.py:370
  60.0 12.7 %all_to_all.16 = bf16[8,8,1920]{2,1,0:T(8,128)(2,1)S(1)} all-to-all(bf16[8,8,1920]{2,1,0:T(8,128)(2,1)S(1)} %get-tuple-element.39), channel_id=1, replica_groups=mesh['context'=4,'x'=4,'z'=8,'core'=2] {'z'}, dimensions={0} | all-to-all | bytes 491520 | tf_op jit(solution)/shard_map/all_to_all | solution.py:398
  72.7 3.1 %collective-permute-start.12 = (bf16[64,1920]{1,0:T(8,128)(2,1)S(1)}, bf16[64,1920]{1,0:T(8,128)(2,1)S(1)}, u32[]{:S(2)}, u32[]{:S(2)}) collective-permute-start(bf16[64,1920]{1,0:T(8,128)(2,1)S(1)} %bitcast.14), channel_id=1, source_target_pairs={{0,48},{16,0},{32,16},{48,32},{1,49},{17,1},{33,17},{49,33},{2,50}... | collective-permute-start | bytes 737288 | tf_op jit(solution)/shard_map/ppermute | solution.py:307
  76.6 7.1 %collective-permute-done.12.refs_3_ = bf16[64,1920]{1,0:T(8,128)(2,1)S(1)} collective-permute-done((bf16[64,1920]{1,0:T(8,128)(2,1)S(1)}, bf16[64,1920]{1,0:T(8,128)(2,1)S(1)}, u32[]{:S(2)}, u32[]{:S(2)}) %collective-permute-start.12) | collective-permute-done | bytes 245792 | tf_op jit(solution)/shard_map/ppermute | solution.py:307
  83.7 1.2 collective-permute-done.11.refs_2_
  85.0 2.2 %collective-permute-done.10.refs_1_ = bf16[64,1920]{1,0:T(8,128)(2,1)S(1)} collective-permute-done((bf16[64,1920]{1,0:T(8,128)(2,1)S(1)}, bf16[64,1920]{1,0:T(8,128)(2,1)S(1)}, u32[]{:S(2)}, u32[]{:S(2)}) %collective-permute-start.10) | collective-permute-done | bytes 245792 | tf_op jit(solution)/shard_map/ppermute | solution.py:307
  87.2 1.7 shard_map.159
  89.0 3.2 %collective-permute-start.14 = (bf16[96,1920]{1,0:T(8,128)(2,1)S(1)}, bf16[96,1920]{1,0:T(8,128)(2,1)S(1)}, u32[]{:S(2)}, u32[]{:S(2)}) collective-permute-start(bf16[96,1920]{1,0:T(8,128)(2,1)S(1)} %get-tuple-element.40.refs_0_), channel_id=1, source_target_pairs={{0,64},{64,128},{128,192},{192,0},{1,65},{65,129},{129,193},{193,1... | collective-permute-start | bytes 1105928 | tf_op jit(solution)/shard_map/ppermute | solution.py:307
  92.2 0.7 shard_map.161
  93.1 0.9 collective-permute-start.24
  94.0 1.1 collective-permute-start.25
  95.1 26.2 %collective-permute-done.19.refs_6_ = bf16[96,1920]{1,0:T(8,128)(2,1)S(1)} collective-permute-done((bf16[96,1920]{1,0:T(8,128)(2,1)S(1)}, bf16[96,1920]{1,0:T(8,128)(2,1)S(1)}, u32[]{:S(2)}, u32[]{:S(2)}) %collective-permute-start.19) | collective-permute-done | bytes 368672 | tf_op jit(solution)/shard_map/ppermute | solution.py:307
  121.3 3.2 %collective-permute-start.15 = (bf16[96,1920]{1,0:T(8,128)(2,1)S(1)}, bf16[96,1920]{1,0:T(8,128)(2,1)S(1)}, u32[]{:S(2)}, u32[]{:S(2)}) collective-permute-start(bf16[96,1920]{1,0:T(8,128)(2,1)S(1)} %collective-permute-done.13.refs_1_), channel_id=1, source_target_pairs={{0,64},{64,128},{128,192},{192,0},{1,65},{65,129},{129,193},{193,1... | collective-permute-start | bytes 1105928 | tf_op jit(solution)/shard_map/ppermute | solution.py:307
  124.6 23.8 %collective-permute-done.17.refs_7_ = bf16[96,1920]{1,0:T(8,128)(2,1)S(1)} collective-permute-done((bf16[96,1920]{1,0:T(8,128)(2,1)S(1)}, bf16[96,1920]{1,0:T(8,128)(2,1)S(1)}, u32[]{:S(2)}, u32[]{:S(2)}) %collective-permute-start.17) | collective-permute-done | bytes 368672 | tf_op jit(solution)/shard_map/ppermute | solution.py:307
  148.4 2.0 collective-permute-start.18
  150.4 8.0 %collective-permute-done.16.refs_4_ = bf16[96,1920]{1,0:T(8,128)(2,1)S(1)} collective-permute-done((bf16[96,1920]{1,0:T(8,128)(2,1)S(1)}, bf16[96,1920]{1,0:T(8,128)(2,1)S(1)}, u32[]{:S(2)}, u32[]{:S(2)}) %collective-permute-start.16) | collective-permute-done | bytes 368672 | tf_op jit(solution)/shard_map/ppermute | solution.py:307
  158.4 1.2 collective-permute-done.18.refs_5_
  159.6 2.3 %shard_map.160 = (bf16[192,256]{1,0:T(8,128)(2,1)S(1)}, f32[192,128]{1,0:T(8,128)S(1)}) custom-call(s32[4]{0:T(128)S(1)} %copy-done.5, bf16[96,1920]{1,0:T(8,128)(2,1)S(1)} %get-tuple-element.40.refs_0_, bf16[96,1920]{1,0:T(8,128)(2,1)S(1)} %collective-permute-done.13.refs_1_, bf16[96,1920]{1,0:T(8,128)(2,1)S(1)} %collective-permute-done.14.refs_2_, ...), custom_call_target="tpu_custom_call" | custom-call | tf_op jit(solution)/shard_map/pallas_call | solution.py:296
  162.6 2.4 %collective-permute-start.21 = (bf16[192,256]{1,0:T(8,128)(2,1)S(1)}, bf16[192,256]{1,0:T(8,128)(2,1)S(1)}, u32[]{:S(2)}, u32[]{:S(2)}) collective-permute-start(bf16[192,256]{1,0:T(8,128)(2,1)S(1)} %get-tuple-element.42.refs_0_), channel_id=1, source_target_pairs={{0,128},{64,192},{128,0},{192,64},{1,129},{65,193},{129,1},{193,65... | collective-permute-start | bytes 294920 | tf_op jit(solution)/shard_map/ppermute | solution.py:307
  165.5 3.4 %collective-permute-done.22.refs_3_ = bf16[192,256]{1,0:T(8,128)(2,1)S(1)} collective-permute-done((bf16[192,256]{1,0:T(8,128)(2,1)S(1)}, bf16[192,256]{1,0:T(8,128)(2,1)S(1)}, u32[]{:S(2)}, u32[]{:S(2)}) %collective-permute-start.22) | collective-permute-done | bytes 98336 | tf_op jit(solution)/shard_map/ppermute | solution.py:307
  168.9 0.9 collective-permute-done.20.refs_1_
  169.8 1.4 shard_map.162
  171.4 1.6 collective-permute-done.26.got_ref
  173.6 1.0 collective-permute-start.27
  174.9 0.8 collective-permute-start.29
  175.7 6.4 %collective-permute-done.27.refs_0_ = bf16[64,1792]{1,0:T(8,128)(2,1)S(1)} collective-permute-done((bf16[64,1792]{1,0:T(8,128)(2,1)S(1)}, bf16[64,1792]{1,0:T(8,128)(2,1)S(1)}, u32[]{:S(2)}, u32[]{:S(2)}) %collective-permute-start.27) | collective-permute-done | bytes 229408 | tf_op jit(solution)/shard_map/ppermute | solution.py:307
  182.2 2.5 %collective-permute-done.28.refs_1_ = bf16[64,1792]{1,0:T(8,128)(2,1)S(1)} collective-permute-done((bf16[64,1792]{1,0:T(8,128)(2,1)S(1)}, bf16[64,1792]{1,0:T(8,128)(2,1)S(1)}, u32[]{:S(2)}, u32[]{:S(2)}) %collective-permute-start.28) | collective-permute-done | bytes 229408 | tf_op jit(solution)/shard_map/ppermute | solution.py:307
  184.7 3.8 %collective-permute-done.29.refs_2_ = bf16[64,1792]{1,0:T(8,128)(2,1)S(1)} collective-permute-done((bf16[64,1792]{1,0:T(8,128)(2,1)S(1)}, bf16[64,1792]{1,0:T(8,128)(2,1)S(1)}, u32[]{:S(2)}, u32[]{:S(2)}) %collective-permute-start.29) | collective-permute-done | bytes 229408 | tf_op jit(solution)/shard_map/ppermute | solution.py:307
  188.5 14.0 %all_to_all.17 = bf16[8,8,1792]{2,1,0:T(8,128)(2,1)S(1)} all-to-all(bf16[8,8,1792]{2,1,0:T(8,128)(2,1)S(1)} %shard_map.164), channel_id=1, replica_groups=mesh['context'=4,'x'=4,'z'=8,'core'=2] {'z'}, dimensions={0} | all-to-all | bytes 458752 | tf_op jit(solution)/shard_map/all_to_all | solution.py:370
  (49 shorter events, 5.3 us)
Async XLA Ops:
  0.5 59.3 %copy-start.6 = (bf16[8,1792]{1,0:T(8,128)(2,1)S(1)}, bf16[8,1792]{1,0:T(8,128)(2,1)}, u32[]{:S(2)}) copy-start(bf16[8,1792]{1,0:T(8,128)(2,1)} %residual_ref.1) | copy-start | bytes 86020
  0.5 59.3 %copy-start.8 = (s32[8,8]{1,0:T(8,128)S(1)}, s32[8,8]{1,0:T(8,128)}, u32[]{:S(2)}) copy-start(s32[8,8]{1,0:T(8,128)} %ids_ref.1) | copy-start | bytes 772
  0.5 59.3 %copy-start.9 = (f32[8,8]{1,0:T(8,128)S(1)}, f32[8,8]{1,0:T(8,128)}, u32[]{:S(2)}) copy-start(f32[8,8]{1,0:T(8,128)} %weights_ref.1) | copy-start | bytes 772
  4.3 6.8 %collective-permute-start = (bf16[144,512]{1,0:T(8,128)(2,1)S(1)}, bf16[144,512]{1,0:T(8,128)(2,1)S(1)}, u32[]{:S(2)}, u32[]{:S(2)}) collective-permute-start(bf16[144,512]{1,0:T(8,128)(2,1)S(1)} %get-tuple-element.30.refs_0_), channel_id=1, source_target_pairs={{0,64},{64,128},{128,192},{192,0},{1,65},{65,129},{129,193},{193,1... | collective-permute-start | bytes 442376 | tf_op jit(solution)/shard_map/ppermute | solution.py:307
  6.3 80.8 %copy-start.5 = (s32[4]{0:T(128)S(1)}, s32[4]{0:T(128)}, u32[]{:S(2)}) copy-start(s32[4]{0:T(128)} %compare_select_fusion.3.place) | copy-start | bytes 52
  6.3 6.6 %collective-permute-start.4 = (bf16[144,512]{1,0:T(8,128)(2,1)S(1)}, bf16[144,512]{1,0:T(8,128)(2,1)S(1)}, u32[]{:S(2)}, u32[]{:S(2)}) collective-permute-start(bf16[144,512]{1,0:T(8,128)(2,1)S(1)} %get-tuple-element.31.refs_4_), channel_id=1, source_target_pairs={{0,192},{64,0},{128,64},{192,128},{1,193},{65,1},{129,65},{193,129... | collective-permute-start | bytes 442376 | tf_op jit(solution)/shard_map/ppermute | solution.py:307
  6.4 9.1 %collective-permute-start.2 = (bf16[144,512]{1,0:T(8,128)(2,1)S(1)}, bf16[144,512]{1,0:T(8,128)(2,1)S(1)}, u32[]{:S(2)}, u32[]{:S(2)}) collective-permute-start(bf16[144,512]{1,0:T(8,128)(2,1)S(1)} %get-tuple-element.30.refs_0_), channel_id=1, source_target_pairs={{0,192},{64,0},{128,64},{192,128},{1,193},{65,1},{129,65},{193,129... | collective-permute-start | bytes 442376 | tf_op jit(solution)/shard_map/ppermute | solution.py:307
  7.2 8.4 %collective-permute-start.3 = (bf16[144,512]{1,0:T(8,128)(2,1)S(1)}, bf16[144,512]{1,0:T(8,128)(2,1)S(1)}, u32[]{:S(2)}, u32[]{:S(2)}) collective-permute-start(bf16[144,512]{1,0:T(8,128)(2,1)S(1)} %get-tuple-element.31.refs_4_), channel_id=1, source_target_pairs={{0,64},{64,128},{128,192},{192,0},{1,65},{65,129},{129,193},{193,1... | collective-permute-start | bytes 442376 | tf_op jit(solution)/shard_map/ppermute | solution.py:307
  11.1 5.2 %collective-permute-start.1 = (bf16[144,512]{1,0:T(8,128)(2,1)S(1)}, bf16[144,512]{1,0:T(8,128)(2,1)S(1)}, u32[]{:S(2)}, u32[]{:S(2)}) collective-permute-start(bf16[144,512]{1,0:T(8,128)(2,1)S(1)} %collective-permute-done.refs_1_), channel_id=1, source_target_pairs={{0,64},{64,128},{128,192},{192,0},{1,65},{65,129},{129,193},{193,1... | collective-permute-start | bytes 442376 | tf_op jit(solution)/shard_map/ppermute | solution.py:307
  12.9 6.4 %collective-permute-start.5 = (bf16[144,512]{1,0:T(8,128)(2,1)S(1)}, bf16[144,512]{1,0:T(8,128)(2,1)S(1)}, u32[]{:S(2)}, u32[]{:S(2)}) collective-permute-start(bf16[144,512]{1,0:T(8,128)(2,1)S(1)} %collective-permute-done.4.refs_7_), channel_id=1, source_target_pairs={{0,192},{64,0},{128,64},{192,128},{1,193},{65,1},{129,65},{193,129... | collective-permute-start | bytes 442376 | tf_op jit(solution)/shard_map/ppermute | solution.py:307
  19.3 1.2 copy-start.3
  20.4 0.7 copy-start.4
  21.1 138.5 %copy-start.2 = (bf16[1,7168,256]{2,1,0:T(8,128)(2,1)S(1)}, bf16[1,7168,256]{2,1,0:T(8,128)(2,1)}, u32[]{:S(2)}) copy-start(bf16[1,7168,256]{2,1,0:T(8,128)(2,1)} %param.30) | copy-start | bytes 11010052
  22.8 69.5 %copy-start = (bf16[1,256,7168]{2,1,0:T(8,128)(2,1)S(1)}, bf16[1,256,7168]{2,1,0:T(8,128)(2,1)}, u32[]{:S(2)}) copy-start(bf16[1,256,7168]{2,1,0:T(8,128)(2,1)} %param.31) | copy-start | bytes 11010052
  22.8 2.6 %collective-permute-start.6 = (bf16[256,1792]{1,0:T(8,128)(2,1)S(1)}, bf16[256,1792]{1,0:T(8,128)(2,1)S(1)}, u32[]{:S(2)}, u32[]{:S(2)}) collective-permute-start(bf16[256,1792]{1,0:T(8,128)(2,1)S(1)} %get-tuple-element.33.after_ref), channel_id=1, source_target_pairs={{0,1},{1,0},{2,3},{3,2},{4,5},{5,4},{6,7},{7,6},{8,9},{9,8},{10,11... | collective-permute-start | bytes 2752520 | tf_op jit(solution)/shard_map/ppermute | solution.py:307
  26.1 9.1 %collective-permute-start.7 = (bf16[64,1792]{1,0:T(8,128)(2,1)S(1)}, bf16[64,1792]{1,0:T(8,128)(2,1)S(1)}, u32[]{:S(2)}, u32[]{:S(2)}) collective-permute-start(bf16[64,1792]{1,0:T(8,128)(2,1)S(1)} %get-tuple-element.35), channel_id=1, source_target_pairs={{0,16},{16,32},{32,48},{48,0},{1,17},{17,33},{33,49},{49,1},{2,18}... | collective-permute-start | bytes 688136 | tf_op jit(solution)/shard_map/ppermute | solution.py:307
  27.3 13.3 %collective-permute-start.8 = (bf16[64,1792]{1,0:T(8,128)(2,1)S(1)}, bf16[64,1792]{1,0:T(8,128)(2,1)S(1)}, u32[]{:S(2)}, u32[]{:S(2)}) collective-permute-start(bf16[64,1792]{1,0:T(8,128)(2,1)S(1)} %get-tuple-element.36), channel_id=1, source_target_pairs={{0,32},{16,48},{32,0},{48,16},{1,33},{17,49},{33,1},{49,17},{2,34}... | collective-permute-start | bytes 688136 | tf_op jit(solution)/shard_map/ppermute | solution.py:307
  30.0 10.5 %collective-permute-start.9 = (bf16[64,1792]{1,0:T(8,128)(2,1)S(1)}, bf16[64,1792]{1,0:T(8,128)(2,1)S(1)}, u32[]{:S(2)}, u32[]{:S(2)}) collective-permute-start(bf16[64,1792]{1,0:T(8,128)(2,1)S(1)} %get-tuple-element.37), channel_id=1, source_target_pairs={{0,48},{16,0},{32,16},{48,32},{1,49},{17,1},{33,17},{49,33},{2,50}... | collective-permute-start | bytes 688136 | tf_op jit(solution)/shard_map/ppermute | solution.py:307
  40.7 118.9 %copy-start.1 = (bf16[1,7168,256]{2,1,0:T(8,128)(2,1)S(1)}, bf16[1,7168,256]{2,1,0:T(8,128)(2,1)}, u32[]{:S(2)}) copy-start(bf16[1,7168,256]{2,1,0:T(8,128)(2,1)} %param.29) | copy-start | bytes 11010052
  40.7 118.9 %copy-start.7 = (f32[7168]{0:T(1024)S(1)}, f32[7168]{0:T(1024)}, u32[]{:S(2)}) copy-start(f32[7168]{0:T(1024)} %param.26) | copy-start | bytes 86020
  72.7 11.0 %collective-permute-start.12 = (bf16[64,1920]{1,0:T(8,128)(2,1)S(1)}, bf16[64,1920]{1,0:T(8,128)(2,1)S(1)}, u32[]{:S(2)}, u32[]{:S(2)}) collective-permute-start(bf16[64,1920]{1,0:T(8,128)(2,1)S(1)} %bitcast.14), channel_id=1, source_target_pairs={{0,48},{16,0},{32,16},{48,32},{1,49},{17,1},{33,17},{49,33},{2,50}... | collective-permute-start | bytes 737288 | tf_op jit(solution)/shard_map/ppermute | solution.py:307
  75.8 9.2 %collective-permute-start.11 = (bf16[64,1920]{1,0:T(8,128)(2,1)S(1)}, bf16[64,1920]{1,0:T(8,128)(2,1)S(1)}, u32[]{:S(2)}, u32[]{:S(2)}) collective-permute-start(bf16[64,1920]{1,0:T(8,128)(2,1)S(1)} %bitcast.15), channel_id=1, source_target_pairs={{0,32},{16,48},{32,0},{48,16},{1,33},{17,49},{33,1},{49,17},{2,34}... | collective-permute-start | bytes 737288 | tf_op jit(solution)/shard_map/ppermute | solution.py:307
  76.2 11.0 %collective-permute-start.10 = (bf16[64,1920]{1,0:T(8,128)(2,1)S(1)}, bf16[64,1920]{1,0:T(8,128)(2,1)S(1)}, u32[]{:S(2)}, u32[]{:S(2)}) collective-permute-start(bf16[64,1920]{1,0:T(8,128)(2,1)S(1)} %bitcast.16), channel_id=1, source_target_pairs={{0,16},{16,32},{32,48},{48,0},{1,17},{17,33},{33,49},{49,1},{2,18}... | collective-permute-start | bytes 737288 | tf_op jit(solution)/shard_map/ppermute | solution.py:307
  88.8 5.2 %collective-permute-start.13 = (bf16[96,1920]{1,0:T(8,128)(2,1)S(1)}, bf16[96,1920]{1,0:T(8,128)(2,1)S(1)}, u32[]{:S(2)}, u32[]{:S(2)}) collective-permute-start(bf16[96,1920]{1,0:T(8,128)(2,1)S(1)} %get-tuple-element.41), channel_id=1, source_target_pairs={{0,1},{1,0},{2,3},{3,2},{4,5},{5,4},{6,7},{7,6},{8,9},{9,8},{10,11... | collective-permute-start | bytes 1105928 | tf_op jit(solution)/shard_map/ppermute | solution.py:307
  88.9 32.4 %collective-permute-start.19 = (bf16[96,1920]{1,0:T(8,128)(2,1)S(1)}, bf16[96,1920]{1,0:T(8,128)(2,1)S(1)}, u32[]{:S(2)}, u32[]{:S(2)}) collective-permute-start(bf16[96,1920]{1,0:T(8,128)(2,1)S(1)} %get-tuple-element.40.refs_0_), channel_id=1, source_target_pairs={{0,192},{64,0},{128,64},{192,128},{1,193},{65,1},{129,65},{193,129... | collective-permute-start | bytes 1105928 | tf_op jit(solution)/shard_map/ppermute | solution.py:307
  89.0 32.3 %collective-permute-start.14 = (bf16[96,1920]{1,0:T(8,128)(2,1)S(1)}, bf16[96,1920]{1,0:T(8,128)(2,1)S(1)}, u32[]{:S(2)}, u32[]{:S(2)}) collective-permute-start(bf16[96,1920]{1,0:T(8,128)(2,1)S(1)} %get-tuple-element.40.refs_0_), channel_id=1, source_target_pairs={{0,64},{64,128},{128,192},{192,0},{1,65},{65,129},{129,193},{193,1... | collective-permute-start | bytes 1105928 | tf_op jit(solution)/shard_map/ppermute | solution.py:307
  93.0 72.0 %collective-permute-start.23 = (bf16[256,1792]{1,0:T(8,128)(2,1)S(1)}, bf16[256,1792]{1,0:T(8,128)(2,1)S(1)}, u32[]{:S(2)}, u32[]{:S(2)}) collective-permute-start(bf16[256,1792]{1,0:T(8,128)(2,1)S(1)} %get-tuple-element.43), channel_id=1, source_target_pairs={{0,64},{64,128},{128,192},{192,0},{1,65},{65,129},{129,193},{193,1... | collective-permute-start | bytes 2752520 | tf_op jit(solution)/shard_map/ppermute | solution.py:307
  93.1 72.5 %collective-permute-start.24 = (bf16[256,1792]{1,0:T(8,128)(2,1)S(1)}, bf16[256,1792]{1,0:T(8,128)(2,1)S(1)}, u32[]{:S(2)}, u32[]{:S(2)}) collective-permute-start(bf16[256,1792]{1,0:T(8,128)(2,1)S(1)} %get-tuple-element.44), channel_id=1, source_target_pairs={{0,128},{64,192},{128,0},{192,64},{1,129},{65,193},{129,1},{193,65... | collective-permute-start | bytes 2752520 | tf_op jit(solution)/shard_map/ppermute | solution.py:307
  94.0 71.5 %collective-permute-start.25 = (bf16[256,1792]{1,0:T(8,128)(2,1)S(1)}, bf16[256,1792]{1,0:T(8,128)(2,1)S(1)}, u32[]{:S(2)}, u32[]{:S(2)}) collective-permute-start(bf16[256,1792]{1,0:T(8,128)(2,1)S(1)} %get-tuple-element.45), channel_id=1, source_target_pairs={{0,192},{64,0},{128,64},{192,128},{1,193},{65,1},{129,65},{193,129... | collective-permute-start | bytes 2752520 | tf_op jit(solution)/shard_map/ppermute | solution.py:307
  121.3 27.0 %collective-permute-start.17 = (bf16[96,1920]{1,0:T(8,128)(2,1)S(1)}, bf16[96,1920]{1,0:T(8,128)(2,1)S(1)}, u32[]{:S(2)}, u32[]{:S(2)}) collective-permute-start(bf16[96,1920]{1,0:T(8,128)(2,1)S(1)} %collective-permute-done.13.refs_1_), channel_id=1, source_target_pairs={{0,192},{64,0},{128,64},{192,128},{1,193},{65,1},{129,65},{193,129... | collective-permute-start | bytes 1105928 | tf_op jit(solution)/shard_map/ppermute | solution.py:307
  121.3 27.0 %collective-permute-start.15 = (bf16[96,1920]{1,0:T(8,128)(2,1)S(1)}, bf16[96,1920]{1,0:T(8,128)(2,1)S(1)}, u32[]{:S(2)}, u32[]{:S(2)}) collective-permute-start(bf16[96,1920]{1,0:T(8,128)(2,1)S(1)} %collective-permute-done.13.refs_1_), channel_id=1, source_target_pairs={{0,64},{64,128},{128,192},{192,0},{1,65},{65,129},{129,193},{193,1... | collective-permute-start | bytes 1105928 | tf_op jit(solution)/shard_map/ppermute | solution.py:307
  148.3 10.1 %collective-permute-start.16 = (bf16[96,1920]{1,0:T(8,128)(2,1)S(1)}, bf16[96,1920]{1,0:T(8,128)(2,1)S(1)}, u32[]{:S(2)}, u32[]{:S(2)}) collective-permute-start(bf16[96,1920]{1,0:T(8,128)(2,1)S(1)} %collective-permute-done.14.refs_2_), channel_id=1, source_target_pairs={{0,64},{64,128},{128,192},{192,0},{1,65},{65,129},{129,193},{193,1... | collective-permute-start | bytes 1105928 | tf_op jit(solution)/shard_map/ppermute | solution.py:307
  148.4 11.3 %collective-permute-start.18 = (bf16[96,1920]{1,0:T(8,128)(2,1)S(1)}, bf16[96,1920]{1,0:T(8,128)(2,1)S(1)}, u32[]{:S(2)}, u32[]{:S(2)}) collective-permute-start(bf16[96,1920]{1,0:T(8,128)(2,1)S(1)} %collective-permute-done.17.refs_7_), channel_id=1, source_target_pairs={{0,192},{64,0},{128,64},{192,128},{1,193},{65,1},{129,65},{193,129... | collective-permute-start | bytes 1105928 | tf_op jit(solution)/shard_map/ppermute | solution.py:307
  162.0 7.0 %collective-permute-start.22 = (bf16[192,256]{1,0:T(8,128)(2,1)S(1)}, bf16[192,256]{1,0:T(8,128)(2,1)S(1)}, u32[]{:S(2)}, u32[]{:S(2)}) collective-permute-start(bf16[192,256]{1,0:T(8,128)(2,1)S(1)} %get-tuple-element.42.refs_0_), channel_id=1, source_target_pairs={{0,192},{64,0},{128,64},{192,128},{1,193},{65,1},{129,65},{193,129... | collective-permute-start | bytes 294920 | tf_op jit(solution)/shard_map/ppermute | solution.py:307
  162.6 6.3 %collective-permute-start.21 = (bf16[192,256]{1,0:T(8,128)(2,1)S(1)}, bf16[192,256]{1,0:T(8,128)(2,1)S(1)}, u32[]{:S(2)}, u32[]{:S(2)}) collective-permute-start(bf16[192,256]{1,0:T(8,128)(2,1)S(1)} %get-tuple-element.42.refs_0_), channel_id=1, source_target_pairs={{0,128},{64,192},{128,0},{192,64},{1,129},{65,193},{129,1},{193,65... | collective-permute-start | bytes 294920 | tf_op jit(solution)/shard_map/ppermute | solution.py:307
  165.0 4.9 %collective-permute-start.20 = (bf16[192,256]{1,0:T(8,128)(2,1)S(1)}, bf16[192,256]{1,0:T(8,128)(2,1)S(1)}, u32[]{:S(2)}, u32[]{:S(2)}) collective-permute-start(bf16[192,256]{1,0:T(8,128)(2,1)S(1)} %get-tuple-element.42.refs_0_), channel_id=1, source_target_pairs={{0,64},{64,128},{128,192},{192,0},{1,65},{65,129},{129,193},{193,1... | collective-permute-start | bytes 294920 | tf_op jit(solution)/shard_map/ppermute | solution.py:307
  171.3 1.7 collective-permute-start.26
  173.6 8.6 %collective-permute-start.27 = (bf16[64,1792]{1,0:T(8,128)(2,1)S(1)}, bf16[64,1792]{1,0:T(8,128)(2,1)S(1)}, u32[]{:S(2)}, u32[]{:S(2)}) collective-permute-start(bf16[64,1792]{1,0:T(8,128)(2,1)S(1)} %get-tuple-element.52), channel_id=1, source_target_pairs={{0,48},{16,0},{32,16},{48,32},{1,49},{17,1},{33,17},{49,33},{2,50}... | collective-permute-start | bytes 688136 | tf_op jit(solution)/shard_map/ppermute | solution.py:307
  174.6 10.0 %collective-permute-start.28 = (bf16[64,1792]{1,0:T(8,128)(2,1)S(1)}, bf16[64,1792]{1,0:T(8,128)(2,1)S(1)}, u32[]{:S(2)}, u32[]{:S(2)}) collective-permute-start(bf16[64,1792]{1,0:T(8,128)(2,1)S(1)} %get-tuple-element.53), channel_id=1, source_target_pairs={{0,32},{16,48},{32,0},{48,16},{1,33},{17,49},{33,1},{49,17},{2,34}... | collective-permute-start | bytes 688136 | tf_op jit(solution)/shard_map/ppermute | solution.py:307
  174.9 13.5 %collective-permute-start.29 = (bf16[64,1792]{1,0:T(8,128)(2,1)S(1)}, bf16[64,1792]{1,0:T(8,128)(2,1)S(1)}, u32[]{:S(2)}, u32[]{:S(2)}) collective-permute-start(bf16[64,1792]{1,0:T(8,128)(2,1)S(1)} %get-tuple-element.54), channel_id=1, source_target_pairs={{0,16},{16,32},{32,48},{48,0},{1,17},{17,33},{33,49},{49,1},{2,18}... | collective-permute-start | bytes 688136 | tf_op jit(solution)/shard_map/ppermute | solution.py:307

commit v4 on v3

--- a/solution.py
+++ b/solution.py
@@ -128,7 +128,9 @@
 
 def merge_kernel(place, *refs):
     core = place[2]
-    parts, (weight_ref, send_ref, keep_ref, scratch) = refs[:8], refs[8:]
+    parts, (weight_ref, send_ref, keep_ref, scratch, weight, done) = refs[:8], refs[8:]
+    load = pltpu.make_async_copy(weight_ref, weight, done)
+    load.start()
     heads = []
     for head in range(2):
         own = parts[4 * head : 4 * head + 4]
@@ -144,7 +146,8 @@
             mixed = mixed + part[:VD, :].astype(F32) * (share * inverse)
         heads.append(mixed)
     attention = jnp.concatenate(heads, axis=0).T.astype(BF16)
-    scratch[...] = dot_nn(attention, weight_ref[...]).reshape(scratch.shape)
+    load.wait()
+    scratch[...] = dot_nn(attention, weight[...]).reshape(scratch.shape)
     send_ref[...] = scratch[:, 1 - core].reshape(send_ref.shape).astype(BF16)
     keep_ref[...] = scratch[:, core].reshape(keep_ref.shape)
 
@@ -204,28 +207,53 @@
         payload_ref[index, :, width:] = tail
 
 
-def select_kernel(place, *refs):
-    parts, (low_ref, send_ref, pick_ref, other_ref) = refs[:4], refs[4:]
-    rows, slots = pick_ref.shape
-    values = jnp.concatenate([part[...] for part in parts], axis=0)
+def select_kernel(place, rows_ref, pick_ref, *outs):
+    rows = rows_ref.shape[0]
+    count = len(outs)
+    slots = pick_ref.shape[1] // (2 * count)
+    values = rows_ref[...]
     width = values.shape[1] - TAIL
     tails = values[:, width:].astype(F32)
     lane = iota((rows, TAIL), 1)
+    base = place[1] - place[3] * place[4]
+    named = jnp.zeros((rows, TAIL), F32)
+    for index in range(2 * count):
+        expert = lax.rem(place[3] + index // 2, count) * place[4] + base
+        if index % 2:
+            expert = expert + 1 - 2 * place[2]
+        found = jnp.max(
+            jnp.where((tails == expert.astype(F32)) & (lane < 8), 1.0, 0.0), axis=1, keepdims=True
+        )
+        named = jnp.where(lane == index, found, named)
     ahead = (iota((rows, rows), 1) < iota((rows, rows), 0)) & (
         iota((rows, rows), 1) // 8 == iota((rows, rows), 0) // 8
     )
-    ahead = jnp.where(ahead, 1.0, 0.0).astype(BF16)
-    first = (iota((rows, 1), 0) // 8 * CAP).astype(F32)
-    slot = iota((rows, slots), 1).astype(F32)
-    partner = place[1] + 1 - 2 * place[2]
-    for expert, out, keep in ((place[1], low_ref, pick_ref), (partner, send_ref, other_ref)):
-        named = jnp.max(
-            jnp.where((tails == expert.astype(F32)) & (lane < 8), 1.0, 0.0), axis=1, keepdims=True
-        )
-        before = dot_nn(ahead, jnp.broadcast_to(named, (rows, TAIL)).astype(BF16))[:, :1]
-        pick = jnp.where((slot == first + before) & (named > 0.5), 1.0, 0.0)
-        keep[...] = pick.astype(BF16)
-        out[...] = dot_nn(pick.T.astype(BF16), values).astype(BF16)
+    before = dot_nn(jnp.where(ahead, 1.0, 0.0).astype(BF16), named.astype(BF16))
+    slot_of = before + (iota((rows, TAIL), 0) // 8 * CAP).astype(F32)
+    slot = iota((rows, pick_ref.shape[1]), 1).astype(F32)
+    pick = jnp.zeros((rows, pick_ref.shape[1]), F32)
+    for index in range(2 * count):
+        match = slot == slot_of[:, index : index + 1] + float(index * slots)
+        pick = jnp.where(match & (named[:, index : index + 1] > 0.5), 1.0, pick)
+    pick_ref[...] = pick.astype(BF16)
+    chosen = dot_nn(pick.T.astype(BF16), values).astype(BF16)
+    for step, out in enumerate(outs):
+        out[...] = chosen[2 * slots * step : 2 * slots * (step + 1)]
+
+
+def sort_kernel(*refs):
+    parts, (low_ref, send_ref) = refs[:-2], refs[-2:]
+    slots = parts[0].shape[0] // 2
+    for step, part in enumerate(parts):
+        low_ref[step * slots : (step + 1) * slots, :] = part[:slots, :]
+        send_ref[step * slots : (step + 1) * slots, :] = part[slots:, :]
+
+
+def back_kernel(low_ref, got_ref, *outs):
+    slots = outs[0].shape[0] // 2
+    for step, out in enumerate(outs):
+        out[:slots, :] = low_ref[step * slots : (step + 1) * slots, :]
+        out[slots:, :] = got_ref[step * slots : (step + 1) * slots, :]
 
 
 def expert_kernel(place, *refs):
@@ -281,26 +309,33 @@
     high_ref[...] = made[half:]
 
 
-def spread_kernel(low_ref, got_ref, pick_ref, other_ref, own_ref, *sends):
-    rows = own_ref.shape[0]
-    total = dot_nn(pick_ref[...], low_ref[...]) + dot_nn(other_ref[...], got_ref[...])
-    own_ref[...] = total[:rows]
-    for step, send in enumerate(sends, 1):
-        send[...] = total[step * rows : (step + 1) * rows].astype(BF16)
-
-
-def call(kernel, outs, inputs, scalars=0, scratch=(), limit=16, hold=True):
-    held = inputs[scalars:]
-    if hold:
-        held = [pltpu.with_memory_space_constraint(value, pltpu.VMEM) for value in held]
+def spread_kernel(pick_ref, *refs):
+    values = jnp.concatenate([ref[...] for ref in refs[:-1]], axis=0)
+    refs[-1][...] = dot_nn(pick_ref[...], values).astype(BF16).reshape(refs[-1].shape)
+
+
+def output_kernel(parts_ref, hidden_ref, out_ref):
+    total = parts_ref[0].astype(F32)
+    for index in range(1, parts_ref.shape[0]):
+        total = total + parts_ref[index].astype(F32)
+    out_ref[...] = (hidden_ref[...].astype(F32) + total).astype(BF16)
+
+
+def call(kernel, outs, inputs, scalars=0, scratch=(), limit=16, hold=True, raw=0):
+    last = len(inputs) - raw
+    spaces = [pltpu.SMEM] * scalars
+    spaces += [pltpu.VMEM if hold else pltpu.HBM] * (last - scalars)
+    spaces += [pltpu.HBM] * raw
+    specs = [SMEM] * scalars + [VMEM] * (last - scalars)
+    specs += [pl.BlockSpec(memory_space=pl.ANY)] * raw
     return pl.pallas_call(
         kernel,
         out_shape=tuple(pltpu.VMEM(shape, dtype) for shape, dtype in outs),
-        in_specs=[SMEM] * scalars + [VMEM] * len(held),
+        in_specs=specs,
         out_specs=tuple(VMEM for _ in outs),
         scratch_shapes=list(scratch),
         compiler_params=pltpu.CompilerParams(vmem_limit_bytes=limit << 20),
-    )(*inputs[:scalars], *held)
+    )(*[pltpu.with_memory_space_constraint(v, space) for v, space in zip(inputs, spaces)])
 
 
 def shift(value, axis, count, step):
@@ -333,9 +368,15 @@
     full = width + TAIL
     hidden_units = gate_matrix.shape[2]
     expert = lax.axis_index(EXPERT)
-    places = (lax.axis_index(CONTEXT), expert, lax.axis_index(CORE), lax.axis_index(WIDE))
-    number = jnp.arange(4, dtype=jnp.int32)
-    place = jnp.zeros((4,), jnp.int32)
+    places = (
+        lax.axis_index(CONTEXT),
+        expert,
+        lax.axis_index(CORE),
+        lax.axis_index(WIDE),
+        2 * deep,
+    )
+    number = jnp.arange(8, dtype=jnp.int32)
+    place = jnp.zeros((8,), jnp.int32)
     for index, value in enumerate(places):
         place = jnp.where(number == index, value, place)
 
@@ -355,7 +396,7 @@
         ],
         scalars=1,
         hold=False,
-        limit=56,
+        limit=24,
     )
 
     def around(low, high):
@@ -363,11 +404,6 @@
         low3, high3 = shift(low, CONTEXT, ring, -1), shift(high, CONTEXT, ring, -1)
         low2, high2 = shift(low1, CONTEXT, ring, 1), shift(high3, CONTEXT, ring, -1)
         return (low, low1, low2, low3), (high, high1, high2, high3)
-
-    def gather(own, sends):
-        chunk = [((deep, row_dev, width), BF16)]
-        (summed,) = call(sum_kernel, chunk, [own, *sends])
-        return lax.all_to_all(summed, DEEP, 0, 0, tiled=True)
 
     lows, highs = around(low, high)
     send, keep = call(
@@ -375,7 +411,12 @@
         [((half, width), BF16), ((half, width), F32)],
         [place, *lows, *highs, out_weight],
         scalars=1,
-        scratch=[pltpu.VMEM((wide * deep, 2, row_dev, width), F32)],
+        scratch=[
+            pltpu.VMEM((wide * deep, 2, row_dev, width), F32),
+            pltpu.VMEM(out_weight.shape, BF16),
+            pltpu.SemaphoreType.DMA(()),
+        ],
+        raw=1,
     )
     cuts = call(
         cut_kernel,
@@ -389,20 +430,27 @@
     split = [((half // wide, width), F32)] + [((half // wide, width), BF16)] * (wide - 1)
     got = shift(send, CORE, 2, 1)
     own, *sends = call(add_kernel, split, [place, keep, got], scalars=1)
-    mixed = gather(own, [shift(part, WIDE, wide, step) for step, part in enumerate(sends, 1)])
+    received = []
+    for step, part in enumerate(sends, 1):
+        received.append(shift(part, WIDE, wide, step))
+    chunk = [((deep, row_dev, width), BF16)]
+    (summed,) = call(sum_kernel, chunk, [own, *received])
+    mixed = lax.all_to_all(summed, DEEP, 0, 0, tiled=True)
     hidden, payload = call(
         hidden_kernel,
         [((row_dev, width), BF16), ((deep, row_dev, full), BF16)],
         [mixed, residual, expert_ids, route_weights],
     )
     near = lax.all_to_all(payload, DEEP, 0, 0, tiled=True).reshape(deep * row_dev, full)
-    parts = [near] + [shift(near, WIDE, wide, step) for step in range(1, wide)]
-    low, send, pick, pick_other = call(
+    share_slots = slots // wide
+    pick, *parts = call(
         select_kernel,
-        [((slots // 2, full), BF16)] * 2 + [((half, slots // 2), BF16)] * 2,
-        [place, *parts],
+        [((deep * row_dev, slots), BF16)] + [((share_slots, full), BF16)] * wide,
+        [place, near],
         scalars=1,
     )
+    parts = [shift(part, WIDE, wide, step) if step else part for step, part in enumerate(parts)]
+    low, send = call(sort_kernel, [((slots // 2, full), BF16)] * 2, parts)
     lows, highs = around(low, shift(send, CORE, 2, 1))
     active, share = call(
         expert_kernel,
@@ -423,12 +471,16 @@
         [place, *actives, *others, down_matrix[0], share],
         scalars=1,
     )
-    own, *sends = call(
-        spread_kernel, split, [low, shift(high, CORE, 2, 1), pick, pick_other]
-    )
-    returned = gather(own, [shift(part, WIDE, wide, -step) for step, part in enumerate(sends, 1)])
-    total = jnp.sum(returned.astype(F32), axis=0)
-    return (hidden.astype(F32) + total).astype(BF16)
+    parts = call(
+        back_kernel,
+        [((share_slots, width), BF16)] * wide,
+        [low, shift(high, CORE, 2, 1)],
+    )
+    parts = [shift(part, WIDE, wide, -step) if step else part for step, part in enumerate(parts)]
+    (summed,) = call(spread_kernel, chunk, [pick, *parts])
+    returned = lax.all_to_all(summed, DEEP, 0, 0, tiled=True)
+    (out,) = call(output_kernel, [((row_dev, width), BF16)], [returned, hidden])
+    return out
 
 
 def solution(mesh):

time: 206 us -> 199 us (0.966)
  waiting for transfers between devices: 108 us -> 99.9 us
  starting transfers between devices: 33.3 us -> 35.9 us
    ppermute x30, waiting for transfers between devices: 108 us -> 99.9 us  [shift(): lax.ppermute(value, axis, [(i, (i + step) % count) for i in range(count)])]
    ppermute x30, starting transfers between devices: 33.3 us -> 35.9 us  [shift(): lax.ppermute(value, axis, [(i, (i + step) % count) for i in range(count)])]
    pallas_call x11 -> x13, Pallas kernels: 13.3 us -> 14.2 us  [call(): pl.pallas_call(kernel, out_shape=tuple((pltpu.VMEM(shape, dtype) for shap...]
  transfers between devices with their start and end apart: 30 -> 30, of which waited for: 20 -> 19; matrix products, arithmetic and copies ran while one was open for 0% -> 0% of each run, Pallas kernels for 1% -> 2%
where the time goes in v4:
time: 199 us; the launch traced here: 197 us
  waiting for transfers between devices  99.9 us (50%)
  blocking collectives  45.9 us (23%)
  starting transfers between devices  35.9 us (18%)
  Pallas kernels  14.2 us (7%)
    ppermute x30, waiting for transfers between devices, shift(): lax.ppermute(value, axis, [(i, (i + step) % count) for i in range(count)])  99.9 us
    ppermute x30, starting transfers between devices, shift(): lax.ppermute(value, axis, [(i, (i + step) % count) for i in range(count)])  35.9 us
    all_to_all x1, blocking collectives, local(): mixed = lax.all_to_all(summed, DEEP, 0, 0, tiled=True)  19.1 us
    pallas_call x13, Pallas kernels, call(): pl.pallas_call(kernel, out_shape=tuple((pltpu.VMEM(shape, dtype) for shap...  14.2 us
    all_to_all x1, blocking collectives, local(): returned = lax.all_to_all(summed, DEEP, 0, 0, tiled=True)  14 us
    all_to_all x1, blocking collectives, local(): lax.all_to_all(payload, DEEP, 0, 0, tiled=True)  12.7 us
  transfers between devices with their start and end apart: 30, of which 19 were waited for; matrix products, arithmetic and copies ran while one was open for 0% of the time, Pallas kernels for 2%

profile of v4, /device:TPU:24, one launch (start us, length us, event | category | flops | bytes accessed | tf_op | source)
XLA Modules:
  0.0 196.6 jit_solution(14471514239304132339)
XLA Ops:
  0.0 3.8 %shard_map.154 = (bf16[144,512]{1,0:T(8,128)(2,1)S(1)}, bf16[144,512]{1,0:T(8,128)(2,1)S(1)}) custom-call(s32[8]{0:T(128)S(1)} %compare_select_fusion.4.place, bf16[512,384]{1,0:T(8,128)(2,1)} %q_ref.1, bf16[2,128,512]{2,1,0:T(8,128)(2,1)} %kl_ref.1, bf16[2,512,128]{2,1,0:T(8,128)(2,1)} %vl_ref.1, bf16[256,576]{1,0:T(8,128)(2,1)} %bitcast.16, ...), custom_call_target="tpu_custom_call" | custom-call | tf_op jit(solution)/shard_map/pallas_call | solution.py:331
  3.8 2.0 %collective-permute-start = (bf16[144,512]{1,0:T(8,128)(2,1)S(1)}, bf16[144,512]{1,0:T(8,128)(2,1)S(1)}, u32[]{:S(2)}, u32[]{:S(2)}) collective-permute-start(bf16[144,512]{1,0:T(8,128)(2,1)S(1)} %get-tuple-element.33.refs_0_), channel_id=1, source_target_pairs={{0,64},{64,128},{128,192},{192,0},{1,65},{65,129},{129,193},{193,1... | collective-permute-start | bytes 442376 | tf_op jit(solution)/shard_map/ppermute | solution.py:342
  5.9 0.7 collective-permute-start.2
  6.7 2.5 %collective-permute-start.3 = (bf16[144,512]{1,0:T(8,128)(2,1)S(1)}, bf16[144,512]{1,0:T(8,128)(2,1)S(1)}, u32[]{:S(2)}, u32[]{:S(2)}) collective-permute-start(bf16[144,512]{1,0:T(8,128)(2,1)S(1)} %get-tuple-element.34.refs_4_), channel_id=1, source_target_pairs={{0,64},{64,128},{128,192},{192,0},{1,65},{65,129},{129,193},{193,1... | collective-permute-start | bytes 442376 | tf_op jit(solution)/shard_map/ppermute | solution.py:342
  9.2 1.5 collective-permute-done.refs_1_
  10.6 1.8 collective-permute-start.1
  12.7 2.4 %collective-permute-done.2.refs_3_ = bf16[144,512]{1,0:T(8,128)(2,1)S(1)} collective-permute-done((bf16[144,512]{1,0:T(8,128)(2,1)S(1)}, bf16[144,512]{1,0:T(8,128)(2,1)S(1)}, u32[]{:S(2)}, u32[]{:S(2)}) %collective-permute-start.2) | collective-permute-done | bytes 147488 | tf_op jit(solution)/shard_map/ppermute | solution.py:342
  15.1 0.7 collective-permute-done.1.refs_2_
  15.8 2.9 %collective-permute-done.5.refs_6_ = bf16[144,512]{1,0:T(8,128)(2,1)S(1)} collective-permute-done((bf16[144,512]{1,0:T(8,128)(2,1)S(1)}, bf16[144,512]{1,0:T(8,128)(2,1)S(1)}, u32[]{:S(2)}, u32[]{:S(2)}) %collective-permute-start.5) | collective-permute-done | bytes 147488 | tf_op jit(solution)/shard_map/ppermute | solution.py:342
  18.7 3.1 %shard_map.155 = (bf16[256,1792]{1,0:T(8,128)(2,1)S(1)}, f32[256,1792]{1,0:T(8,128)S(1)}) custom-call(s32[8]{0:T(128)S(1)} %compare_select_fusion.4.place, bf16[144,512]{1,0:T(8,128)(2,1)S(1)} %get-tuple-element.33.refs_0_, bf16[144,512]{1,0:T(8,128)(2,1)S(1)} %collective-permute-done.refs_1_, bf16[144,512]{1,0:T(8,128)(2,1)S(1)} %collective-permute-done.1.refs_2_, ...), custom_call_target="tpu_custom_call" | custom-call | tf_op jit(solution)/shard_map/pallas_call | solution.py:331
  22.0 2.5 %collective-permute-done.6.got_ref = bf16[256,1792]{1,0:T(8,128)(2,1)S(1)} collective-permute-done((bf16[256,1792]{1,0:T(8,128)(2,1)S(1)}, bf16[256,1792]{1,0:T(8,128)(2,1)S(1)}, u32[]{:S(2)}, u32[]{:S(2)}) %collective-permute-start.6) | collective-permute-done | bytes 917536 | tf_op jit(solution)/shard_map/ppermute | solution.py:342
  24.5 0.7 shard_map.156
  25.2 1.2 collective-permute-start.7
  26.5 2.7 %collective-permute-start.8 = (bf16[64,1792]{1,0:T(8,128)(2,1)S(1)}, bf16[64,1792]{1,0:T(8,128)(2,1)S(1)}, u32[]{:S(2)}, u32[]{:S(2)}) collective-permute-start(bf16[64,1792]{1,0:T(8,128)(2,1)S(1)} %get-tuple-element.39), channel_id=1, source_target_pairs={{0,32},{16,48},{32,0},{48,16},{1,33},{17,49},{33,1},{49,17},{2,34}... | collective-permute-start | bytes 688136 | tf_op jit(solution)/shard_map/ppermute | solution.py:342
  29.2 1.4 collective-permute-start.9
  30.6 3.7 %collective-permute-done.7.refs_0_ = bf16[64,1792]{1,0:T(8,128)(2,1)S(1)} collective-permute-done((bf16[64,1792]{1,0:T(8,128)(2,1)S(1)}, bf16[64,1792]{1,0:T(8,128)(2,1)S(1)}, u32[]{:S(2)}, u32[]{:S(2)}) %collective-permute-start.7) | collective-permute-done | bytes 229408 | tf_op jit(solution)/shard_map/ppermute | solution.py:342
  34.3 5.4 %collective-permute-done.8.refs_1_ = bf16[64,1792]{1,0:T(8,128)(2,1)S(1)} collective-permute-done((bf16[64,1792]{1,0:T(8,128)(2,1)S(1)}, bf16[64,1792]{1,0:T(8,128)(2,1)S(1)}, u32[]{:S(2)}, u32[]{:S(2)}) %collective-permute-start.8) | collective-permute-done | bytes 229408 | tf_op jit(solution)/shard_map/ppermute | solution.py:342
  39.9 19.1 %all_to_all.15.parts_ref = bf16[8,8,1792]{2,1,0:T(8,128)(2,1)S(1)} all-to-all(bf16[8,8,1792]{2,1,0:T(8,128)(2,1)S(1)} %shard_map.157), channel_id=1, replica_groups=mesh['context'=4,'x'=4,'z'=8,'core'=2] {'z'}, dimensions={0} | all-to-all | bytes 458752 | tf_op jit(solution)/shard_map/all_to_all | solution.py:438
  59.2 12.7 %all_to_all.16 = bf16[8,8,1920]{2,1,0:T(8,128)(2,1)S(1)} all-to-all(bf16[8,8,1920]{2,1,0:T(8,128)(2,1)S(1)} %get-tuple-element.41), channel_id=1, replica_groups=mesh['context'=4,'x'=4,'z'=8,'core'=2] {'z'}, dimensions={0} | all-to-all | bytes 491520 | tf_op jit(solution)/shard_map/all_to_all | solution.py:444
  71.9 1.4 shard_map.159
  73.3 1.6 collective-permute-start.10
  74.9 3.1 %collective-permute-start.11 = (bf16[48,1920]{1,0:T(8,128)(2,1)S(1)}, bf16[48,1920]{1,0:T(8,128)(2,1)S(1)}, u32[]{:S(2)}, u32[]{:S(2)}) collective-permute-start(bf16[48,1920]{1,0:T(8,128)(2,1)S(1)} %get-tuple-element.45), channel_id=1, source_target_pairs={{0,32},{16,48},{32,0},{48,16},{1,33},{17,49},{33,1},{49,17},{2,34}... | collective-permute-start | bytes 552968 | tf_op jit(solution)/shard_map/ppermute | solution.py:342
  78.6 3.3 %collective-permute-done.10.refs_1_ = bf16[48,1920]{1,0:T(8,128)(2,1)S(1)} collective-permute-done((bf16[48,1920]{1,0:T(8,128)(2,1)S(1)}, bf16[48,1920]{1,0:T(8,128)(2,1)S(1)}, u32[]{:S(2)}, u32[]{:S(2)}) %collective-permute-start.10) | collective-permute-done | bytes 184352 | tf_op jit(solution)/shard_map/ppermute | solution.py:342
  81.9 2.0 %collective-permute-done.11.refs_2_ = bf16[48,1920]{1,0:T(8,128)(2,1)S(1)} collective-permute-done((bf16[48,1920]{1,0:T(8,128)(2,1)S(1)}, bf16[48,1920]{1,0:T(8,128)(2,1)S(1)}, u32[]{:S(2)}, u32[]{:S(2)}) %collective-permute-start.11) | collective-permute-done | bytes 184352 | tf_op jit(solution)/shard_map/ppermute | solution.py:342
  84.1 3.2 %collective-permute-start.14 = (bf16[96,1920]{1,0:T(8,128)(2,1)S(1)}, bf16[96,1920]{1,0:T(8,128)(2,1)S(1)}, u32[]{:S(2)}, u32[]{:S(2)}) collective-permute-start(bf16[96,1920]{1,0:T(8,128)(2,1)S(1)} %get-tuple-element.47.refs_0_), channel_id=1, source_target_pairs={{0,64},{64,128},{128,192},{192,0},{1,65},{65,129},{129,193},{193,1... | collective-permute-start | bytes 1105928 | tf_op jit(solution)/shard_map/ppermute | solution.py:342
  87.3 0.7 shard_map.162
  88.2 0.9 collective-permute-start.24
  89.1 1.1 collective-permute-start.25
  90.2 26.2 %collective-permute-done.19.refs_6_ = bf16[96,1920]{1,0:T(8,128)(2,1)S(1)} collective-permute-done((bf16[96,1920]{1,0:T(8,128)(2,1)S(1)}, bf16[96,1920]{1,0:T(8,128)(2,1)S(1)}, u32[]{:S(2)}, u32[]{:S(2)}) %collective-permute-start.19) | collective-permute-done | bytes 368672 | tf_op jit(solution)/shard_map/ppermute | solution.py:342
  116.4 3.2 %collective-permute-start.15 = (bf16[96,1920]{1,0:T(8,128)(2,1)S(1)}, bf16[96,1920]{1,0:T(8,128)(2,1)S(1)}, u32[]{:S(2)}, u32[]{:S(2)}) collective-permute-start(bf16[96,1920]{1,0:T(8,128)(2,1)S(1)} %collective-permute-done.13.refs_1_), channel_id=1, source_target_pairs={{0,64},{64,128},{128,192},{192,0},{1,65},{65,129},{129,193},{193,1... | collective-permute-start | bytes 1105928 | tf_op jit(solution)/shard_map/ppermute | solution.py:342
  119.7 23.8 %collective-permute-done.17.refs_7_ = bf16[96,1920]{1,0:T(8,128)(2,1)S(1)} collective-permute-done((bf16[96,1920]{1,0:T(8,128)(2,1)S(1)}, bf16[96,1920]{1,0:T(8,128)(2,1)S(1)}, u32[]{:S(2)}, u32[]{:S(2)}) %collective-permute-start.17) | collective-permute-done | bytes 368672 | tf_op jit(solution)/shard_map/ppermute | solution.py:342
  143.4 2.0 %collective-permute-start.18 = (bf16[96,1920]{1,0:T(8,128)(2,1)S(1)}, bf16[96,1920]{1,0:T(8,128)(2,1)S(1)}, u32[]{:S(2)}, u32[]{:S(2)}) collective-permute-start(bf16[96,1920]{1,0:T(8,128)(2,1)S(1)} %collective-permute-done.17.refs_7_), channel_id=1, source_target_pairs={{0,192},{64,0},{128,64},{192,128},{1,193},{65,1},{129,65},{193,129... | collective-permute-start | bytes 1105928 | tf_op jit(solution)/shard_map/ppermute | solution.py:342
  145.5 8.0 %collective-permute-done.16.refs_4_ = bf16[96,1920]{1,0:T(8,128)(2,1)S(1)} collective-permute-done((bf16[96,1920]{1,0:T(8,128)(2,1)S(1)}, bf16[96,1920]{1,0:T(8,128)(2,1)S(1)}, u32[]{:S(2)}, u32[]{:S(2)}) %collective-permute-start.16) | collective-permute-done | bytes 368672 | tf_op jit(solution)/shard_map/ppermute | solution.py:342
  153.5 1.2 collective-permute-done.18.refs_5_
  154.7 2.3 %shard_map.161 = (bf16[192,256]{1,0:T(8,128)(2,1)S(1)}, f32[192,128]{1,0:T(8,128)S(1)}) custom-call(s32[8]{0:T(128)S(1)} %compare_select_fusion.4.place, bf16[96,1920]{1,0:T(8,128)(2,1)S(1)} %get-tuple-element.47.refs_0_, bf16[96,1920]{1,0:T(8,128)(2,1)S(1)} %collective-permute-done.13.refs_1_, bf16[96,1920]{1,0:T(8,128)(2,1)S(1)} %collective-permute-done.14.refs_2_, ...), custom_call_target="tpu_custom_call" | custom-call | tf_op jit(solution)/shard_map/pallas_call | solution.py:331
  157.0 0.6 collective-permute-start.22
  157.6 2.4 %collective-permute-start.21 = (bf16[192,256]{1,0:T(8,128)(2,1)S(1)}, bf16[192,256]{1,0:T(8,128)(2,1)S(1)}, u32[]{:S(2)}, u32[]{:S(2)}) collective-permute-start(bf16[192,256]{1,0:T(8,128)(2,1)S(1)} %get-tuple-element.49.refs_0_), channel_id=1, source_target_pairs={{0,128},{64,192},{128,0},{192,64},{1,129},{65,193},{129,1},{193,65... | collective-permute-start | bytes 294920 | tf_op jit(solution)/shard_map/ppermute | solution.py:342
  160.6 3.4 %collective-permute-done.22.refs_3_ = bf16[192,256]{1,0:T(8,128)(2,1)S(1)} collective-permute-done((bf16[192,256]{1,0:T(8,128)(2,1)S(1)}, bf16[192,256]{1,0:T(8,128)(2,1)S(1)}, u32[]{:S(2)}, u32[]{:S(2)}) %collective-permute-start.22) | collective-permute-done | bytes 98336 | tf_op jit(solution)/shard_map/ppermute | solution.py:342
  164.0 0.9 collective-permute-done.20.refs_1_
  164.9 1.4 shard_map.163
  166.4 1.6 collective-permute-done.26.got_ref
  168.1 2.2 %collective-permute-start.27 = (bf16[48,1792]{1,0:T(8,128)(2,1)S(1)}, bf16[48,1792]{1,0:T(8,128)(2,1)S(1)}, u32[]{:S(2)}, u32[]{:S(2)}) collective-permute-start(bf16[48,1792]{1,0:T(8,128)(2,1)S(1)} %get-tuple-element.57), channel_id=1, source_target_pairs={{0,48},{16,0},{32,16},{48,32},{1,49},{17,1},{33,17},{49,33},{2,50}... | collective-permute-start | bytes 516104 | tf_op jit(solution)/shard_map/ppermute | solution.py:342
  170.4 1.0 collective-permute-start.28
  171.4 6.6 %collective-permute-done.27.refs_1_ = bf16[48,1792]{1,0:T(8,128)(2,1)S(1)} collective-permute-done((bf16[48,1792]{1,0:T(8,128)(2,1)S(1)}, bf16[48,1792]{1,0:T(8,128)(2,1)S(1)}, u32[]{:S(2)}, u32[]{:S(2)}) %collective-permute-start.27) | collective-permute-done | bytes 172064 | tf_op jit(solution)/shard_map/ppermute | solution.py:342
  178.0 1.1 collective-permute-done.28.refs_2_
  179.2 2.5 %collective-permute-done.29.refs_3_ = bf16[48,1792]{1,0:T(8,128)(2,1)S(1)} collective-permute-done((bf16[48,1792]{1,0:T(8,128)(2,1)S(1)}, bf16[48,1792]{1,0:T(8,128)(2,1)S(1)}, u32[]{:S(2)}, u32[]{:S(2)}) %collective-permute-start.29) | collective-permute-done | bytes 172064 | tf_op jit(solution)/shard_map/ppermute | solution.py:342
  181.9 14.0 %all_to_all.17.parts_ref = bf16[8,8,1792]{2,1,0:T(8,128)(2,1)S(1)} all-to-all(bf16[8,8,1792]{2,1,0:T(8,128)(2,1)S(1)} %shard_map.165), channel_id=1, replica_groups=mesh['context'=4,'x'=4,'z'=8,'core'=2] {'z'}, dimensions={0} | all-to-all | bytes 458752 | tf_op jit(solution)/shard_map/all_to_all | solution.py:481
  196.0 0.6 copy.17
  (44 shorter events, 2.7 us)
Async XLA Ops:
  3.8 55.2 %copy-start.3 = (bf16[8,1792]{1,0:T(8,128)(2,1)S(1)}, bf16[8,1792]{1,0:T(8,128)(2,1)}, u32[]{:S(2)}) copy-start(bf16[8,1792]{1,0:T(8,128)(2,1)} %residual_ref.1) | copy-start | bytes 86020
  3.8 55.2 %copy-start.5 = (s32[8,8]{1,0:T(8,128)S(1)}, s32[8,8]{1,0:T(8,128)}, u32[]{:S(2)}) copy-start(s32[8,8]{1,0:T(8,128)} %ids_ref.1) | copy-start | bytes 772
  3.8 55.2 %copy-start.6 = (f32[8,8]{1,0:T(8,128)S(1)}, f32[8,8]{1,0:T(8,128)}, u32[]{:S(2)}) copy-start(f32[8,8]{1,0:T(8,128)} %weights_ref.1) | copy-start | bytes 772
  3.8 6.8 %collective-permute-start = (bf16[144,512]{1,0:T(8,128)(2,1)S(1)}, bf16[144,512]{1,0:T(8,128)(2,1)S(1)}, u32[]{:S(2)}, u32[]{:S(2)}) collective-permute-start(bf16[144,512]{1,0:T(8,128)(2,1)S(1)} %get-tuple-element.33.refs_0_), channel_id=1, source_target_pairs={{0,64},{64,128},{128,192},{192,0},{1,65},{65,129},{129,193},{193,1... | collective-permute-start | bytes 442376 | tf_op jit(solution)/shard_map/ppermute | solution.py:342
  5.8 6.6 %collective-permute-start.4 = (bf16[144,512]{1,0:T(8,128)(2,1)S(1)}, bf16[144,512]{1,0:T(8,128)(2,1)S(1)}, u32[]{:S(2)}, u32[]{:S(2)}) collective-permute-start(bf16[144,512]{1,0:T(8,128)(2,1)S(1)} %get-tuple-element.34.refs_4_), channel_id=1, source_target_pairs={{0,192},{64,0},{128,64},{192,128},{1,193},{65,1},{129,65},{193,129... | collective-permute-start | bytes 442376 | tf_op jit(solution)/shard_map/ppermute | solution.py:342
  5.9 9.1 %collective-permute-start.2 = (bf16[144,512]{1,0:T(8,128)(2,1)S(1)}, bf16[144,512]{1,0:T(8,128)(2,1)S(1)}, u32[]{:S(2)}, u32[]{:S(2)}) collective-permute-start(bf16[144,512]{1,0:T(8,128)(2,1)S(1)} %get-tuple-element.33.refs_0_), channel_id=1, source_target_pairs={{0,192},{64,0},{128,64},{192,128},{1,193},{65,1},{129,65},{193,129... | collective-permute-start | bytes 442376 | tf_op jit(solution)/shard_map/ppermute | solution.py:342
  6.7 8.4 %collective-permute-start.3 = (bf16[144,512]{1,0:T(8,128)(2,1)S(1)}, bf16[144,512]{1,0:T(8,128)(2,1)S(1)}, u32[]{:S(2)}, u32[]{:S(2)}) collective-permute-start(bf16[144,512]{1,0:T(8,128)(2,1)S(1)} %get-tuple-element.34.refs_4_), channel_id=1, source_target_pairs={{0,64},{64,128},{128,192},{192,0},{1,65},{65,129},{129,193},{193,1... | collective-permute-start | bytes 442376 | tf_op jit(solution)/shard_map/ppermute | solution.py:342
  10.6 5.2 %collective-permute-start.1 = (bf16[144,512]{1,0:T(8,128)(2,1)S(1)}, bf16[144,512]{1,0:T(8,128)(2,1)S(1)}, u32[]{:S(2)}, u32[]{:S(2)}) collective-permute-start(bf16[144,512]{1,0:T(8,128)(2,1)S(1)} %collective-permute-done.refs_1_), channel_id=1, source_target_pairs={{0,64},{64,128},{128,192},{192,0},{1,65},{65,129},{129,193},{193,1... | collective-permute-start | bytes 442376 | tf_op jit(solution)/shard_map/ppermute | solution.py:342
  12.4 6.4 %collective-permute-start.5 = (bf16[144,512]{1,0:T(8,128)(2,1)S(1)}, bf16[144,512]{1,0:T(8,128)(2,1)S(1)}, u32[]{:S(2)}, u32[]{:S(2)}) collective-permute-start(bf16[144,512]{1,0:T(8,128)(2,1)S(1)} %collective-permute-done.4.refs_7_), channel_id=1, source_target_pairs={{0,192},{64,0},{128,64},{192,128},{1,193},{65,1},{129,65},{193,129... | collective-permute-start | bytes 442376 | tf_op jit(solution)/shard_map/ppermute | solution.py:342
  18.7 136.0 %copy-start.2 = (bf16[1,7168,256]{2,1,0:T(8,128)(2,1)S(1)}, bf16[1,7168,256]{2,1,0:T(8,128)(2,1)}, u32[]{:S(2)}) copy-start(bf16[1,7168,256]{2,1,0:T(8,128)(2,1)} %param.30) | copy-start | bytes 11010052
  21.9 65.4 %copy-start = (bf16[1,256,7168]{2,1,0:T(8,128)(2,1)S(1)}, bf16[1,256,7168]{2,1,0:T(8,128)(2,1)}, u32[]{:S(2)}) copy-start(bf16[1,256,7168]{2,1,0:T(8,128)(2,1)} %param.31) | copy-start | bytes 11010052
  21.9 2.6 %collective-permute-start.6 = (bf16[256,1792]{1,0:T(8,128)(2,1)S(1)}, bf16[256,1792]{1,0:T(8,128)(2,1)S(1)}, u32[]{:S(2)}, u32[]{:S(2)}) collective-permute-start(bf16[256,1792]{1,0:T(8,128)(2,1)S(1)} %get-tuple-element.36.after_ref), channel_id=1, source_target_pairs={{0,1},{1,0},{2,3},{3,2},{4,5},{5,4},{6,7},{7,6},{8,9},{9,8},{10,11... | collective-permute-start | bytes 2752520 | tf_op jit(solution)/shard_map/ppermute | solution.py:342
  25.2 9.1 %collective-permute-start.7 = (bf16[64,1792]{1,0:T(8,128)(2,1)S(1)}, bf16[64,1792]{1,0:T(8,128)(2,1)S(1)}, u32[]{:S(2)}, u32[]{:S(2)}) collective-permute-start(bf16[64,1792]{1,0:T(8,128)(2,1)S(1)} %get-tuple-element.38), channel_id=1, source_target_pairs={{0,16},{16,32},{32,48},{48,0},{1,17},{17,33},{33,49},{49,1},{2,18}... | collective-permute-start | bytes 688136 | tf_op jit(solution)/shard_map/ppermute | solution.py:342
  26.5 13.3 %collective-permute-start.8 = (bf16[64,1792]{1,0:T(8,128)(2,1)S(1)}, bf16[64,1792]{1,0:T(8,128)(2,1)S(1)}, u32[]{:S(2)}, u32[]{:S(2)}) collective-permute-start(bf16[64,1792]{1,0:T(8,128)(2,1)S(1)} %get-tuple-element.39), channel_id=1, source_target_pairs={{0,32},{16,48},{32,0},{48,16},{1,33},{17,49},{33,1},{49,17},{2,34}... | collective-permute-start | bytes 688136 | tf_op jit(solution)/shard_map/ppermute | solution.py:342
  29.2 10.5 %collective-permute-start.9 = (bf16[64,1792]{1,0:T(8,128)(2,1)S(1)}, bf16[64,1792]{1,0:T(8,128)(2,1)S(1)}, u32[]{:S(2)}, u32[]{:S(2)}) collective-permute-start(bf16[64,1792]{1,0:T(8,128)(2,1)S(1)} %get-tuple-element.40), channel_id=1, source_target_pairs={{0,48},{16,0},{32,16},{48,32},{1,49},{17,1},{33,17},{49,33},{2,50}... | collective-permute-start | bytes 688136 | tf_op jit(solution)/shard_map/ppermute | solution.py:342
  39.8 114.9 %copy-start.1 = (bf16[1,7168,256]{2,1,0:T(8,128)(2,1)S(1)}, bf16[1,7168,256]{2,1,0:T(8,128)(2,1)}, u32[]{:S(2)}) copy-start(bf16[1,7168,256]{2,1,0:T(8,128)(2,1)} %param.29) | copy-start | bytes 11010052
  39.8 114.9 %copy-start.4 = (f32[7168]{0:T(1024)S(1)}, f32[7168]{0:T(1024)}, u32[]{:S(2)}) copy-start(f32[7168]{0:T(1024)} %param.26) | copy-start | bytes 86020
  73.3 8.6 %collective-permute-start.10 = (bf16[48,1920]{1,0:T(8,128)(2,1)S(1)}, bf16[48,1920]{1,0:T(8,128)(2,1)S(1)}, u32[]{:S(2)}, u32[]{:S(2)}) collective-permute-start(bf16[48,1920]{1,0:T(8,128)(2,1)S(1)} %get-tuple-element.44), channel_id=1, source_target_pairs={{0,16},{16,32},{32,48},{48,0},{1,17},{17,33},{33,49},{49,1},{2,18}... | collective-permute-start | bytes 552968 | tf_op jit(solution)/shard_map/ppermute | solution.py:342
  74.9 8.9 %collective-permute-start.11 = (bf16[48,1920]{1,0:T(8,128)(2,1)S(1)}, bf16[48,1920]{1,0:T(8,128)(2,1)S(1)}, u32[]{:S(2)}, u32[]{:S(2)}) collective-permute-start(bf16[48,1920]{1,0:T(8,128)(2,1)S(1)} %get-tuple-element.45), channel_id=1, source_target_pairs={{0,32},{16,48},{32,0},{48,16},{1,33},{17,49},{33,1},{49,17},{2,34}... | collective-permute-start | bytes 552968 | tf_op jit(solution)/shard_map/ppermute | solution.py:342
  78.0 5.8 %collective-permute-start.12 = (bf16[48,1920]{1,0:T(8,128)(2,1)S(1)}, bf16[48,1920]{1,0:T(8,128)(2,1)S(1)}, u32[]{:S(2)}, u32[]{:S(2)}) collective-permute-start(bf16[48,1920]{1,0:T(8,128)(2,1)S(1)} %get-tuple-element.46), channel_id=1, source_target_pairs={{0,48},{16,0},{32,16},{48,32},{1,49},{17,1},{33,17},{49,33},{2,50}... | collective-permute-start | bytes 552968 | tf_op jit(solution)/shard_map/ppermute | solution.py:342
  83.9 5.2 %collective-permute-start.13 = (bf16[96,1920]{1,0:T(8,128)(2,1)S(1)}, bf16[96,1920]{1,0:T(8,128)(2,1)S(1)}, u32[]{:S(2)}, u32[]{:S(2)}) collective-permute-start(bf16[96,1920]{1,0:T(8,128)(2,1)S(1)} %get-tuple-element.48), channel_id=1, source_target_pairs={{0,1},{1,0},{2,3},{3,2},{4,5},{5,4},{6,7},{7,6},{8,9},{9,8},{10,11... | collective-permute-start | bytes 1105928 | tf_op jit(solution)/shard_map/ppermute | solution.py:342
  84.0 32.4 %collective-permute-start.19 = (bf16[96,1920]{1,0:T(8,128)(2,1)S(1)}, bf16[96,1920]{1,0:T(8,128)(2,1)S(1)}, u32[]{:S(2)}, u32[]{:S(2)}) collective-permute-start(bf16[96,1920]{1,0:T(8,128)(2,1)S(1)} %get-tuple-element.47.refs_0_), channel_id=1, source_target_pairs={{0,192},{64,0},{128,64},{192,128},{1,193},{65,1},{129,65},{193,129... | collective-permute-start | bytes 1105928 | tf_op jit(solution)/shard_map/ppermute | solution.py:342
  84.1 32.3 %collective-permute-start.14 = (bf16[96,1920]{1,0:T(8,128)(2,1)S(1)}, bf16[96,1920]{1,0:T(8,128)(2,1)S(1)}, u32[]{:S(2)}, u32[]{:S(2)}) collective-permute-start(bf16[96,1920]{1,0:T(8,128)(2,1)S(1)} %get-tuple-element.47.refs_0_), channel_id=1, source_target_pairs={{0,64},{64,128},{128,192},{192,0},{1,65},{65,129},{129,193},{193,1... | collective-permute-start | bytes 1105928 | tf_op jit(solution)/shard_map/ppermute | solution.py:342
  88.1 72.0 %collective-permute-start.23 = (bf16[256,1792]{1,0:T(8,128)(2,1)S(1)}, bf16[256,1792]{1,0:T(8,128)(2,1)S(1)}, u32[]{:S(2)}, u32[]{:S(2)}) collective-permute-start(bf16[256,1792]{1,0:T(8,128)(2,1)S(1)} %get-tuple-element.50), channel_id=1, source_target_pairs={{0,64},{64,128},{128,192},{192,0},{1,65},{65,129},{129,193},{193,1... | collective-permute-start | bytes 2752520 | tf_op jit(solution)/shard_map/ppermute | solution.py:342
  88.2 72.5 %collective-permute-start.24 = (bf16[256,1792]{1,0:T(8,128)(2,1)S(1)}, bf16[256,1792]{1,0:T(8,128)(2,1)S(1)}, u32[]{:S(2)}, u32[]{:S(2)}) collective-permute-start(bf16[256,1792]{1,0:T(8,128)(2,1)S(1)} %get-tuple-element.51), channel_id=1, source_target_pairs={{0,128},{64,192},{128,0},{192,64},{1,129},{65,193},{129,1},{193,65... | collective-permute-start | bytes 2752520 | tf_op jit(solution)/shard_map/ppermute | solution.py:342
  89.1 71.5 %collective-permute-start.25 = (bf16[256,1792]{1,0:T(8,128)(2,1)S(1)}, bf16[256,1792]{1,0:T(8,128)(2,1)S(1)}, u32[]{:S(2)}, u32[]{:S(2)}) collective-permute-start(bf16[256,1792]{1,0:T(8,128)(2,1)S(1)} %get-tuple-element.52), channel_id=1, source_target_pairs={{0,192},{64,0},{128,64},{192,128},{1,193},{65,1},{129,65},{193,129... | collective-permute-start | bytes 2752520 | tf_op jit(solution)/shard_map/ppermute | solution.py:342
  116.4 27.0 %collective-permute-start.17 = (bf16[96,1920]{1,0:T(8,128)(2,1)S(1)}, bf16[96,1920]{1,0:T(8,128)(2,1)S(1)}, u32[]{:S(2)}, u32[]{:S(2)}) collective-permute-start(bf16[96,1920]{1,0:T(8,128)(2,1)S(1)} %collective-permute-done.13.refs_1_), channel_id=1, source_target_pairs={{0,192},{64,0},{128,64},{192,128},{1,193},{65,1},{129,65},{193,129... | collective-permute-start | bytes 1105928 | tf_op jit(solution)/shard_map/ppermute | solution.py:342
  116.4 27.0 %collective-permute-start.15 = (bf16[96,1920]{1,0:T(8,128)(2,1)S(1)}, bf16[96,1920]{1,0:T(8,128)(2,1)S(1)}, u32[]{:S(2)}, u32[]{:S(2)}) collective-permute-start(bf16[96,1920]{1,0:T(8,128)(2,1)S(1)} %collective-permute-done.13.refs_1_), channel_id=1, source_target_pairs={{0,64},{64,128},{128,192},{192,0},{1,65},{65,129},{129,193},{193,1... | collective-permute-start | bytes 1105928 | tf_op jit(solution)/shard_map/ppermute | solution.py:342
  143.4 10.1 %collective-permute-start.16 = (bf16[96,1920]{1,0:T(8,128)(2,1)S(1)}, bf16[96,1920]{1,0:T(8,128)(2,1)S(1)}, u32[]{:S(2)}, u32[]{:S(2)}) collective-permute-start(bf16[96,1920]{1,0:T(8,128)(2,1)S(1)} %collective-permute-done.14.refs_2_), channel_id=1, source_target_pairs={{0,64},{64,128},{128,192},{192,0},{1,65},{65,129},{129,193},{193,1... | collective-permute-start | bytes 1105928 | tf_op jit(solution)/shard_map/ppermute | solution.py:342
  143.4 11.3 %collective-permute-start.18 = (bf16[96,1920]{1,0:T(8,128)(2,1)S(1)}, bf16[96,1920]{1,0:T(8,128)(2,1)S(1)}, u32[]{:S(2)}, u32[]{:S(2)}) collective-permute-start(bf16[96,1920]{1,0:T(8,128)(2,1)S(1)} %collective-permute-done.17.refs_7_), channel_id=1, source_target_pairs={{0,192},{64,0},{128,64},{192,128},{1,193},{65,1},{129,65},{193,129... | collective-permute-start | bytes 1105928 | tf_op jit(solution)/shard_map/ppermute | solution.py:342
  157.0 7.0 %collective-permute-start.22 = (bf16[192,256]{1,0:T(8,128)(2,1)S(1)}, bf16[192,256]{1,0:T(8,128)(2,1)S(1)}, u32[]{:S(2)}, u32[]{:S(2)}) collective-permute-start(bf16[192,256]{1,0:T(8,128)(2,1)S(1)} %get-tuple-element.49.refs_0_), channel_id=1, source_target_pairs={{0,192},{64,0},{128,64},{192,128},{1,193},{65,1},{129,65},{193,129... | collective-permute-start | bytes 294920 | tf_op jit(solution)/shard_map/ppermute | solution.py:342
  157.6 6.3 %collective-permute-start.21 = (bf16[192,256]{1,0:T(8,128)(2,1)S(1)}, bf16[192,256]{1,0:T(8,128)(2,1)S(1)}, u32[]{:S(2)}, u32[]{:S(2)}) collective-permute-start(bf16[192,256]{1,0:T(8,128)(2,1)S(1)} %get-tuple-element.49.refs_0_), channel_id=1, source_target_pairs={{0,128},{64,192},{128,0},{192,64},{1,129},{65,193},{129,1},{193,65... | collective-permute-start | bytes 294920 | tf_op jit(solution)/shard_map/ppermute | solution.py:342
  160.0 4.9 %collective-permute-start.20 = (bf16[192,256]{1,0:T(8,128)(2,1)S(1)}, bf16[192,256]{1,0:T(8,128)(2,1)S(1)}, u32[]{:S(2)}, u32[]{:S(2)}) collective-permute-start(bf16[192,256]{1,0:T(8,128)(2,1)S(1)} %get-tuple-element.49.refs_0_), channel_id=1, source_target_pairs={{0,64},{64,128},{128,192},{192,0},{1,65},{65,129},{129,193},{193,1... | collective-permute-start | bytes 294920 | tf_op jit(solution)/shard_map/ppermute | solution.py:342
  166.3 1.7 collective-permute-start.26
  168.1 9.9 %collective-permute-start.27 = (bf16[48,1792]{1,0:T(8,128)(2,1)S(1)}, bf16[48,1792]{1,0:T(8,128)(2,1)S(1)}, u32[]{:S(2)}, u32[]{:S(2)}) collective-permute-start(bf16[48,1792]{1,0:T(8,128)(2,1)S(1)} %get-tuple-element.57), channel_id=1, source_target_pairs={{0,48},{16,0},{32,16},{48,32},{1,49},{17,1},{33,17},{49,33},{2,50}... | collective-permute-start | bytes 516104 | tf_op jit(solution)/shard_map/ppermute | solution.py:342
  170.4 8.8 %collective-permute-start.28 = (bf16[48,1792]{1,0:T(8,128)(2,1)S(1)}, bf16[48,1792]{1,0:T(8,128)(2,1)S(1)}, u32[]{:S(2)}, u32[]{:S(2)}) collective-permute-start(bf16[48,1792]{1,0:T(8,128)(2,1)S(1)} %get-tuple-element.58), channel_id=1, source_target_pairs={{0,32},{16,48},{32,0},{48,16},{1,33},{17,49},{33,1},{49,17},{2,34}... | collective-permute-start | bytes 516104 | tf_op jit(solution)/shard_map/ppermute | solution.py:342
  171.4 10.3 %collective-permute-start.29 = (bf16[48,1792]{1,0:T(8,128)(2,1)S(1)}, bf16[48,1792]{1,0:T(8,128)(2,1)S(1)}, u32[]{:S(2)}, u32[]{:S(2)}) collective-permute-start(bf16[48,1792]{1,0:T(8,128)(2,1)S(1)} %get-tuple-element.59), channel_id=1, source_target_pairs={{0,16},{16,32},{32,48},{48,0},{1,17},{17,33},{33,49},{49,1},{2,18}... | collective-permute-start | bytes 516104 | tf_op jit(solution)/shard_map/ppermute | solution.py:342

commit v5 on v4

--- a/solution.py
+++ b/solution.py
@@ -50,8 +50,11 @@
 
 
 def attention_kernel(
-    place, q_ref, kl_ref, vl_ref, pool_ref, fresh_ref, table_ref, length_ref, parent_ref, *outs
+    place, q_ref, kl_ref, vl_ref, pool_ref, fresh_ref, table_ref, length_ref, parent_ref, *refs
 ):
+    out_weight, *outs, held_weight, done = refs
+    load = pltpu.make_async_copy(out_weight, held_weight, done)
+    load.start()
     context = place[0]
     pool_rows = pool_ref.shape[0]
     fresh_rows = fresh_ref.shape[0]
@@ -124,13 +127,12 @@
             jnp.where(line == 1, middle.astype(F32), jnp.where(line == 2, low.astype(F32), 0.0)),
         )
         out[VD:, :] = extra.astype(BF16)
+    load.wait()
 
 
 def merge_kernel(place, *refs):
     core = place[2]
-    parts, (weight_ref, send_ref, keep_ref, scratch, weight, done) = refs[:8], refs[8:]
-    load = pltpu.make_async_copy(weight_ref, weight, done)
-    load.start()
+    parts, (weight_ref, send_ref, keep_ref, scratch) = refs[:8], refs[8:]
     heads = []
     for head in range(2):
         own = parts[4 * head : 4 * head + 4]
@@ -145,11 +147,12 @@
         for part, share in zip(own, shares):
             mixed = mixed + part[:VD, :].astype(F32) * (share * inverse)
         heads.append(mixed)
-    attention = jnp.concatenate(heads, axis=0).T.astype(BF16)
-    load.wait()
-    scratch[...] = dot_nn(attention, weight[...]).reshape(scratch.shape)
-    send_ref[...] = scratch[:, 1 - core].reshape(send_ref.shape).astype(BF16)
-    keep_ref[...] = scratch[:, core].reshape(keep_ref.shape)
+    scratch[...] = jnp.concatenate(heads, axis=0).T.reshape(scratch.shape)
+    half = send_ref.shape[0]
+    sent = scratch[:, 1 - core].reshape(half, -1).astype(BF16)
+    send_ref[...] = dot_nn(sent, weight_ref[...]).astype(BF16)
+    kept = scratch[:, core].reshape(half, -1).astype(BF16)
+    keep_ref[...] = dot_nn(kept, weight_ref[...])
 
 
 def add_kernel(place, keep_ref, got_ref, own_ref, *sends):
@@ -256,8 +259,31 @@
         out[slots:, :] = got_ref[step * slots : (step + 1) * slots, :]
 
 
-def expert_kernel(place, *refs):
-    context, expert = place[0], place[1].astype(F32)
+def partial_sums(place, index, low_ref, high_ref, gain_ref, gate_ref, up_ref):
+    count, width = gain_ref.shape[0], gain_ref.shape[2]
+    source = lax.rem(place[0] + (count - index), count)
+    rows = jnp.concatenate([low_ref[:, :width], high_ref[:, :width]], axis=0)
+    scaled = (rows.astype(F32) * gain_ref[source]).astype(BF16)
+    at = pl.ds(pl.multiple_of(source * width, width), width)
+    return dot_nn(scaled, gate_ref[at, :]), dot_nn(scaled, up_ref[at, :])
+
+
+def own_kernel(place, low_ref, high_ref, gain_ref, gate_ref, up_ref, gate_sum, up_sum):
+    gate_sum[...], up_sum[...] = partial_sums(
+        place, 0, low_ref, high_ref, gain_ref, gate_ref, up_ref
+    )
+
+
+def near_kernel(place, gate_old, up_old, low1, high1, low3, high3, *refs):
+    gate_sum, up_sum = refs[3:]
+    gate1, up1 = partial_sums(place, 1, low1, high1, *refs[:3])
+    gate3, up3 = partial_sums(place, 3, low3, high3, *refs[:3])
+    gate_sum[...] = gate_old[...] + gate1 + gate3
+    up_sum[...] = up_old[...] + up1 + up3
+
+
+def expert_kernel(place, gate_old, up_old, *refs):
+    expert = place[1].astype(F32)
     parts = refs[:8]
     gain_ref, gate_ref, up_ref, active_ref, share_ref = refs[8:]
     slots = active_ref.shape[0]
@@ -282,17 +308,9 @@
             )
             share_ref[...] = jnp.broadcast_to(share, share_ref.shape)
     inverse = lax.rsqrt(squares * (1.0 / (count * width)) + NORM_EPSILON)
-    gate_part = jnp.zeros((slots, gate_ref.shape[1]), F32)
-    up_part = gate_part
-    for index in range(count):
-        source = lax.rem(context + (count - index), count)
-        rows = jnp.concatenate(
-            [parts[2 * index][:, :width], parts[2 * index + 1][:, :width]], axis=0
-        )
-        normed = (rows.astype(F32) * inverse * gain_ref[source]).astype(BF16)
-        at = pl.ds(pl.multiple_of(source * width, width), width)
-        gate_part = gate_part + dot_nn(normed, gate_ref[at, :])
-        up_part = up_part + dot_nn(normed, up_ref[at, :])
+    gate2, up2 = partial_sums(place, 2, parts[4], parts[5], gain_ref, gate_ref, up_ref)
+    gate_part = (gate_old[...] + gate2) * inverse
+    up_part = (up_old[...] + up2) * inverse
     active_ref[...] = (gate_part / (1.0 + jnp.exp(-gate_part)) * up_part).astype(BF16)
 
 
@@ -321,7 +339,7 @@
     out_ref[...] = (hidden_ref[...].astype(F32) + total).astype(BF16)
 
 
-def call(kernel, outs, inputs, scalars=0, scratch=(), limit=16, hold=True, raw=0):
+def call(kernel, outs, inputs, scalars=0, scratch=(), limit=16, hold=True, raw=0, out=pltpu.VMEM):
     last = len(inputs) - raw
     spaces = [pltpu.SMEM] * scalars
     spaces += [pltpu.VMEM if hold else pltpu.HBM] * (last - scalars)
@@ -330,7 +348,7 @@
     specs += [pl.BlockSpec(memory_space=pl.ANY)] * raw
     return pl.pallas_call(
         kernel,
-        out_shape=tuple(pltpu.VMEM(shape, dtype) for shape, dtype in outs),
+        out_shape=tuple(out(shape, dtype) for shape, dtype in outs),
         in_specs=specs,
         out_specs=tuple(VMEM for _ in outs),
         scratch_shapes=list(scratch),
@@ -380,9 +398,9 @@
     for index, value in enumerate(places):
         place = jnp.where(number == index, value, place)
 
-    low, high = call(
+    low, high, held_weight = call(
         attention_kernel,
-        [((VD + 16, rows), BF16)] * 2,
+        [((VD + 16, rows), BF16)] * 2 + [(out_weight.shape, BF16)],
         [
             place,
             queries,
@@ -393,10 +411,13 @@
             page_table.T,
             context_lengths.reshape(1, -1),
             tree_parents.T,
+            out_weight,
         ],
         scalars=1,
         hold=False,
         limit=24,
+        raw=1,
+        scratch=[pltpu.SemaphoreType.DMA(())],
     )
 
     def around(low, high):
@@ -409,14 +430,9 @@
     send, keep = call(
         merge_kernel,
         [((half, width), BF16), ((half, width), F32)],
-        [place, *lows, *highs, out_weight],
-        scalars=1,
-        scratch=[
-            pltpu.VMEM((wide * deep, 2, row_dev, width), F32),
-            pltpu.VMEM(out_weight.shape, BF16),
-            pltpu.SemaphoreType.DMA(()),
-        ],
-        raw=1,
+        [place, *lows, *highs, held_weight],
+        scalars=1,
+        scratch=[pltpu.VMEM((wide * deep, 2, row_dev, out_weight.shape[0]), F32)],
     )
     cuts = call(
         cut_kernel,
@@ -452,16 +468,19 @@
     parts = [shift(part, WIDE, wide, step) if step else part for step, part in enumerate(parts)]
     low, send = call(sort_kernel, [((slots // 2, full), BF16)] * 2, parts)
     lows, highs = around(low, shift(send, CORE, 2, 1))
+    weights = [norm_gain.reshape(ring, 1, width), gate_matrix[0], up_matrix[0]]
+    sums = [((slots, hidden_units), F32)] * 2
+    partial = call(own_kernel, sums, [place, lows[0], highs[0], *weights], scalars=1)
+    partial = call(
+        near_kernel,
+        sums,
+        [place, *partial, lows[1], highs[1], lows[3], highs[3], *weights],
+        scalars=1,
+    )
     active, share = call(
         expert_kernel,
         [((slots, hidden_units), BF16), ((slots, TAIL), F32)],
-        [
-            place,
-            *[part for pair in zip(lows, highs) for part in pair],
-            norm_gain.reshape(ring, 1, width),
-            gate_matrix[0],
-            up_matrix[0],
-        ],
+        [place, *partial, *[part for pair in zip(lows, highs) for part in pair], *weights],
         scalars=1,
     )
     actives = [active] + [shift(active, CONTEXT, ring, step) for step in range(1, ring)]
@@ -479,8 +498,8 @@
     parts = [shift(part, WIDE, wide, -step) if step else part for step, part in enumerate(parts)]
     (summed,) = call(spread_kernel, chunk, [pick, *parts])
     returned = lax.all_to_all(summed, DEEP, 0, 0, tiled=True)
-    (out,) = call(output_kernel, [((row_dev, width), BF16)], [returned, hidden])
-    return out
+    done = [((row_dev, width), BF16)]
+    return call(output_kernel, done, [returned, hidden], out=jax.ShapeDtypeStruct)[0]
 
 
 def solution(mesh):

time: 199 us -> 196 us (0.985)
  waiting for transfers between devices: 99.9 us -> 97.3 us
    ppermute x30, waiting for transfers between devices: 99.9 us -> 97.3 us  [shift(): lax.ppermute(value, axis, [(i, (i + step) % count) for i in range(count)])]
    pallas_call x13 -> x15, Pallas kernels: 14.2 us -> 14.5 us  [call(): pl.pallas_call(kernel, out_shape=tuple((out(shape, dtype) for shape, dtyp...]
where the time goes in v5:
time: 196 us; the launch traced here: 194 us
  waiting for transfers between devices  97.3 us (50%)
  blocking collectives  45.9 us (23%)
  starting transfers between devices  35.8 us (18%)
  Pallas kernels  14.5 us (7%)
    ppermute x30, waiting for transfers between devices, shift(): lax.ppermute(value, axis, [(i, (i + step) % count) for i in range(count)])  97.3 us
    ppermute x30, starting transfers between devices, shift(): lax.ppermute(value, axis, [(i, (i + step) % count) for i in range(count)])  35.8 us
    all_to_all x1, blocking collectives, local(): mixed = lax.all_to_all(summed, DEEP, 0, 0, tiled=True)  19.2 us
    pallas_call x15, Pallas kernels, call(): pl.pallas_call(kernel, out_shape=tuple((out(shape, dtype) for shape, dtyp...  14.5 us
    all_to_all x1, blocking collectives, local(): returned = lax.all_to_all(summed, DEEP, 0, 0, tiled=True)  14 us
    all_to_all x1, blocking collectives, local(): lax.all_to_all(payload, DEEP, 0, 0, tiled=True)  12.7 us
  transfers between devices with their start and end apart: 30, of which 19 were waited for; matrix products, arithmetic and copies ran while one was open for 0% of the time, Pallas kernels for 2%

profile of v5, /device:TPU:24, one launch (start us, length us, event | category | flops | bytes accessed | tf_op | source)
XLA Modules:
  0.0 193.8 jit_solution(2323688029189172405)
XLA Ops:
  0.0 3.8 %shard_map.154 = (bf16[144,512]{1,0:T(8,128)(2,1)S(1)}, bf16[144,512]{1,0:T(8,128)(2,1)S(1)}, bf16[256,1792]{1,0:T(8,128)(2,1)S(1)}) custom-call(s32[8]{0:T(128)S(1)} %compare_select_fusion.4.place, bf16[512,384]{1,0:T(8,128)(2,1)} %q_ref.1, bf16[2,128,512]{2,1,0:T(8,128)(2,1)} %kl_ref.1, bf16[2,512,128]{2,1,0:T(8,128)(2,1)} %vl_ref.1, ...), custom_call_target="tpu_custom_call" | custom-call | tf_op jit(solution)/shard_map/pallas_call | solution.py:349
  3.8 2.0 %collective-permute-start = (bf16[144,512]{1,0:T(8,128)(2,1)S(1)}, bf16[144,512]{1,0:T(8,128)(2,1)S(1)}, u32[]{:S(2)}, u32[]{:S(2)}) collective-permute-start(bf16[144,512]{1,0:T(8,128)(2,1)S(1)} %get-tuple-element.38.refs_0_), channel_id=1, source_target_pairs={{0,64},{64,128},{128,192},{192,0},{1,65},{65,129},{129,193},{193,1... | collective-permute-start | bytes 442376 | tf_op jit(solution)/shard_map/ppermute | solution.py:360
  5.9 0.7 collective-permute-start.2
  6.7 2.5 %collective-permute-start.3 = (bf16[144,512]{1,0:T(8,128)(2,1)S(1)}, bf16[144,512]{1,0:T(8,128)(2,1)S(1)}, u32[]{:S(2)}, u32[]{:S(2)}) collective-permute-start(bf16[144,512]{1,0:T(8,128)(2,1)S(1)} %get-tuple-element.39.refs_4_), channel_id=1, source_target_pairs={{0,64},{64,128},{128,192},{192,0},{1,65},{65,129},{129,193},{193,1... | collective-permute-start | bytes 442376 | tf_op jit(solution)/shard_map/ppermute | solution.py:360
  9.2 1.5 collective-permute-done.refs_1_
  10.6 1.8 collective-permute-start.1
  12.7 2.4 %collective-permute-done.2.refs_3_ = bf16[144,512]{1,0:T(8,128)(2,1)S(1)} collective-permute-done((bf16[144,512]{1,0:T(8,128)(2,1)S(1)}, bf16[144,512]{1,0:T(8,128)(2,1)S(1)}, u32[]{:S(2)}, u32[]{:S(2)}) %collective-permute-start.2) | collective-permute-done | bytes 147488 | tf_op jit(solution)/shard_map/ppermute | solution.py:360
  15.1 0.7 collective-permute-done.1.refs_2_
  15.8 2.9 %collective-permute-done.5.refs_6_ = bf16[144,512]{1,0:T(8,128)(2,1)S(1)} collective-permute-done((bf16[144,512]{1,0:T(8,128)(2,1)S(1)}, bf16[144,512]{1,0:T(8,128)(2,1)S(1)}, u32[]{:S(2)}, u32[]{:S(2)}) %collective-permute-start.5) | collective-permute-done | bytes 147488 | tf_op jit(solution)/shard_map/ppermute | solution.py:360
  18.8 1.5 shard_map.155
  20.4 2.5 %collective-permute-done.6.got_ref = bf16[256,1792]{1,0:T(8,128)(2,1)S(1)} collective-permute-done((bf16[256,1792]{1,0:T(8,128)(2,1)S(1)}, bf16[256,1792]{1,0:T(8,128)(2,1)S(1)}, u32[]{:S(2)}, u32[]{:S(2)}) %collective-permute-start.6) | collective-permute-done | bytes 917536 | tf_op jit(solution)/shard_map/ppermute | solution.py:360
  22.8 0.7 shard_map.156
  23.5 1.2 collective-permute-start.7
  24.8 2.7 %collective-permute-start.8 = (bf16[64,1792]{1,0:T(8,128)(2,1)S(1)}, bf16[64,1792]{1,0:T(8,128)(2,1)S(1)}, u32[]{:S(2)}, u32[]{:S(2)}) collective-permute-start(bf16[64,1792]{1,0:T(8,128)(2,1)S(1)} %get-tuple-element.45), channel_id=1, source_target_pairs={{0,32},{16,48},{32,0},{48,16},{1,33},{17,49},{33,1},{49,17},{2,34}... | collective-permute-start | bytes 688136 | tf_op jit(solution)/shard_map/ppermute | solution.py:360
  27.5 1.4 collective-permute-start.9
  28.9 3.7 %collective-permute-done.7.refs_0_ = bf16[64,1792]{1,0:T(8,128)(2,1)S(1)} collective-permute-done((bf16[64,1792]{1,0:T(8,128)(2,1)S(1)}, bf16[64,1792]{1,0:T(8,128)(2,1)S(1)}, u32[]{:S(2)}, u32[]{:S(2)}) %collective-permute-start.7) | collective-permute-done | bytes 229408 | tf_op jit(solution)/shard_map/ppermute | solution.py:360
  32.7 5.4 %collective-permute-done.8.refs_1_ = bf16[64,1792]{1,0:T(8,128)(2,1)S(1)} collective-permute-done((bf16[64,1792]{1,0:T(8,128)(2,1)S(1)}, bf16[64,1792]{1,0:T(8,128)(2,1)S(1)}, u32[]{:S(2)}, u32[]{:S(2)}) %collective-permute-start.8) | collective-permute-done | bytes 229408 | tf_op jit(solution)/shard_map/ppermute | solution.py:360
  38.2 19.2 %all_to_all.15.parts_ref = bf16[8,8,1792]{2,1,0:T(8,128)(2,1)S(1)} all-to-all(bf16[8,8,1792]{2,1,0:T(8,128)(2,1)S(1)} %shard_map.157), channel_id=1, replica_groups=mesh['context'=4,'x'=4,'z'=8,'core'=2] {'z'}, dimensions={0} | all-to-all | bytes 458752 | tf_op jit(solution)/shard_map/all_to_all | solution.py:454
  57.5 12.7 %all_to_all.16 = bf16[8,8,1920]{2,1,0:T(8,128)(2,1)S(1)} all-to-all(bf16[8,8,1920]{2,1,0:T(8,128)(2,1)S(1)} %get-tuple-element.47), channel_id=1, replica_groups=mesh['context'=4,'x'=4,'z'=8,'core'=2] {'z'}, dimensions={0} | all-to-all | bytes 491520 | tf_op jit(solution)/shard_map/all_to_all | solution.py:460
  70.2 1.4 shard_map.159
  71.6 1.5 collective-permute-start.10
  73.1 3.1 %collective-permute-start.11 = (bf16[48,1920]{1,0:T(8,128)(2,1)S(1)}, bf16[48,1920]{1,0:T(8,128)(2,1)S(1)}, u32[]{:S(2)}, u32[]{:S(2)}) collective-permute-start(bf16[48,1920]{1,0:T(8,128)(2,1)S(1)} %get-tuple-element.51), channel_id=1, source_target_pairs={{0,32},{16,48},{32,0},{48,16},{1,33},{17,49},{33,1},{49,17},{2,34}... | collective-permute-start | bytes 552968 | tf_op jit(solution)/shard_map/ppermute | solution.py:360
  76.8 3.2 %collective-permute-done.10.refs_1_ = bf16[48,1920]{1,0:T(8,128)(2,1)S(1)} collective-permute-done((bf16[48,1920]{1,0:T(8,128)(2,1)S(1)}, bf16[48,1920]{1,0:T(8,128)(2,1)S(1)}, u32[]{:S(2)}, u32[]{:S(2)}) %collective-permute-start.10) | collective-permute-done | bytes 184352 | tf_op jit(solution)/shard_map/ppermute | solution.py:360
  80.0 2.0 %collective-permute-done.11.refs_2_ = bf16[48,1920]{1,0:T(8,128)(2,1)S(1)} collective-permute-done((bf16[48,1920]{1,0:T(8,128)(2,1)S(1)}, bf16[48,1920]{1,0:T(8,128)(2,1)S(1)}, u32[]{:S(2)}, u32[]{:S(2)}) %collective-permute-start.11) | collective-permute-done | bytes 184352 | tf_op jit(solution)/shard_map/ppermute | solution.py:360
  82.3 3.2 %collective-permute-start.14 = (bf16[96,1920]{1,0:T(8,128)(2,1)S(1)}, bf16[96,1920]{1,0:T(8,128)(2,1)S(1)}, u32[]{:S(2)}, u32[]{:S(2)}) collective-permute-start(bf16[96,1920]{1,0:T(8,128)(2,1)S(1)} %get-tuple-element.53.low_ref.refs_0_), channel_id=1, source_target_pairs={{0,64},{64,128},{128,192},{192,0},{1,65},{65,129},{129,193},{193,1... | collective-permute-start | bytes 1105928 | tf_op jit(solution)/shard_map/ppermute | solution.py:360
  85.5 0.7 shard_map.164
  86.3 0.9 collective-permute-start.24
  87.2 1.1 collective-permute-start.25
  88.3 26.2 %collective-permute-done.16.low3.refs_6_ = bf16[96,1920]{1,0:T(8,128)(2,1)S(1)} collective-permute-done((bf16[96,1920]{1,0:T(8,128)(2,1)S(1)}, bf16[96,1920]{1,0:T(8,128)(2,1)S(1)}, u32[]{:S(2)}, u32[]{:S(2)}) %collective-permute-start.16) | collective-permute-done | bytes 368672 | tf_op jit(solution)/shard_map/ppermute | solution.py:360
  114.6 3.2 %collective-permute-start.15 = (bf16[96,1920]{1,0:T(8,128)(2,1)S(1)}, bf16[96,1920]{1,0:T(8,128)(2,1)S(1)}, u32[]{:S(2)}, u32[]{:S(2)}) collective-permute-start(bf16[96,1920]{1,0:T(8,128)(2,1)S(1)} %collective-permute-done.13.high_ref.refs_1_), channel_id=1, source_target_pairs={{0,64},{64,128},{128,192},{192,0},{1,65},{65,129},{129,193},{193,1... | collective-permute-start | bytes 1105928 | tf_op jit(solution)/shard_map/ppermute | solution.py:360
  117.8 23.8 %collective-permute-done.17.high3.refs_7_ = bf16[96,1920]{1,0:T(8,128)(2,1)S(1)} collective-permute-done((bf16[96,1920]{1,0:T(8,128)(2,1)S(1)}, bf16[96,1920]{1,0:T(8,128)(2,1)S(1)}, u32[]{:S(2)}, u32[]{:S(2)}) %collective-permute-start.17) | collective-permute-done | bytes 368672 | tf_op jit(solution)/shard_map/ppermute | solution.py:360
  141.6 2.0 %collective-permute-start.19 = (bf16[96,1920]{1,0:T(8,128)(2,1)S(1)}, bf16[96,1920]{1,0:T(8,128)(2,1)S(1)}, u32[]{:S(2)}, u32[]{:S(2)}) collective-permute-start(bf16[96,1920]{1,0:T(8,128)(2,1)S(1)} %collective-permute-done.17.high3.refs_7_), channel_id=1, source_target_pairs={{0,192},{64,0},{128,64},{192,128},{1,193},{65,1},{129,65},{193,129... | collective-permute-start | bytes 1105928 | tf_op jit(solution)/shard_map/ppermute | solution.py:360
  143.6 1.1 shard_map.161
  144.7 1.5 shard_map.162
  146.2 5.5 %collective-permute-done.18.refs_4_ = bf16[96,1920]{1,0:T(8,128)(2,1)S(1)} collective-permute-done((bf16[96,1920]{1,0:T(8,128)(2,1)S(1)}, bf16[96,1920]{1,0:T(8,128)(2,1)S(1)}, u32[]{:S(2)}, u32[]{:S(2)}) %collective-permute-start.18) | collective-permute-done | bytes 368672 | tf_op jit(solution)/shard_map/ppermute | solution.py:360
  151.6 1.2 collective-permute-done.19.refs_5_
  152.9 1.1 shard_map.163
  154.6 2.4 %collective-permute-start.21 = (bf16[192,256]{1,0:T(8,128)(2,1)S(1)}, bf16[192,256]{1,0:T(8,128)(2,1)S(1)}, u32[]{:S(2)}, u32[]{:S(2)}) collective-permute-start(bf16[192,256]{1,0:T(8,128)(2,1)S(1)} %get-tuple-element.59.refs_0_), channel_id=1, source_target_pairs={{0,128},{64,192},{128,0},{192,64},{1,129},{65,193},{129,1},{193,65... | collective-permute-start | bytes 294920 | tf_op jit(solution)/shard_map/ppermute | solution.py:360
  157.6 3.4 %collective-permute-done.22.refs_3_ = bf16[192,256]{1,0:T(8,128)(2,1)S(1)} collective-permute-done((bf16[192,256]{1,0:T(8,128)(2,1)S(1)}, bf16[192,256]{1,0:T(8,128)(2,1)S(1)}, u32[]{:S(2)}, u32[]{:S(2)}) %collective-permute-start.22) | collective-permute-done | bytes 98336 | tf_op jit(solution)/shard_map/ppermute | solution.py:360
  161.0 0.9 collective-permute-done.20.refs_1_
  161.9 1.4 shard_map.165
  163.4 1.6 collective-permute-done.26.got_ref
  165.1 2.4 %collective-permute-start.27 = (bf16[48,1792]{1,0:T(8,128)(2,1)S(1)}, bf16[48,1792]{1,0:T(8,128)(2,1)S(1)}, u32[]{:S(2)}, u32[]{:S(2)}) collective-permute-start(bf16[48,1792]{1,0:T(8,128)(2,1)S(1)} %get-tuple-element.67), channel_id=1, source_target_pairs={{0,48},{16,0},{32,16},{48,32},{1,49},{17,1},{33,17},{49,33},{2,50}... | collective-permute-start | bytes 516104 | tf_op jit(solution)/shard_map/ppermute | solution.py:360
  167.5 0.8 collective-permute-start.28
  168.5 6.7 %collective-permute-done.27.refs_1_ = bf16[48,1792]{1,0:T(8,128)(2,1)S(1)} collective-permute-done((bf16[48,1792]{1,0:T(8,128)(2,1)S(1)}, bf16[48,1792]{1,0:T(8,128)(2,1)S(1)}, u32[]{:S(2)}, u32[]{:S(2)}) %collective-permute-start.27) | collective-permute-done | bytes 172064 | tf_op jit(solution)/shard_map/ppermute | solution.py:360
  175.2 1.1 collective-permute-done.28.refs_2_
  176.3 2.5 %collective-permute-done.29.refs_3_ = bf16[48,1792]{1,0:T(8,128)(2,1)S(1)} collective-permute-done((bf16[48,1792]{1,0:T(8,128)(2,1)S(1)}, bf16[48,1792]{1,0:T(8,128)(2,1)S(1)}, u32[]{:S(2)}, u32[]{:S(2)}) %collective-permute-start.29) | collective-permute-done | bytes 172064 | tf_op jit(solution)/shard_map/ppermute | solution.py:360
  179.1 14.0 %all_to_all.17.parts_ref = bf16[8,8,1792]{2,1,0:T(8,128)(2,1)S(1)} all-to-all(bf16[8,8,1792]{2,1,0:T(8,128)(2,1)S(1)} %shard_map.167), channel_id=1, replica_groups=mesh['context'=4,'x'=4,'z'=8,'core'=2] {'z'}, dimensions={0} | all-to-all | bytes 458752 | tf_op jit(solution)/shard_map/all_to_all | solution.py:500
  (45 shorter events, 4.0 us)
Async XLA Ops:
  3.8 53.5 %copy-start.4 = (bf16[8,1792]{1,0:T(8,128)(2,1)S(1)}, bf16[8,1792]{1,0:T(8,128)(2,1)}, u32[]{:S(2)}) copy-start(bf16[8,1792]{1,0:T(8,128)(2,1)} %residual_ref.1) | copy-start | bytes 86020
  3.8 53.5 %copy-start.5 = (s32[8,8]{1,0:T(8,128)S(1)}, s32[8,8]{1,0:T(8,128)}, u32[]{:S(2)}) copy-start(s32[8,8]{1,0:T(8,128)} %ids_ref.1) | copy-start | bytes 772
  3.8 53.5 %copy-start.6 = (f32[8,8]{1,0:T(8,128)S(1)}, f32[8,8]{1,0:T(8,128)}, u32[]{:S(2)}) copy-start(f32[8,8]{1,0:T(8,128)} %weights_ref.1) | copy-start | bytes 772
  3.8 6.8 %collective-permute-start = (bf16[144,512]{1,0:T(8,128)(2,1)S(1)}, bf16[144,512]{1,0:T(8,128)(2,1)S(1)}, u32[]{:S(2)}, u32[]{:S(2)}) collective-permute-start(bf16[144,512]{1,0:T(8,128)(2,1)S(1)} %get-tuple-element.38.refs_0_), channel_id=1, source_target_pairs={{0,64},{64,128},{128,192},{192,0},{1,65},{65,129},{129,193},{193,1... | collective-permute-start | bytes 442376 | tf_op jit(solution)/shard_map/ppermute | solution.py:360
  5.8 6.6 %collective-permute-start.4 = (bf16[144,512]{1,0:T(8,128)(2,1)S(1)}, bf16[144,512]{1,0:T(8,128)(2,1)S(1)}, u32[]{:S(2)}, u32[]{:S(2)}) collective-permute-start(bf16[144,512]{1,0:T(8,128)(2,1)S(1)} %get-tuple-element.39.refs_4_), channel_id=1, source_target_pairs={{0,192},{64,0},{128,64},{192,128},{1,193},{65,1},{129,65},{193,129... | collective-permute-start | bytes 442376 | tf_op jit(solution)/shard_map/ppermute | solution.py:360
  5.9 9.1 %collective-permute-start.2 = (bf16[144,512]{1,0:T(8,128)(2,1)S(1)}, bf16[144,512]{1,0:T(8,128)(2,1)S(1)}, u32[]{:S(2)}, u32[]{:S(2)}) collective-permute-start(bf16[144,512]{1,0:T(8,128)(2,1)S(1)} %get-tuple-element.38.refs_0_), channel_id=1, source_target_pairs={{0,192},{64,0},{128,64},{192,128},{1,193},{65,1},{129,65},{193,129... | collective-permute-start | bytes 442376 | tf_op jit(solution)/shard_map/ppermute | solution.py:360
  6.7 8.4 %collective-permute-start.3 = (bf16[144,512]{1,0:T(8,128)(2,1)S(1)}, bf16[144,512]{1,0:T(8,128)(2,1)S(1)}, u32[]{:S(2)}, u32[]{:S(2)}) collective-permute-start(bf16[144,512]{1,0:T(8,128)(2,1)S(1)} %get-tuple-element.39.refs_4_), channel_id=1, source_target_pairs={{0,64},{64,128},{128,192},{192,0},{1,65},{65,129},{129,193},{193,1... | collective-permute-start | bytes 442376 | tf_op jit(solution)/shard_map/ppermute | solution.py:360
  10.6 5.2 %collective-permute-start.1 = (bf16[144,512]{1,0:T(8,128)(2,1)S(1)}, bf16[144,512]{1,0:T(8,128)(2,1)S(1)}, u32[]{:S(2)}, u32[]{:S(2)}) collective-permute-start(bf16[144,512]{1,0:T(8,128)(2,1)S(1)} %collective-permute-done.refs_1_), channel_id=1, source_target_pairs={{0,64},{64,128},{128,192},{192,0},{1,65},{65,129},{129,193},{193,1... | collective-permute-start | bytes 442376 | tf_op jit(solution)/shard_map/ppermute | solution.py:360
  12.4 6.4 %collective-permute-start.5 = (bf16[144,512]{1,0:T(8,128)(2,1)S(1)}, bf16[144,512]{1,0:T(8,128)(2,1)S(1)}, u32[]{:S(2)}, u32[]{:S(2)}) collective-permute-start(bf16[144,512]{1,0:T(8,128)(2,1)S(1)} %collective-permute-done.4.refs_7_), channel_id=1, source_target_pairs={{0,192},{64,0},{128,64},{192,128},{1,193},{65,1},{129,65},{193,129... | collective-permute-start | bytes 442376 | tf_op jit(solution)/shard_map/ppermute | solution.py:360
  18.8 66.7 %copy-start.2 = (bf16[1,256,7168]{2,1,0:T(8,128)(2,1)S(1)}, bf16[1,256,7168]{2,1,0:T(8,128)(2,1)}, u32[]{:S(2)}) copy-start(bf16[1,256,7168]{2,1,0:T(8,128)(2,1)} %param.31) | copy-start | bytes 11010052
  20.3 2.6 %collective-permute-start.6 = (bf16[256,1792]{1,0:T(8,128)(2,1)S(1)}, bf16[256,1792]{1,0:T(8,128)(2,1)S(1)}, u32[]{:S(2)}, u32[]{:S(2)}) collective-permute-start(bf16[256,1792]{1,0:T(8,128)(2,1)S(1)} %get-tuple-element.42.after_ref), channel_id=1, source_target_pairs={{0,1},{1,0},{2,3},{3,2},{4,5},{5,4},{6,7},{7,6},{8,9},{9,8},{10,11... | collective-permute-start | bytes 2752520 | tf_op jit(solution)/shard_map/ppermute | solution.py:360
  23.5 9.1 %collective-permute-start.7 = (bf16[64,1792]{1,0:T(8,128)(2,1)S(1)}, bf16[64,1792]{1,0:T(8,128)(2,1)S(1)}, u32[]{:S(2)}, u32[]{:S(2)}) collective-permute-start(bf16[64,1792]{1,0:T(8,128)(2,1)S(1)} %get-tuple-element.44), channel_id=1, source_target_pairs={{0,16},{16,32},{32,48},{48,0},{1,17},{17,33},{33,49},{49,1},{2,18}... | collective-permute-start | bytes 688136 | tf_op jit(solution)/shard_map/ppermute | solution.py:360
  24.8 13.3 %collective-permute-start.8 = (bf16[64,1792]{1,0:T(8,128)(2,1)S(1)}, bf16[64,1792]{1,0:T(8,128)(2,1)S(1)}, u32[]{:S(2)}, u32[]{:S(2)}) collective-permute-start(bf16[64,1792]{1,0:T(8,128)(2,1)S(1)} %get-tuple-element.45), channel_id=1, source_target_pairs={{0,32},{16,48},{32,0},{48,16},{1,33},{17,49},{33,1},{49,17},{2,34}... | collective-permute-start | bytes 688136 | tf_op jit(solution)/shard_map/ppermute | solution.py:360
  27.5 10.5 %collective-permute-start.9 = (bf16[64,1792]{1,0:T(8,128)(2,1)S(1)}, bf16[64,1792]{1,0:T(8,128)(2,1)S(1)}, u32[]{:S(2)}, u32[]{:S(2)}) collective-permute-start(bf16[64,1792]{1,0:T(8,128)(2,1)S(1)} %get-tuple-element.46), channel_id=1, source_target_pairs={{0,48},{16,0},{32,16},{48,32},{1,49},{17,1},{33,17},{49,33},{2,50}... | collective-permute-start | bytes 688136 | tf_op jit(solution)/shard_map/ppermute | solution.py:360
  38.0 105.6 %copy-start.1 = (bf16[1,7168,256]{2,1,0:T(8,128)(2,1)S(1)}, bf16[1,7168,256]{2,1,0:T(8,128)(2,1)}, u32[]{:S(2)}) copy-start(bf16[1,7168,256]{2,1,0:T(8,128)(2,1)} %param.30) | copy-start | bytes 11010052
  38.2 105.5 %copy-start = (bf16[1,7168,256]{2,1,0:T(8,128)(2,1)S(1)}, bf16[1,7168,256]{2,1,0:T(8,128)(2,1)}, u32[]{:S(2)}) copy-start(bf16[1,7168,256]{2,1,0:T(8,128)(2,1)} %param.29) | copy-start | bytes 11010052
  38.2 105.4 %copy-start.3 = (f32[7168]{0:T(1024)S(1)}, f32[7168]{0:T(1024)}, u32[]{:S(2)}) copy-start(f32[7168]{0:T(1024)} %param.26) | copy-start | bytes 86020
  71.6 8.4 %collective-permute-start.10 = (bf16[48,1920]{1,0:T(8,128)(2,1)S(1)}, bf16[48,1920]{1,0:T(8,128)(2,1)S(1)}, u32[]{:S(2)}, u32[]{:S(2)}) collective-permute-start(bf16[48,1920]{1,0:T(8,128)(2,1)S(1)} %get-tuple-element.50), channel_id=1, source_target_pairs={{0,16},{16,32},{32,48},{48,0},{1,17},{17,33},{33,49},{49,1},{2,18}... | collective-permute-start | bytes 552968 | tf_op jit(solution)/shard_map/ppermute | solution.py:360
  73.1 8.9 %collective-permute-start.11 = (bf16[48,1920]{1,0:T(8,128)(2,1)S(1)}, bf16[48,1920]{1,0:T(8,128)(2,1)S(1)}, u32[]{:S(2)}, u32[]{:S(2)}) collective-permute-start(bf16[48,1920]{1,0:T(8,128)(2,1)S(1)} %get-tuple-element.51), channel_id=1, source_target_pairs={{0,32},{16,48},{32,0},{48,16},{1,33},{17,49},{33,1},{49,17},{2,34}... | collective-permute-start | bytes 552968 | tf_op jit(solution)/shard_map/ppermute | solution.py:360
  76.2 5.8 %collective-permute-start.12 = (bf16[48,1920]{1,0:T(8,128)(2,1)S(1)}, bf16[48,1920]{1,0:T(8,128)(2,1)S(1)}, u32[]{:S(2)}, u32[]{:S(2)}) collective-permute-start(bf16[48,1920]{1,0:T(8,128)(2,1)S(1)} %get-tuple-element.52), channel_id=1, source_target_pairs={{0,48},{16,0},{32,16},{48,32},{1,49},{17,1},{33,17},{49,33},{2,50}... | collective-permute-start | bytes 552968 | tf_op jit(solution)/shard_map/ppermute | solution.py:360
  82.1 5.2 %collective-permute-start.13 = (bf16[96,1920]{1,0:T(8,128)(2,1)S(1)}, bf16[96,1920]{1,0:T(8,128)(2,1)S(1)}, u32[]{:S(2)}, u32[]{:S(2)}) collective-permute-start(bf16[96,1920]{1,0:T(8,128)(2,1)S(1)} %get-tuple-element.54), channel_id=1, source_target_pairs={{0,1},{1,0},{2,3},{3,2},{4,5},{5,4},{6,7},{7,6},{8,9},{9,8},{10,11... | collective-permute-start | bytes 1105928 | tf_op jit(solution)/shard_map/ppermute | solution.py:360
  82.2 32.4 %collective-permute-start.16 = (bf16[96,1920]{1,0:T(8,128)(2,1)S(1)}, bf16[96,1920]{1,0:T(8,128)(2,1)S(1)}, u32[]{:S(2)}, u32[]{:S(2)}) collective-permute-start(bf16[96,1920]{1,0:T(8,128)(2,1)S(1)} %get-tuple-element.53.low_ref.refs_0_), channel_id=1, source_target_pairs={{0,192},{64,0},{128,64},{192,128},{1,193},{65,1},{129,65},{193,129... | collective-permute-start | bytes 1105928 | tf_op jit(solution)/shard_map/ppermute | solution.py:360
  82.3 32.3 %collective-permute-start.14 = (bf16[96,1920]{1,0:T(8,128)(2,1)S(1)}, bf16[96,1920]{1,0:T(8,128)(2,1)S(1)}, u32[]{:S(2)}, u32[]{:S(2)}) collective-permute-start(bf16[96,1920]{1,0:T(8,128)(2,1)S(1)} %get-tuple-element.53.low_ref.refs_0_), channel_id=1, source_target_pairs={{0,64},{64,128},{128,192},{192,0},{1,65},{65,129},{129,193},{193,1... | collective-permute-start | bytes 1105928 | tf_op jit(solution)/shard_map/ppermute | solution.py:360
  86.2 70.8 %collective-permute-start.23 = (bf16[256,1792]{1,0:T(8,128)(2,1)S(1)}, bf16[256,1792]{1,0:T(8,128)(2,1)S(1)}, u32[]{:S(2)}, u32[]{:S(2)}) collective-permute-start(bf16[256,1792]{1,0:T(8,128)(2,1)S(1)} %get-tuple-element.60), channel_id=1, source_target_pairs={{0,64},{64,128},{128,192},{192,0},{1,65},{65,129},{129,193},{193,1... | collective-permute-start | bytes 2752520 | tf_op jit(solution)/shard_map/ppermute | solution.py:360
  86.3 71.3 %collective-permute-start.24 = (bf16[256,1792]{1,0:T(8,128)(2,1)S(1)}, bf16[256,1792]{1,0:T(8,128)(2,1)S(1)}, u32[]{:S(2)}, u32[]{:S(2)}) collective-permute-start(bf16[256,1792]{1,0:T(8,128)(2,1)S(1)} %get-tuple-element.61), channel_id=1, source_target_pairs={{0,128},{64,192},{128,0},{192,64},{1,129},{65,193},{129,1},{193,65... | collective-permute-start | bytes 2752520 | tf_op jit(solution)/shard_map/ppermute | solution.py:360
  87.2 70.3 %collective-permute-start.25 = (bf16[256,1792]{1,0:T(8,128)(2,1)S(1)}, bf16[256,1792]{1,0:T(8,128)(2,1)S(1)}, u32[]{:S(2)}, u32[]{:S(2)}) collective-permute-start(bf16[256,1792]{1,0:T(8,128)(2,1)S(1)} %get-tuple-element.62), channel_id=1, source_target_pairs={{0,192},{64,0},{128,64},{192,128},{1,193},{65,1},{129,65},{193,129... | collective-permute-start | bytes 2752520 | tf_op jit(solution)/shard_map/ppermute | solution.py:360
  114.6 27.0 %collective-permute-start.17 = (bf16[96,1920]{1,0:T(8,128)(2,1)S(1)}, bf16[96,1920]{1,0:T(8,128)(2,1)S(1)}, u32[]{:S(2)}, u32[]{:S(2)}) collective-permute-start(bf16[96,1920]{1,0:T(8,128)(2,1)S(1)} %collective-permute-done.13.high_ref.refs_1_), channel_id=1, source_target_pairs={{0,192},{64,0},{128,64},{192,128},{1,193},{65,1},{129,65},{193,129... | collective-permute-start | bytes 1105928 | tf_op jit(solution)/shard_map/ppermute | solution.py:360
  114.6 27.0 %collective-permute-start.15 = (bf16[96,1920]{1,0:T(8,128)(2,1)S(1)}, bf16[96,1920]{1,0:T(8,128)(2,1)S(1)}, u32[]{:S(2)}, u32[]{:S(2)}) collective-permute-start(bf16[96,1920]{1,0:T(8,128)(2,1)S(1)} %collective-permute-done.13.high_ref.refs_1_), channel_id=1, source_target_pairs={{0,64},{64,128},{128,192},{192,0},{1,65},{65,129},{129,193},{193,1... | collective-permute-start | bytes 1105928 | tf_op jit(solution)/shard_map/ppermute | solution.py:360
  141.6 10.1 %collective-permute-start.18 = (bf16[96,1920]{1,0:T(8,128)(2,1)S(1)}, bf16[96,1920]{1,0:T(8,128)(2,1)S(1)}, u32[]{:S(2)}, u32[]{:S(2)}) collective-permute-start(bf16[96,1920]{1,0:T(8,128)(2,1)S(1)} %collective-permute-done.14.low1.refs_2_), channel_id=1, source_target_pairs={{0,64},{64,128},{128,192},{192,0},{1,65},{65,129},{129,193},{193,1... | collective-permute-start | bytes 1105928 | tf_op jit(solution)/shard_map/ppermute | solution.py:360
  141.6 11.3 %collective-permute-start.19 = (bf16[96,1920]{1,0:T(8,128)(2,1)S(1)}, bf16[96,1920]{1,0:T(8,128)(2,1)S(1)}, u32[]{:S(2)}, u32[]{:S(2)}) collective-permute-start(bf16[96,1920]{1,0:T(8,128)(2,1)S(1)} %collective-permute-done.17.high3.refs_7_), channel_id=1, source_target_pairs={{0,192},{64,0},{128,64},{192,128},{1,193},{65,1},{129,65},{193,129... | collective-permute-start | bytes 1105928 | tf_op jit(solution)/shard_map/ppermute | solution.py:360
  154.0 7.0 %collective-permute-start.22 = (bf16[192,256]{1,0:T(8,128)(2,1)S(1)}, bf16[192,256]{1,0:T(8,128)(2,1)S(1)}, u32[]{:S(2)}, u32[]{:S(2)}) collective-permute-start(bf16[192,256]{1,0:T(8,128)(2,1)S(1)} %get-tuple-element.59.refs_0_), channel_id=1, source_target_pairs={{0,192},{64,0},{128,64},{192,128},{1,193},{65,1},{129,65},{193,129... | collective-permute-start | bytes 294920 | tf_op jit(solution)/shard_map/ppermute | solution.py:360
  154.6 6.4 %collective-permute-start.21 = (bf16[192,256]{1,0:T(8,128)(2,1)S(1)}, bf16[192,256]{1,0:T(8,128)(2,1)S(1)}, u32[]{:S(2)}, u32[]{:S(2)}) collective-permute-start(bf16[192,256]{1,0:T(8,128)(2,1)S(1)} %get-tuple-element.59.refs_0_), channel_id=1, source_target_pairs={{0,128},{64,192},{128,0},{192,64},{1,129},{65,193},{129,1},{193,65... | collective-permute-start | bytes 294920 | tf_op jit(solution)/shard_map/ppermute | solution.py:360
  157.0 4.9 %collective-permute-start.20 = (bf16[192,256]{1,0:T(8,128)(2,1)S(1)}, bf16[192,256]{1,0:T(8,128)(2,1)S(1)}, u32[]{:S(2)}, u32[]{:S(2)}) collective-permute-start(bf16[192,256]{1,0:T(8,128)(2,1)S(1)} %get-tuple-element.59.refs_0_), channel_id=1, source_target_pairs={{0,64},{64,128},{128,192},{192,0},{1,65},{65,129},{129,193},{193,1... | collective-permute-start | bytes 294920 | tf_op jit(solution)/shard_map/ppermute | solution.py:360
  163.3 1.7 collective-permute-start.26
  165.1 10.1 %collective-permute-start.27 = (bf16[48,1792]{1,0:T(8,128)(2,1)S(1)}, bf16[48,1792]{1,0:T(8,128)(2,1)S(1)}, u32[]{:S(2)}, u32[]{:S(2)}) collective-permute-start(bf16[48,1792]{1,0:T(8,128)(2,1)S(1)} %get-tuple-element.67), channel_id=1, source_target_pairs={{0,48},{16,0},{32,16},{48,32},{1,49},{17,1},{33,17},{49,33},{2,50}... | collective-permute-start | bytes 516104 | tf_op jit(solution)/shard_map/ppermute | solution.py:360
  167.5 8.8 %collective-permute-start.28 = (bf16[48,1792]{1,0:T(8,128)(2,1)S(1)}, bf16[48,1792]{1,0:T(8,128)(2,1)S(1)}, u32[]{:S(2)}, u32[]{:S(2)}) collective-permute-start(bf16[48,1792]{1,0:T(8,128)(2,1)S(1)} %get-tuple-element.68), channel_id=1, source_target_pairs={{0,32},{16,48},{32,0},{48,16},{1,33},{17,49},{33,1},{49,17},{2,34}... | collective-permute-start | bytes 516104 | tf_op jit(solution)/shard_map/ppermute | solution.py:360
  168.4 10.5 %collective-permute-start.29 = (bf16[48,1792]{1,0:T(8,128)(2,1)S(1)}, bf16[48,1792]{1,0:T(8,128)(2,1)S(1)}, u32[]{:S(2)}, u32[]{:S(2)}) collective-permute-start(bf16[48,1792]{1,0:T(8,128)(2,1)S(1)} %get-tuple-element.69), channel_id=1, source_target_pairs={{0,16},{16,32},{32,48},{48,0},{1,17},{17,33},{33,49},{49,1},{2,18}... | collective-permute-start | bytes 516104 | tf_op jit(solution)/shard_map/ppermute | solution.py:360

commit v6 on v5

--- a/solution.py
+++ b/solution.py
@@ -52,7 +52,7 @@
 def attention_kernel(
     place, q_ref, kl_ref, vl_ref, pool_ref, fresh_ref, table_ref, length_ref, parent_ref, *refs
 ):
-    out_weight, *outs, held_weight, done = refs
+    out_weight, out, q_next, kl_next, vl_next, keys_ref, mask_ref, held_weight, done = refs
     load = pltpu.make_async_copy(out_weight, held_weight, done)
     load.start()
     context = place[0]
@@ -100,39 +100,43 @@
     fresh_mask = jnp.concatenate([linked.T] * (rows // fresh_rows), axis=1)
     here = iota((fresh_rows, rows), 1) // fresh_rows == context
     fresh_mask = jnp.where(here, fresh_mask, 0.0)
-    mask = jnp.concatenate([page_mask, fresh_mask], axis=0) > 0.5
-
-    keys = jnp.concatenate([pool_ref[...], fresh_ref[...]], axis=0)
-    latents = keys[:, :LAT]
-    turned = keys[:, LAT:]
-    scale = (QK + ROPE) ** (-0.5)
-    for head, out in enumerate(outs):
-        start = head * (QK + ROPE)
-        plain = q_ref[:, start : start + QK]
-        rotary = q_ref[:, start + QK : start + QK + ROPE]
-        lifted = dot_nn(plain, kl_ref[head]).astype(BF16)
-        scores = (dot_nt(latents, lifted) + dot_nt(turned, rotary)) * scale
-        scores = jnp.where(mask, scores, NEGATIVE_FILL)
-        best = jnp.max(scores, axis=0, keepdims=True)
-        weights = jnp.exp(scores - best)
-        total = jnp.sum(weights, axis=0, keepdims=True)
-        values = dot_nn(latents, vl_ref[head]).T.astype(BF16)
-        mixed = dot_nn(values, weights.astype(BF16)) / total
-        out[:VD, :] = mixed.astype(BF16)
-        high, middle, low = split3(best + jnp.log(total))
-        line = iota((16, rows), 0)
-        extra = jnp.where(
-            line == 0,
-            high.astype(F32),
-            jnp.where(line == 1, middle.astype(F32), jnp.where(line == 2, low.astype(F32), 0.0)),
-        )
-        out[VD:, :] = extra.astype(BF16)
+    mask_ref[...] = jnp.concatenate([page_mask, fresh_mask], axis=0).astype(BF16)
+    keys_ref[...] = jnp.concatenate([pool_ref[...], fresh_ref[...]], axis=0)
+    second_kernel(q_ref, kl_ref.at[0], vl_ref.at[0], keys_ref, mask_ref, out)
+    q_next[...] = q_ref[:, QK + ROPE :]
+    kl_next[...] = kl_ref[1]
+    vl_next[...] = vl_ref[1]
     load.wait()
+
+
+def second_kernel(q_ref, kl_ref, vl_ref, keys_ref, mask_ref, out):
+    rows = q_ref.shape[0]
+    latents = keys_ref[:, :LAT]
+    turned = keys_ref[:, LAT:]
+    plain = q_ref[:, :QK]
+    rotary = q_ref[:, QK : QK + ROPE]
+    lifted = dot_nn(plain, kl_ref[...]).astype(BF16)
+    scores = (dot_nt(latents, lifted) + dot_nt(turned, rotary)) * (QK + ROPE) ** (-0.5)
+    scores = jnp.where(mask_ref[...].astype(F32) > 0.5, scores, NEGATIVE_FILL)
+    best = jnp.max(scores, axis=0, keepdims=True)
+    weights = jnp.exp(scores - best)
+    total = jnp.sum(weights, axis=0, keepdims=True)
+    values = dot_nn(latents, vl_ref[...]).T.astype(BF16)
+    mixed = dot_nn(values, weights.astype(BF16)) / total
+    out[:VD, :] = mixed.astype(BF16)
+    high, middle, low = split3(best + jnp.log(total))
+    line = iota((16, rows), 0)
+    extra = jnp.where(
+        line == 0,
+        high.astype(F32),
+        jnp.where(line == 1, middle.astype(F32), jnp.where(line == 2, low.astype(F32), 0.0)),
+    )
+    out[VD:, :] = extra.astype(BF16)
 
 
 def merge_kernel(place, *refs):
     core = place[2]
-    parts, (weight_ref, send_ref, keep_ref, scratch) = refs[:8], refs[8:]
+    parts, (weight_ref, send_ref, rest_ref, scratch) = refs[:8], refs[8:]
     heads = []
     for head in range(2):
         own = parts[4 * head : 4 * head + 4]
@@ -148,11 +152,13 @@
             mixed = mixed + part[:VD, :].astype(F32) * (share * inverse)
         heads.append(mixed)
     scratch[...] = jnp.concatenate(heads, axis=0).T.reshape(scratch.shape)
-    half = send_ref.shape[0]
-    sent = scratch[:, 1 - core].reshape(half, -1).astype(BF16)
+    rest_ref[...] = scratch[:, core].reshape(rest_ref.shape).astype(BF16)
+    sent = scratch[:, 1 - core].reshape(rest_ref.shape).astype(BF16)
     send_ref[...] = dot_nn(sent, weight_ref[...]).astype(BF16)
-    kept = scratch[:, core].reshape(half, -1).astype(BF16)
-    keep_ref[...] = dot_nn(kept, weight_ref[...])
+
+
+def keep_kernel(rest_ref, weight_ref, keep_ref):
+    keep_ref[...] = dot_nn(rest_ref[...], weight_ref[...])
 
 
 def add_kernel(place, keep_ref, got_ref, own_ref, *sends):
@@ -274,55 +280,55 @@
     )
 
 
-def near_kernel(place, gate_old, up_old, low1, high1, low3, high3, *refs):
-    gate_sum, up_sum = refs[3:]
+def squares_of(low_ref, high_ref, width):
+    tail = jnp.concatenate([low_ref[:, width:], high_ref[:, width:]], axis=0).astype(F32)
+    lane = iota(tail.shape, 1)
+    return tail, jnp.sum(jnp.where((lane >= 32) & (lane < 35), tail, 0.0), axis=1, keepdims=True)
+
+
+def near_kernel(place, gate_old, up_old, low0, high0, low1, high1, low3, high3, *refs):
+    gate_sum, up_sum, squares_ref, share_ref = refs[3:]
     gate1, up1 = partial_sums(place, 1, low1, high1, *refs[:3])
     gate3, up3 = partial_sums(place, 3, low3, high3, *refs[:3])
     gate_sum[...] = gate_old[...] + gate1 + gate3
     up_sum[...] = up_old[...] + up1 + up3
-
-
-def expert_kernel(place, gate_old, up_old, *refs):
-    expert = place[1].astype(F32)
-    parts = refs[:8]
-    gain_ref, gate_ref, up_ref, active_ref, share_ref = refs[8:]
-    slots = active_ref.shape[0]
-    width = gain_ref.shape[2]
-    count = 4
-    lane = iota((slots, TAIL), 1)
-    squares = 0.0
-    for index in range(count):
-        tail = jnp.concatenate([parts[2 * index][:, width:], parts[2 * index + 1][:, width:]], axis=0)
-        tail = tail.astype(F32)
-        squares = squares + jnp.sum(
-            jnp.where((lane >= 32) & (lane < 35), tail, 0.0), axis=1, keepdims=True
-        )
-        if index == 0:
-            shares = (
-                pltpu.roll(tail, TAIL - 8, 1)
-                + pltpu.roll(tail, TAIL - 16, 1)
-                + pltpu.roll(tail, TAIL - 24, 1)
-            )
-            share = jnp.sum(
-                jnp.where((tail == expert) & (lane < 8), shares, 0.0), axis=1, keepdims=True
-            )
-            share_ref[...] = jnp.broadcast_to(share, share_ref.shape)
+    width = refs[0].shape[2]
+    tail, squares = squares_of(low0, high0, width)
+    squares = squares + squares_of(low1, high1, width)[1] + squares_of(low3, high3, width)[1]
+    squares_ref[...] = jnp.broadcast_to(squares, squares_ref.shape)
+    shares = (
+        pltpu.roll(tail, TAIL - 8, 1)
+        + pltpu.roll(tail, TAIL - 16, 1)
+        + pltpu.roll(tail, TAIL - 24, 1)
+    )
+    named = (tail == place[1].astype(F32)) & (iota(tail.shape, 1) < 8)
+    share = jnp.sum(jnp.where(named, shares, 0.0), axis=1, keepdims=True)
+    share_ref[...] = jnp.broadcast_to(share, share_ref.shape)
+
+
+def expert_kernel(place, gate_old, up_old, squares_ref, low2, high2, *refs):
+    gain_ref, active_ref = refs[0], refs[3]
+    count, width = gain_ref.shape[0], gain_ref.shape[2]
+    squares = squares_ref[:, :1] + squares_of(low2, high2, width)[1]
     inverse = lax.rsqrt(squares * (1.0 / (count * width)) + NORM_EPSILON)
-    gate2, up2 = partial_sums(place, 2, parts[4], parts[5], gain_ref, gate_ref, up_ref)
+    gate2, up2 = partial_sums(place, 2, low2, high2, *refs[:3])
     gate_part = (gate_old[...] + gate2) * inverse
     up_part = (up_old[...] + up2) * inverse
     active_ref[...] = (gate_part / (1.0 + jnp.exp(-gate_part)) * up_part).astype(BF16)
 
 
-def down_kernel(place, *refs):
-    actives, others, (down_ref, share_ref, low_ref, high_ref) = refs[:4], refs[4:7], refs[7:]
-    width = low_ref.shape[1]
+def first_kernel(place, active0, active1, active3, other1, other3, down_ref, sum_ref):
+    width = sum_ref.shape[1]
+    at = pl.ds(pl.multiple_of(place[0] * width, 128), width)
+    made = dot_nn(active0[...], down_ref[:, at])
+    made = made + dot_nn(active1[...], other1[...])
+    sum_ref[...] = made + dot_nn(active3[...], other3[...])
+
+
+def down_kernel(sum_ref, active2, other2, share_ref, low_ref, high_ref):
+    made = sum_ref[...] + dot_nn(active2[...], other2[...])
+    made = (made * share_ref[:, :1]).astype(BF16)
     half = low_ref.shape[0]
-    at = pl.ds(pl.multiple_of(place[0] * width, 128), width)
-    made = dot_nn(actives[0][...], down_ref[:, at])
-    for active, other in zip(actives[1:], others):
-        made = made + dot_nn(active[...], other[...])
-    made = (made * share_ref[:, :1]).astype(BF16)
     low_ref[...] = made[:half]
     high_ref[...] = made[half:]
 
@@ -398,16 +404,28 @@
     for index, value in enumerate(places):
         place = jnp.where(number == index, value, place)
 
-    low, high, held_weight = call(
+    pool = page_pool.reshape(-1, page_pool.shape[-1])
+    fresh = fresh_latents.reshape(-1, fresh_latents.shape[-1])
+    key_rows = pool.shape[0] + fresh.shape[0]
+    piece = ((VD + 16, rows), BF16)
+    low, *rest, held_weight = call(
         attention_kernel,
-        [((VD + 16, rows), BF16)] * 2 + [(out_weight.shape, BF16)],
+        [
+            piece,
+            ((rows, QK + ROPE), BF16),
+            (key_lift.shape[1:], BF16),
+            (value_lift.shape[1:], BF16),
+            ((key_rows, pool.shape[1]), BF16),
+            ((key_rows, rows), BF16),
+            (out_weight.shape, BF16),
+        ],
         [
             place,
             queries,
             key_lift,
             value_lift,
-            page_pool.reshape(-1, page_pool.shape[-1]),
-            fresh_latents.reshape(-1, fresh_latents.shape[-1]),
+            pool,
+            fresh,
             page_table.T,
             context_lengths.reshape(1, -1),
             tree_parents.T,
@@ -419,17 +437,20 @@
         raw=1,
         scratch=[pltpu.SemaphoreType.DMA(())],
     )
+    (high,) = call(second_kernel, [piece], rest)
 
     def around(low, high):
-        low1, high1 = shift(low, CONTEXT, ring, 1), shift(high, CONTEXT, ring, 1)
-        low3, high3 = shift(low, CONTEXT, ring, -1), shift(high, CONTEXT, ring, -1)
-        low2, high2 = shift(low1, CONTEXT, ring, 1), shift(high3, CONTEXT, ring, -1)
+        low1 = shift(low, CONTEXT, ring, 1)
+        low3 = shift(low, CONTEXT, ring, -1)
+        high1, high3 = shift(high, CONTEXT, ring, 1), shift(high, CONTEXT, ring, -1)
+        low2 = shift(low1, CONTEXT, ring, 1)
+        high2 = shift(high3, CONTEXT, ring, -1)
         return (low, low1, low2, low3), (high, high1, high2, high3)
 
     lows, highs = around(low, high)
-    send, keep = call(
+    send, rest = call(
         merge_kernel,
-        [((half, width), BF16), ((half, width), F32)],
+        [((half, width), BF16), ((half, out_weight.shape[0]), BF16)],
         [place, *lows, *highs, held_weight],
         scalars=1,
         scratch=[pltpu.VMEM((wide * deep, 2, row_dev, out_weight.shape[0]), F32)],
@@ -445,6 +466,7 @@
         others.append(shift(cut, CONTEXT, ring, step))
     split = [((half // wide, width), F32)] + [((half // wide, width), BF16)] * (wide - 1)
     got = shift(send, CORE, 2, 1)
+    (keep,) = call(keep_kernel, [((half, width), F32)], [rest, held_weight])
     own, *sends = call(add_kernel, split, [place, keep, got], scalars=1)
     received = []
     for step, part in enumerate(sends, 1):
@@ -471,24 +493,32 @@
     weights = [norm_gain.reshape(ring, 1, width), gate_matrix[0], up_matrix[0]]
     sums = [((slots, hidden_units), F32)] * 2
     partial = call(own_kernel, sums, [place, lows[0], highs[0], *weights], scalars=1)
-    partial = call(
+    *partial, squares, share = call(
         near_kernel,
-        sums,
-        [place, *partial, lows[1], highs[1], lows[3], highs[3], *weights],
-        scalars=1,
-    )
-    active, share = call(
+        sums + [((slots, TAIL), F32)] * 2,
+        [place, *partial]
+        + [lows[0], highs[0], lows[1], highs[1], lows[3], highs[3]]
+        + weights,
+        scalars=1,
+    )
+    (active,) = call(
         expert_kernel,
-        [((slots, hidden_units), BF16), ((slots, TAIL), F32)],
-        [place, *partial, *[part for pair in zip(lows, highs) for part in pair], *weights],
-        scalars=1,
-    )
-    actives = [active] + [shift(active, CONTEXT, ring, step) for step in range(1, ring)]
+        [((slots, hidden_units), BF16)],
+        [place, *partial, squares, lows[2], highs[2], *weights],
+        scalars=1,
+    )
+    active2 = shift(active, CONTEXT, ring, 2)
+    active1, active3 = (shift(active, CONTEXT, ring, step) for step in (1, 3))
+    (made,) = call(
+        first_kernel,
+        [((slots, width), F32)],
+        [place, active, active1, active3, others[0], others[2], down_matrix[0]],
+        scalars=1,
+    )
     low, high = call(
         down_kernel,
         [((slots // 2, width), BF16)] * 2,
-        [place, *actives, *others, down_matrix[0], share],
-        scalars=1,
+        [made, active2, others[1], share],
     )
     parts = call(
         back_kernel,

time: 196 us -> 198 us (1.010)
  starting transfers between devices: 35.8 us -> 41.7 us
  waiting for transfers between devices: 97.3 us -> 92.8 us
    ppermute x30, starting transfers between devices: 35.8 us -> 41.7 us  [shift(): lax.ppermute(value, axis, [(i, (i + step) % count) for i in range(count)])]
    ppermute x30, waiting for transfers between devices: 97.3 us -> 92.8 us  [shift(): lax.ppermute(value, axis, [(i, (i + step) % count) for i in range(count)])]
    pallas_call x15 -> x18, Pallas kernels: 14.5 us -> 15.8 us  [call(): pl.pallas_call(kernel, out_shape=tuple((out(shape, dtype) for shape, dtyp...]
  transfers between devices with their start and end apart: 30 -> 30, of which waited for: 19 -> 20; matrix products, arithmetic and copies ran while one was open for 0% -> 0% of each run, Pallas kernels for 2% -> 3%
where the time goes in v6:
time: 198 us; the launch traced here: 196 us
  waiting for transfers between devices  92.8 us (47%)
  blocking collectives  45.9 us (23%)
  starting transfers between devices  41.7 us (21%)
  Pallas kernels  15.8 us (8%)
    ppermute x30, waiting for transfers between devices, shift(): lax.ppermute(value, axis, [(i, (i + step) % count) for i in range(count)])  92.8 us
    ppermute x30, starting transfers between devices, shift(): lax.ppermute(value, axis, [(i, (i + step) % count) for i in range(count)])  41.7 us
    all_to_all x1, blocking collectives, local(): mixed = lax.all_to_all(summed, DEEP, 0, 0, tiled=True)  19.2 us
    pallas_call x18, Pallas kernels, call(): pl.pallas_call(kernel, out_shape=tuple((out(shape, dtype) for shape, dtyp...  15.8 us
    all_to_all x1, blocking collectives, local(): returned = lax.all_to_all(summed, DEEP, 0, 0, tiled=True)  14 us
    all_to_all x1, blocking collectives, local(): lax.all_to_all(payload, DEEP, 0, 0, tiled=True)  12.7 us
  transfers between devices with their start and end apart: 30, of which 20 were waited for; matrix products, arithmetic and copies ran while one was open for 0% of the time, Pallas kernels for 3%

profile of v6, /device:TPU:24, one launch (start us, length us, event | category | flops | bytes accessed | tf_op | source)
XLA Modules:
  0.0 196.4 jit_solution(6175646829685823327)
XLA Ops:
  0.0 3.6 %shard_map.154 = (bf16[144,512]{1,0:T(8,128)(2,1)S(1)}, bf16[512,192]{1,0:T(8,128)(2,1)S(1)}, bf16[128,512]{1,0:T(8,128)(2,1)S(1)}, bf16[512,128]{1,0:T(8,128)(2...) custom-call(s32[8]{0:T(128)S(1)} %compare_select_fusion.4.place, ...), custom_call_target="tpu_custom_call" | custom-call | tf_op jit(solution)/shard_map/pallas_call | solution.py:355
  3.6 1.1 shard_map.155.refs_4_
  4.7 0.8 collective-permute-start.4
  5.5 2.5 %collective-permute-start = (bf16[144,512]{1,0:T(8,128)(2,1)S(1)}, bf16[144,512]{1,0:T(8,128)(2,1)S(1)}, u32[]{:S(2)}, u32[]{:S(2)}) collective-permute-start(bf16[144,512]{1,0:T(8,128)(2,1)S(1)} %get-tuple-element.42.refs_0_), channel_id=1, source_target_pairs={{0,64},{64,128},{128,192},{192,0},{1,65},{65,129},{129,193},{193,1... | collective-permute-start | bytes 442376 | tf_op jit(solution)/shard_map/ppermute | solution.py:366
  8.0 0.7 collective-permute-start.3
  8.7 1.3 collective-permute-start.2
  10.1 2.0 %collective-permute-done.4.refs_7_ = bf16[144,512]{1,0:T(8,128)(2,1)S(1)} collective-permute-done((bf16[144,512]{1,0:T(8,128)(2,1)S(1)}, bf16[144,512]{1,0:T(8,128)(2,1)S(1)}, u32[]{:S(2)}, u32[]{:S(2)}) %collective-permute-start.4) | collective-permute-done | bytes 147488 | tf_op jit(solution)/shard_map/ppermute | solution.py:366
  12.3 3.7 %collective-permute-start.1 = (bf16[144,512]{1,0:T(8,128)(2,1)S(1)}, bf16[144,512]{1,0:T(8,128)(2,1)S(1)}, u32[]{:S(2)}, u32[]{:S(2)}) collective-permute-start(bf16[144,512]{1,0:T(8,128)(2,1)S(1)} %collective-permute-done.refs_1_), channel_id=1, source_target_pairs={{0,64},{64,128},{128,192},{192,0},{1,65},{65,129},{129,193},{193,1... | collective-permute-start | bytes 442376 | tf_op jit(solution)/shard_map/ppermute | solution.py:366
  16.0 2.4 %collective-permute-done.5.refs_6_ = bf16[144,512]{1,0:T(8,128)(2,1)S(1)} collective-permute-done((bf16[144,512]{1,0:T(8,128)(2,1)S(1)}, bf16[144,512]{1,0:T(8,128)(2,1)S(1)}, u32[]{:S(2)}, u32[]{:S(2)}) %collective-permute-start.5) | collective-permute-done | bytes 147488 | tf_op jit(solution)/shard_map/ppermute | solution.py:366
  18.6 1.3 shard_map.156
  20.5 2.0 %collective-permute-done.6.got_ref = bf16[256,1792]{1,0:T(8,128)(2,1)S(1)} collective-permute-done((bf16[256,1792]{1,0:T(8,128)(2,1)S(1)}, bf16[256,1792]{1,0:T(8,128)(2,1)S(1)}, u32[]{:S(2)}, u32[]{:S(2)}) %collective-permute-start.6) | collective-permute-done | bytes 917536 | tf_op jit(solution)/shard_map/ppermute | solution.py:366
  22.5 0.7 shard_map.158
  23.2 1.6 collective-permute-start.7
  24.8 2.7 %collective-permute-start.8 = (bf16[64,1792]{1,0:T(8,128)(2,1)S(1)}, bf16[64,1792]{1,0:T(8,128)(2,1)S(1)}, u32[]{:S(2)}, u32[]{:S(2)}) collective-permute-start(bf16[64,1792]{1,0:T(8,128)(2,1)S(1)} %get-tuple-element.53), channel_id=1, source_target_pairs={{0,32},{16,48},{32,0},{48,16},{1,33},{17,49},{33,1},{49,17},{2,34}... | collective-permute-start | bytes 688136 | tf_op jit(solution)/shard_map/ppermute | solution.py:366
  27.5 1.4 collective-permute-start.9
  28.9 3.2 %collective-permute-done.7.refs_0_ = bf16[64,1792]{1,0:T(8,128)(2,1)S(1)} collective-permute-done((bf16[64,1792]{1,0:T(8,128)(2,1)S(1)}, bf16[64,1792]{1,0:T(8,128)(2,1)S(1)}, u32[]{:S(2)}, u32[]{:S(2)}) %collective-permute-start.7) | collective-permute-done | bytes 229408 | tf_op jit(solution)/shard_map/ppermute | solution.py:366
  32.1 5.9 %collective-permute-done.8.refs_1_ = bf16[64,1792]{1,0:T(8,128)(2,1)S(1)} collective-permute-done((bf16[64,1792]{1,0:T(8,128)(2,1)S(1)}, bf16[64,1792]{1,0:T(8,128)(2,1)S(1)}, u32[]{:S(2)}, u32[]{:S(2)}) %collective-permute-start.8) | collective-permute-done | bytes 229408 | tf_op jit(solution)/shard_map/ppermute | solution.py:366
  38.2 19.2 %all_to_all.15.parts_ref = bf16[8,8,1792]{2,1,0:T(8,128)(2,1)S(1)} all-to-all(bf16[8,8,1792]{2,1,0:T(8,128)(2,1)S(1)} %shard_map.159), channel_id=1, replica_groups=mesh['context'=4,'x'=4,'z'=8,'core'=2] {'z'}, dimensions={0} | all-to-all | bytes 458752 | tf_op jit(solution)/shard_map/all_to_all | solution.py:476
  57.5 12.7 %all_to_all.16 = bf16[8,8,1920]{2,1,0:T(8,128)(2,1)S(1)} all-to-all(bf16[8,8,1920]{2,1,0:T(8,128)(2,1)S(1)} %get-tuple-element.55), channel_id=1, replica_groups=mesh['context'=4,'x'=4,'z'=8,'core'=2] {'z'}, dimensions={0} | all-to-all | bytes 491520 | tf_op jit(solution)/shard_map/all_to_all | solution.py:482
  70.2 1.4 shard_map.161
  71.6 1.7 collective-permute-start.10
  73.3 3.1 %collective-permute-start.11 = (bf16[48,1920]{1,0:T(8,128)(2,1)S(1)}, bf16[48,1920]{1,0:T(8,128)(2,1)S(1)}, u32[]{:S(2)}, u32[]{:S(2)}) collective-permute-start(bf16[48,1920]{1,0:T(8,128)(2,1)S(1)} %get-tuple-element.59), channel_id=1, source_target_pairs={{0,32},{16,48},{32,0},{48,16},{1,33},{17,49},{33,1},{49,17},{2,34}... | collective-permute-start | bytes 552968 | tf_op jit(solution)/shard_map/ppermute | solution.py:366
  76.9 3.3 %collective-permute-done.10.refs_1_ = bf16[48,1920]{1,0:T(8,128)(2,1)S(1)} collective-permute-done((bf16[48,1920]{1,0:T(8,128)(2,1)S(1)}, bf16[48,1920]{1,0:T(8,128)(2,1)S(1)}, u32[]{:S(2)}, u32[]{:S(2)}) %collective-permute-start.10) | collective-permute-done | bytes 184352 | tf_op jit(solution)/shard_map/ppermute | solution.py:366
  80.2 2.0 %collective-permute-done.11.refs_2_ = bf16[48,1920]{1,0:T(8,128)(2,1)S(1)} collective-permute-done((bf16[48,1920]{1,0:T(8,128)(2,1)S(1)}, bf16[48,1920]{1,0:T(8,128)(2,1)S(1)}, u32[]{:S(2)}, u32[]{:S(2)}) %collective-permute-start.11) | collective-permute-done | bytes 184352 | tf_op jit(solution)/shard_map/ppermute | solution.py:366
  82.3 3.7 %collective-permute-start.14 = (bf16[96,1920]{1,0:T(8,128)(2,1)S(1)}, bf16[96,1920]{1,0:T(8,128)(2,1)S(1)}, u32[]{:S(2)}, u32[]{:S(2)}) collective-permute-start(bf16[96,1920]{1,0:T(8,128)(2,1)S(1)} %get-tuple-element.61.low_ref.low0), channel_id=1, source_target_pairs={{0,64},{64,128},{128,192},{192,0},{1,65},{65,129},{129,193},{193,1... | collective-permute-start | bytes 1105928 | tf_op jit(solution)/shard_map/ppermute | solution.py:366
  86.1 0.7 shard_map.166
  86.8 3.3 %collective-permute-start.22 = (bf16[256,1792]{1,0:T(8,128)(2,1)S(1)}, bf16[256,1792]{1,0:T(8,128)(2,1)S(1)}, u32[]{:S(2)}, u32[]{:S(2)}) collective-permute-start(bf16[256,1792]{1,0:T(8,128)(2,1)S(1)} %get-tuple-element.68), channel_id=1, source_target_pairs={{0,64},{64,128},{128,192},{192,0},{1,65},{65,129},{129,193},{193,1... | collective-permute-start | bytes 2752520 | tf_op jit(solution)/shard_map/ppermute | solution.py:366
  90.1 1.6 collective-permute-start.25
  91.7 3.4 %collective-permute-done.14.low1 = bf16[96,1920]{1,0:T(8,128)(2,1)S(1)} collective-permute-done((bf16[96,1920]{1,0:T(8,128)(2,1)S(1)}, bf16[96,1920]{1,0:T(8,128)(2,1)S(1)}, u32[]{:S(2)}, u32[]{:S(2)}) %collective-permute-start.14) | collective-permute-done | bytes 368672 | tf_op jit(solution)/shard_map/ppermute | solution.py:366
  95.1 3.7 %collective-permute-start.15 = (bf16[96,1920]{1,0:T(8,128)(2,1)S(1)}, bf16[96,1920]{1,0:T(8,128)(2,1)S(1)}, u32[]{:S(2)}, u32[]{:S(2)}) collective-permute-start(bf16[96,1920]{1,0:T(8,128)(2,1)S(1)} %collective-permute-done.13.high_ref.high0), channel_id=1, source_target_pairs={{0,64},{64,128},{128,192},{192,0},{1,65},{65,129},{129,193},{193,1... | collective-permute-start | bytes 1105928 | tf_op jit(solution)/shard_map/ppermute | solution.py:366
  98.8 43.0 %collective-permute-done.15.high1 = bf16[96,1920]{1,0:T(8,128)(2,1)S(1)} collective-permute-done((bf16[96,1920]{1,0:T(8,128)(2,1)S(1)}, bf16[96,1920]{1,0:T(8,128)(2,1)S(1)}, u32[]{:S(2)}, u32[]{:S(2)}) %collective-permute-start.15) | collective-permute-done | bytes 368672 | tf_op jit(solution)/shard_map/ppermute | solution.py:366
  141.7 3.7 %collective-permute-start.18 = (bf16[96,1920]{1,0:T(8,128)(2,1)S(1)}, bf16[96,1920]{1,0:T(8,128)(2,1)S(1)}, u32[]{:S(2)}, u32[]{:S(2)}) collective-permute-start(bf16[96,1920]{1,0:T(8,128)(2,1)S(1)} %collective-permute-done.14.low1), channel_id=1, source_target_pairs={{0,64},{64,128},{128,192},{192,0},{1,65},{65,129},{129,193},{193,1... | collective-permute-start | bytes 1105928 | tf_op jit(solution)/shard_map/ppermute | solution.py:366
  145.5 1.1 shard_map.163
  146.6 1.5 shard_map.164
  148.0 5.0 %collective-permute-done.18.low2 = bf16[96,1920]{1,0:T(8,128)(2,1)S(1)} collective-permute-done((bf16[96,1920]{1,0:T(8,128)(2,1)S(1)}, bf16[96,1920]{1,0:T(8,128)(2,1)S(1)}, u32[]{:S(2)}, u32[]{:S(2)}) %collective-permute-start.18) | collective-permute-done | bytes 368672 | tf_op jit(solution)/shard_map/ppermute | solution.py:366
  153.0 3.4 %collective-permute-done.19.high2 = bf16[96,1920]{1,0:T(8,128)(2,1)S(1)} collective-permute-done((bf16[96,1920]{1,0:T(8,128)(2,1)S(1)}, bf16[96,1920]{1,0:T(8,128)(2,1)S(1)}, u32[]{:S(2)}, u32[]{:S(2)}) %collective-permute-start.19) | collective-permute-done | bytes 368672 | tf_op jit(solution)/shard_map/ppermute | solution.py:366
  156.4 1.1 shard_map.165.active0
  157.9 1.7 collective-permute-start.21
  159.7 3.2 %collective-permute-done.20.active1 = bf16[192,256]{1,0:T(8,128)(2,1)S(1)} collective-permute-done((bf16[192,256]{1,0:T(8,128)(2,1)S(1)}, bf16[192,256]{1,0:T(8,128)(2,1)S(1)}, u32[]{:S(2)}, u32[]{:S(2)}) %collective-permute-start.20) | collective-permute-done | bytes 98336 | tf_op jit(solution)/shard_map/ppermute | solution.py:366
  162.8 1.3 collective-permute-done.21.active3
  164.2 1.2 shard_map.167.sum_ref
  166.3 1.6 collective-permute-done.26.got_ref
  167.9 2.2 %collective-permute-start.27 = (bf16[48,1792]{1,0:T(8,128)(2,1)S(1)}, bf16[48,1792]{1,0:T(8,128)(2,1)S(1)}, u32[]{:S(2)}, u32[]{:S(2)}) collective-permute-start(bf16[48,1792]{1,0:T(8,128)(2,1)S(1)} %get-tuple-element.75), channel_id=1, source_target_pairs={{0,48},{16,0},{32,16},{48,32},{1,49},{17,1},{33,17},{49,33},{2,50}... | collective-permute-start | bytes 516104 | tf_op jit(solution)/shard_map/ppermute | solution.py:366
  170.2 1.0 collective-permute-start.28
  171.2 6.6 %collective-permute-done.27.refs_1_ = bf16[48,1792]{1,0:T(8,128)(2,1)S(1)} collective-permute-done((bf16[48,1792]{1,0:T(8,128)(2,1)S(1)}, bf16[48,1792]{1,0:T(8,128)(2,1)S(1)}, u32[]{:S(2)}, u32[]{:S(2)}) %collective-permute-start.27) | collective-permute-done | bytes 172064 | tf_op jit(solution)/shard_map/ppermute | solution.py:366
  177.8 1.1 collective-permute-done.28.refs_2_
  179.0 2.5 %collective-permute-done.29.refs_3_ = bf16[48,1792]{1,0:T(8,128)(2,1)S(1)} collective-permute-done((bf16[48,1792]{1,0:T(8,128)(2,1)S(1)}, bf16[48,1792]{1,0:T(8,128)(2,1)S(1)}, u32[]{:S(2)}, u32[]{:S(2)}) %collective-permute-start.29) | collective-permute-done | bytes 172064 | tf_op jit(solution)/shard_map/ppermute | solution.py:366
  181.8 14.0 %all_to_all.17.parts_ref = bf16[8,8,1792]{2,1,0:T(8,128)(2,1)S(1)} all-to-all(bf16[8,8,1792]{2,1,0:T(8,128)(2,1)S(1)} %shard_map.170), channel_id=1, replica_groups=mesh['context'=4,'x'=4,'z'=8,'core'=2] {'z'}, dimensions={0} | all-to-all | bytes 458752 | tf_op jit(solution)/shard_map/all_to_all | solution.py:530
  (48 shorter events, 4.1 us)
Async XLA Ops:
  4.7 7.3 %collective-permute-start.4 = (bf16[144,512]{1,0:T(8,128)(2,1)S(1)}, bf16[144,512]{1,0:T(8,128)(2,1)S(1)}, u32[]{:S(2)}, u32[]{:S(2)}) collective-permute-start(bf16[144,512]{1,0:T(8,128)(2,1)S(1)} %shard_map.155.refs_4_), channel_id=1, source_target_pairs={{0,192},{64,0},{128,64},{192,128},{1,193},{65,1},{129,65},{193,129... | collective-permute-start | bytes 442376 | tf_op jit(solution)/shard_map/ppermute | solution.py:366
  5.5 6.7 %collective-permute-start = (bf16[144,512]{1,0:T(8,128)(2,1)S(1)}, bf16[144,512]{1,0:T(8,128)(2,1)S(1)}, u32[]{:S(2)}, u32[]{:S(2)}) collective-permute-start(bf16[144,512]{1,0:T(8,128)(2,1)S(1)} %get-tuple-element.42.refs_0_), channel_id=1, source_target_pairs={{0,64},{64,128},{128,192},{192,0},{1,65},{65,129},{129,193},{193,1... | collective-permute-start | bytes 442376 | tf_op jit(solution)/shard_map/ppermute | solution.py:366
  8.0 7.9 %collective-permute-start.3 = (bf16[144,512]{1,0:T(8,128)(2,1)S(1)}, bf16[144,512]{1,0:T(8,128)(2,1)S(1)}, u32[]{:S(2)}, u32[]{:S(2)}) collective-permute-start(bf16[144,512]{1,0:T(8,128)(2,1)S(1)} %shard_map.155.refs_4_), channel_id=1, source_target_pairs={{0,64},{64,128},{128,192},{192,0},{1,65},{65,129},{129,193},{193,1... | collective-permute-start | bytes 442376 | tf_op jit(solution)/shard_map/ppermute | solution.py:366
  8.7 7.2 %collective-permute-start.2 = (bf16[144,512]{1,0:T(8,128)(2,1)S(1)}, bf16[144,512]{1,0:T(8,128)(2,1)S(1)}, u32[]{:S(2)}, u32[]{:S(2)}) collective-permute-start(bf16[144,512]{1,0:T(8,128)(2,1)S(1)} %get-tuple-element.42.refs_0_), channel_id=1, source_target_pairs={{0,192},{64,0},{128,64},{192,128},{1,193},{65,1},{129,65},{193,129... | collective-permute-start | bytes 442376 | tf_op jit(solution)/shard_map/ppermute | solution.py:366
  12.1 6.4 %collective-permute-start.5 = (bf16[144,512]{1,0:T(8,128)(2,1)S(1)}, bf16[144,512]{1,0:T(8,128)(2,1)S(1)}, u32[]{:S(2)}, u32[]{:S(2)}) collective-permute-start(bf16[144,512]{1,0:T(8,128)(2,1)S(1)} %collective-permute-done.4.refs_7_), channel_id=1, source_target_pairs={{0,192},{64,0},{128,64},{192,128},{1,193},{65,1},{129,65},{193,129... | collective-permute-start | bytes 442376 | tf_op jit(solution)/shard_map/ppermute | solution.py:366
  12.3 6.4 %collective-permute-start.1 = (bf16[144,512]{1,0:T(8,128)(2,1)S(1)}, bf16[144,512]{1,0:T(8,128)(2,1)S(1)}, u32[]{:S(2)}, u32[]{:S(2)}) collective-permute-start(bf16[144,512]{1,0:T(8,128)(2,1)S(1)} %collective-permute-done.refs_1_), channel_id=1, source_target_pairs={{0,64},{64,128},{128,192},{192,0},{1,65},{65,129},{129,193},{193,1... | collective-permute-start | bytes 442376 | tf_op jit(solution)/shard_map/ppermute | solution.py:366
  19.9 2.6 %collective-permute-start.6 = (bf16[256,1792]{1,0:T(8,128)(2,1)S(1)}, bf16[256,1792]{1,0:T(8,128)(2,1)S(1)}, u32[]{:S(2)}, u32[]{:S(2)}) collective-permute-start(bf16[256,1792]{1,0:T(8,128)(2,1)S(1)} %get-tuple-element.50.after_ref), channel_id=1, source_target_pairs={{0,1},{1,0},{2,3},{3,2},{4,5},{5,4},{6,7},{7,6},{8,9},{9,8},{10,11... | collective-permute-start | bytes 2752520 | tf_op jit(solution)/shard_map/ppermute | solution.py:366
  20.0 37.3 %copy-start.4 = (bf16[8,1792]{1,0:T(8,128)(2,1)S(1)}, bf16[8,1792]{1,0:T(8,128)(2,1)}, u32[]{:S(2)}) copy-start(bf16[8,1792]{1,0:T(8,128)(2,1)} %residual_ref.1) | copy-start | bytes 86020
  20.1 37.3 %copy-start.5 = (s32[8,8]{1,0:T(8,128)S(1)}, s32[8,8]{1,0:T(8,128)}, u32[]{:S(2)}) copy-start(s32[8,8]{1,0:T(8,128)} %ids_ref.1) | copy-start | bytes 772
  20.1 37.3 %copy-start.6 = (f32[8,8]{1,0:T(8,128)S(1)}, f32[8,8]{1,0:T(8,128)}, u32[]{:S(2)}) copy-start(f32[8,8]{1,0:T(8,128)} %weights_ref.1) | copy-start | bytes 772
  20.1 66.0 %copy-start.2 = (bf16[1,256,7168]{2,1,0:T(8,128)(2,1)S(1)}, bf16[1,256,7168]{2,1,0:T(8,128)(2,1)}, u32[]{:S(2)}) copy-start(bf16[1,256,7168]{2,1,0:T(8,128)(2,1)} %param.31) | copy-start | bytes 11010052
  23.2 8.9 %collective-permute-start.7 = (bf16[64,1792]{1,0:T(8,128)(2,1)S(1)}, bf16[64,1792]{1,0:T(8,128)(2,1)S(1)}, u32[]{:S(2)}, u32[]{:S(2)}) collective-permute-start(bf16[64,1792]{1,0:T(8,128)(2,1)S(1)} %get-tuple-element.52), channel_id=1, source_target_pairs={{0,16},{16,32},{32,48},{48,0},{1,17},{17,33},{33,49},{49,1},{2,18}... | collective-permute-start | bytes 688136 | tf_op jit(solution)/shard_map/ppermute | solution.py:366
  24.8 13.3 %collective-permute-start.8 = (bf16[64,1792]{1,0:T(8,128)(2,1)S(1)}, bf16[64,1792]{1,0:T(8,128)(2,1)S(1)}, u32[]{:S(2)}, u32[]{:S(2)}) collective-permute-start(bf16[64,1792]{1,0:T(8,128)(2,1)S(1)} %get-tuple-element.53), channel_id=1, source_target_pairs={{0,32},{16,48},{32,0},{48,16},{1,33},{17,49},{33,1},{49,17},{2,34}... | collective-permute-start | bytes 688136 | tf_op jit(solution)/shard_map/ppermute | solution.py:366
  27.5 10.5 %collective-permute-start.9 = (bf16[64,1792]{1,0:T(8,128)(2,1)S(1)}, bf16[64,1792]{1,0:T(8,128)(2,1)S(1)}, u32[]{:S(2)}, u32[]{:S(2)}) collective-permute-start(bf16[64,1792]{1,0:T(8,128)(2,1)S(1)} %get-tuple-element.54), channel_id=1, source_target_pairs={{0,48},{16,0},{32,16},{48,32},{1,49},{17,1},{33,17},{49,33},{2,50}... | collective-permute-start | bytes 688136 | tf_op jit(solution)/shard_map/ppermute | solution.py:366
  38.0 107.4 %copy-start.1 = (bf16[1,7168,256]{2,1,0:T(8,128)(2,1)S(1)}, bf16[1,7168,256]{2,1,0:T(8,128)(2,1)}, u32[]{:S(2)}) copy-start(bf16[1,7168,256]{2,1,0:T(8,128)(2,1)} %param.30) | copy-start | bytes 11010052
  38.2 107.3 %copy-start = (bf16[1,7168,256]{2,1,0:T(8,128)(2,1)S(1)}, bf16[1,7168,256]{2,1,0:T(8,128)(2,1)}, u32[]{:S(2)}) copy-start(bf16[1,7168,256]{2,1,0:T(8,128)(2,1)} %param.29) | copy-start | bytes 11010052
  38.2 107.3 %copy-start.3 = (f32[7168]{0:T(1024)S(1)}, f32[7168]{0:T(1024)}, u32[]{:S(2)}) copy-start(f32[7168]{0:T(1024)} %param.26) | copy-start | bytes 86020
  71.6 8.6 %collective-permute-start.10 = (bf16[48,1920]{1,0:T(8,128)(2,1)S(1)}, bf16[48,1920]{1,0:T(8,128)(2,1)S(1)}, u32[]{:S(2)}, u32[]{:S(2)}) collective-permute-start(bf16[48,1920]{1,0:T(8,128)(2,1)S(1)} %get-tuple-element.58), channel_id=1, source_target_pairs={{0,16},{16,32},{32,48},{48,0},{1,17},{17,33},{33,49},{49,1},{2,18}... | collective-permute-start | bytes 552968 | tf_op jit(solution)/shard_map/ppermute | solution.py:366
  73.3 8.9 %collective-permute-start.11 = (bf16[48,1920]{1,0:T(8,128)(2,1)S(1)}, bf16[48,1920]{1,0:T(8,128)(2,1)S(1)}, u32[]{:S(2)}, u32[]{:S(2)}) collective-permute-start(bf16[48,1920]{1,0:T(8,128)(2,1)S(1)} %get-tuple-element.59), channel_id=1, source_target_pairs={{0,32},{16,48},{32,0},{48,16},{1,33},{17,49},{33,1},{49,17},{2,34}... | collective-permute-start | bytes 552968 | tf_op jit(solution)/shard_map/ppermute | solution.py:366
  76.4 5.8 %collective-permute-start.12 = (bf16[48,1920]{1,0:T(8,128)(2,1)S(1)}, bf16[48,1920]{1,0:T(8,128)(2,1)S(1)}, u32[]{:S(2)}, u32[]{:S(2)}) collective-permute-start(bf16[48,1920]{1,0:T(8,128)(2,1)S(1)} %get-tuple-element.60), channel_id=1, source_target_pairs={{0,48},{16,0},{32,16},{48,32},{1,49},{17,1},{33,17},{49,33},{2,50}... | collective-permute-start | bytes 552968 | tf_op jit(solution)/shard_map/ppermute | solution.py:366
  82.2 7.9 %collective-permute-start.13 = (bf16[96,1920]{1,0:T(8,128)(2,1)S(1)}, bf16[96,1920]{1,0:T(8,128)(2,1)S(1)}, u32[]{:S(2)}, u32[]{:S(2)}) collective-permute-start(bf16[96,1920]{1,0:T(8,128)(2,1)S(1)} %get-tuple-element.62), channel_id=1, source_target_pairs={{0,1},{1,0},{2,3},{3,2},{4,5},{5,4},{6,7},{7,6},{8,9},{9,8},{10,11... | collective-permute-start | bytes 1105928 | tf_op jit(solution)/shard_map/ppermute | solution.py:366
  82.3 12.7 %collective-permute-start.14 = (bf16[96,1920]{1,0:T(8,128)(2,1)S(1)}, bf16[96,1920]{1,0:T(8,128)(2,1)S(1)}, u32[]{:S(2)}, u32[]{:S(2)}) collective-permute-start(bf16[96,1920]{1,0:T(8,128)(2,1)S(1)} %get-tuple-element.61.low_ref.low0), channel_id=1, source_target_pairs={{0,64},{64,128},{128,192},{192,0},{1,65},{65,129},{129,193},{193,1... | collective-permute-start | bytes 1105928 | tf_op jit(solution)/shard_map/ppermute | solution.py:366
  86.1 12.7 %collective-permute-start.16 = (bf16[96,1920]{1,0:T(8,128)(2,1)S(1)}, bf16[96,1920]{1,0:T(8,128)(2,1)S(1)}, u32[]{:S(2)}, u32[]{:S(2)}) collective-permute-start(bf16[96,1920]{1,0:T(8,128)(2,1)S(1)} %get-tuple-element.61.low_ref.low0), channel_id=1, source_target_pairs={{0,192},{64,0},{128,64},{192,128},{1,193},{65,1},{129,65},{193,129... | collective-permute-start | bytes 1105928 | tf_op jit(solution)/shard_map/ppermute | solution.py:366
  86.8 72.8 %collective-permute-start.22 = (bf16[256,1792]{1,0:T(8,128)(2,1)S(1)}, bf16[256,1792]{1,0:T(8,128)(2,1)S(1)}, u32[]{:S(2)}, u32[]{:S(2)}) collective-permute-start(bf16[256,1792]{1,0:T(8,128)(2,1)S(1)} %get-tuple-element.68), channel_id=1, source_target_pairs={{0,64},{64,128},{128,192},{192,0},{1,65},{65,129},{129,193},{193,1... | collective-permute-start | bytes 2752520 | tf_op jit(solution)/shard_map/ppermute | solution.py:366
  90.1 69.5 %collective-permute-start.23 = (bf16[256,1792]{1,0:T(8,128)(2,1)S(1)}, bf16[256,1792]{1,0:T(8,128)(2,1)S(1)}, u32[]{:S(2)}, u32[]{:S(2)}) collective-permute-start(bf16[256,1792]{1,0:T(8,128)(2,1)S(1)} %get-tuple-element.69), channel_id=1, source_target_pairs={{0,192},{64,0},{128,64},{192,128},{1,193},{65,1},{129,65},{193,129... | collective-permute-start | bytes 2752520 | tf_op jit(solution)/shard_map/ppermute | solution.py:366
  90.1 75.3 %collective-permute-start.25 = (bf16[256,1792]{1,0:T(8,128)(2,1)S(1)}, bf16[256,1792]{1,0:T(8,128)(2,1)S(1)}, u32[]{:S(2)}, u32[]{:S(2)}) collective-permute-start(bf16[256,1792]{1,0:T(8,128)(2,1)S(1)} %get-tuple-element.70), channel_id=1, source_target_pairs={{0,128},{64,192},{128,0},{192,64},{1,129},{65,193},{129,1},{193,65... | collective-permute-start | bytes 2752520 | tf_op jit(solution)/shard_map/ppermute | solution.py:366
  95.1 46.7 %collective-permute-start.15 = (bf16[96,1920]{1,0:T(8,128)(2,1)S(1)}, bf16[96,1920]{1,0:T(8,128)(2,1)S(1)}, u32[]{:S(2)}, u32[]{:S(2)}) collective-permute-start(bf16[96,1920]{1,0:T(8,128)(2,1)S(1)} %collective-permute-done.13.high_ref.high0), channel_id=1, source_target_pairs={{0,64},{64,128},{128,192},{192,0},{1,65},{65,129},{129,193},{193,1... | collective-permute-start | bytes 1105928 | tf_op jit(solution)/shard_map/ppermute | solution.py:366
  98.8 46.7 %collective-permute-start.17 = (bf16[96,1920]{1,0:T(8,128)(2,1)S(1)}, bf16[96,1920]{1,0:T(8,128)(2,1)S(1)}, u32[]{:S(2)}, u32[]{:S(2)}) collective-permute-start(bf16[96,1920]{1,0:T(8,128)(2,1)S(1)} %collective-permute-done.13.high_ref.high0), channel_id=1, source_target_pairs={{0,192},{64,0},{128,64},{192,128},{1,193},{65,1},{129,65},{193,129... | collective-permute-start | bytes 1105928 | tf_op jit(solution)/shard_map/ppermute | solution.py:366
  141.7 11.3 %collective-permute-start.18 = (bf16[96,1920]{1,0:T(8,128)(2,1)S(1)}, bf16[96,1920]{1,0:T(8,128)(2,1)S(1)}, u32[]{:S(2)}, u32[]{:S(2)}) collective-permute-start(bf16[96,1920]{1,0:T(8,128)(2,1)S(1)} %collective-permute-done.14.low1), channel_id=1, source_target_pairs={{0,64},{64,128},{128,192},{192,0},{1,65},{65,129},{129,193},{193,1... | collective-permute-start | bytes 1105928 | tf_op jit(solution)/shard_map/ppermute | solution.py:366
  145.4 11.0 %collective-permute-start.19 = (bf16[96,1920]{1,0:T(8,128)(2,1)S(1)}, bf16[96,1920]{1,0:T(8,128)(2,1)S(1)}, u32[]{:S(2)}, u32[]{:S(2)}) collective-permute-start(bf16[96,1920]{1,0:T(8,128)(2,1)S(1)} %collective-permute-done.17.high3), channel_id=1, source_target_pairs={{0,192},{64,0},{128,64},{192,128},{1,193},{65,1},{129,65},{193,129... | collective-permute-start | bytes 1105928 | tf_op jit(solution)/shard_map/ppermute | solution.py:366
  157.6 5.3 %collective-permute-start.20 = (bf16[192,256]{1,0:T(8,128)(2,1)S(1)}, bf16[192,256]{1,0:T(8,128)(2,1)S(1)}, u32[]{:S(2)}, u32[]{:S(2)}) collective-permute-start(bf16[192,256]{1,0:T(8,128)(2,1)S(1)} %shard_map.165.active0), channel_id=1, source_target_pairs={{0,64},{64,128},{128,192},{192,0},{1,65},{65,129},{129,193},{193,1... | collective-permute-start | bytes 294920 | tf_op jit(solution)/shard_map/ppermute | solution.py:366
  157.9 6.2 %collective-permute-start.21 = (bf16[192,256]{1,0:T(8,128)(2,1)S(1)}, bf16[192,256]{1,0:T(8,128)(2,1)S(1)}, u32[]{:S(2)}, u32[]{:S(2)}) collective-permute-start(bf16[192,256]{1,0:T(8,128)(2,1)S(1)} %shard_map.165.active0), channel_id=1, source_target_pairs={{0,192},{64,0},{128,64},{192,128},{1,193},{65,1},{129,65},{193,129... | collective-permute-start | bytes 294920 | tf_op jit(solution)/shard_map/ppermute | solution.py:366
  159.7 6.1 %collective-permute-start.24 = (bf16[192,256]{1,0:T(8,128)(2,1)S(1)}, bf16[192,256]{1,0:T(8,128)(2,1)S(1)}, u32[]{:S(2)}, u32[]{:S(2)}) collective-permute-start(bf16[192,256]{1,0:T(8,128)(2,1)S(1)} %shard_map.165.active0), channel_id=1, source_target_pairs={{0,128},{64,192},{128,0},{192,64},{1,129},{65,193},{129,1},{193,65... | collective-permute-start | bytes 294920 | tf_op jit(solution)/shard_map/ppermute | solution.py:366
  166.2 1.7 collective-permute-start.26
  167.9 9.9 %collective-permute-start.27 = (bf16[48,1792]{1,0:T(8,128)(2,1)S(1)}, bf16[48,1792]{1,0:T(8,128)(2,1)S(1)}, u32[]{:S(2)}, u32[]{:S(2)}) collective-permute-start(bf16[48,1792]{1,0:T(8,128)(2,1)S(1)} %get-tuple-element.75), channel_id=1, source_target_pairs={{0,48},{16,0},{32,16},{48,32},{1,49},{17,1},{33,17},{49,33},{2,50}... | collective-permute-start | bytes 516104 | tf_op jit(solution)/shard_map/ppermute | solution.py:366
  170.2 8.8 %collective-permute-start.28 = (bf16[48,1792]{1,0:T(8,128)(2,1)S(1)}, bf16[48,1792]{1,0:T(8,128)(2,1)S(1)}, u32[]{:S(2)}, u32[]{:S(2)}) collective-permute-start(bf16[48,1792]{1,0:T(8,128)(2,1)S(1)} %get-tuple-element.76), channel_id=1, source_target_pairs={{0,32},{16,48},{32,0},{48,16},{1,33},{17,49},{33,1},{49,17},{2,34}... | collective-permute-start | bytes 516104 | tf_op jit(solution)/shard_map/ppermute | solution.py:366
  171.2 10.3 %collective-permute-start.29 = (bf16[48,1792]{1,0:T(8,128)(2,1)S(1)}, bf16[48,1792]{1,0:T(8,128)(2,1)S(1)}, u32[]{:S(2)}, u32[]{:S(2)}) collective-permute-start(bf16[48,1792]{1,0:T(8,128)(2,1)S(1)} %get-tuple-element.77), channel_id=1, source_target_pairs={{0,16},{16,32},{32,48},{48,0},{1,17},{17,33},{33,49},{49,1},{2,18}... | collective-permute-start | bytes 516104 | tf_op jit(solution)/shard_map/ppermute | solution.py:366

commit v7 on v6

--- a/solution.py
+++ b/solution.py
@@ -52,7 +52,7 @@
 def attention_kernel(
     place, q_ref, kl_ref, vl_ref, pool_ref, fresh_ref, table_ref, length_ref, parent_ref, *refs
 ):
-    out_weight, out, q_next, kl_next, vl_next, keys_ref, mask_ref, held_weight, done = refs
+    out_weight, *outs, held_weight, keys_ref, mask_ref, done = refs
     load = pltpu.make_async_copy(out_weight, held_weight, done)
     load.start()
     context = place[0]
@@ -102,26 +102,25 @@
     fresh_mask = jnp.where(here, fresh_mask, 0.0)
     mask_ref[...] = jnp.concatenate([page_mask, fresh_mask], axis=0).astype(BF16)
     keys_ref[...] = jnp.concatenate([pool_ref[...], fresh_ref[...]], axis=0)
-    second_kernel(q_ref, kl_ref.at[0], vl_ref.at[0], keys_ref, mask_ref, out)
-    q_next[...] = q_ref[:, QK + ROPE :]
-    kl_next[...] = kl_ref[1]
-    vl_next[...] = vl_ref[1]
+    for head, out in enumerate(outs):
+        attend(head, q_ref, kl_ref, vl_ref, keys_ref, mask_ref, out)
     load.wait()
 
 
-def second_kernel(q_ref, kl_ref, vl_ref, keys_ref, mask_ref, out):
+def attend(head, q_ref, kl_ref, vl_ref, keys_ref, mask_ref, out):
     rows = q_ref.shape[0]
     latents = keys_ref[:, :LAT]
     turned = keys_ref[:, LAT:]
-    plain = q_ref[:, :QK]
-    rotary = q_ref[:, QK : QK + ROPE]
-    lifted = dot_nn(plain, kl_ref[...]).astype(BF16)
+    start = head * (QK + ROPE)
+    plain = q_ref[:, start : start + QK]
+    rotary = q_ref[:, start + QK : start + QK + ROPE]
+    lifted = dot_nn(plain, kl_ref[head]).astype(BF16)
     scores = (dot_nt(latents, lifted) + dot_nt(turned, rotary)) * (QK + ROPE) ** (-0.5)
     scores = jnp.where(mask_ref[...].astype(F32) > 0.5, scores, NEGATIVE_FILL)
     best = jnp.max(scores, axis=0, keepdims=True)
     weights = jnp.exp(scores - best)
     total = jnp.sum(weights, axis=0, keepdims=True)
-    values = dot_nn(latents, vl_ref[...]).T.astype(BF16)
+    values = dot_nn(latents, vl_ref[head]).T.astype(BF16)
     mixed = dot_nn(values, weights.astype(BF16)) / total
     out[:VD, :] = mixed.astype(BF16)
     high, middle, low = split3(best + jnp.log(total))
@@ -267,7 +266,7 @@
 
 def partial_sums(place, index, low_ref, high_ref, gain_ref, gate_ref, up_ref):
     count, width = gain_ref.shape[0], gain_ref.shape[2]
-    source = lax.rem(place[0] + (count - index), count)
+    source = lax.rem(place[0] + count + index * (2 * place[2] - 1), count)
     rows = jnp.concatenate([low_ref[:, :width], high_ref[:, :width]], axis=0)
     scaled = (rows.astype(F32) * gain_ref[source]).astype(BF16)
     at = pl.ds(pl.multiple_of(source * width, width), width)
@@ -407,18 +406,9 @@
     pool = page_pool.reshape(-1, page_pool.shape[-1])
     fresh = fresh_latents.reshape(-1, fresh_latents.shape[-1])
     key_rows = pool.shape[0] + fresh.shape[0]
-    piece = ((VD + 16, rows), BF16)
-    low, *rest, held_weight = call(
+    low, high, held_weight = call(
         attention_kernel,
-        [
-            piece,
-            ((rows, QK + ROPE), BF16),
-            (key_lift.shape[1:], BF16),
-            (value_lift.shape[1:], BF16),
-            ((key_rows, pool.shape[1]), BF16),
-            ((key_rows, rows), BF16),
-            (out_weight.shape, BF16),
-        ],
+        [((VD + 16, rows), BF16)] * 2 + [(out_weight.shape, BF16)],
         [
             place,
             queries,
@@ -435,19 +425,37 @@
         hold=False,
         limit=24,
         raw=1,
-        scratch=[pltpu.SemaphoreType.DMA(())],
-    )
-    (high,) = call(second_kernel, [piece], rest)
-
-    def around(low, high):
-        low1 = shift(low, CONTEXT, ring, 1)
-        low3 = shift(low, CONTEXT, ring, -1)
-        high1, high3 = shift(high, CONTEXT, ring, 1), shift(high, CONTEXT, ring, -1)
-        low2 = shift(low1, CONTEXT, ring, 1)
-        high2 = shift(high3, CONTEXT, ring, -1)
+        scratch=[
+            pltpu.VMEM((key_rows, pool.shape[1]), BF16),
+            pltpu.VMEM((key_rows, rows), BF16),
+            pltpu.SemaphoreType.DMA(()),
+        ],
+    )
+
+    def around(low, high, turn):
+        low1, high3 = turn(low, 1), turn(high, -1)
+        high1, low3 = turn(high, 1), turn(low, -1)
+        low2, high2 = turn(low1, 1), turn(high3, -1)
         return (low, low1, low2, low3), (high, high1, high2, high3)
 
-    lows, highs = around(low, high)
+    def across(parts, sign):
+        moved = []
+        for step, part in enumerate(parts, 1):
+            moved.append(shift(part, WIDE, wide, sign * step))
+        return moved
+
+    def same(value, step):
+        return shift(value, CONTEXT, ring, step)
+
+    def mirrored(value, step):
+        pairs = [
+            (2 * at + side, 2 * ((at + step * (1 - 2 * side)) % ring) + side)
+            for at in range(ring)
+            for side in range(2)
+        ]
+        return lax.ppermute(value, (CONTEXT, CORE), pairs)
+
+    lows, highs = around(low, high, same)
     send, rest = call(
         merge_kernel,
         [((half, width), BF16), ((half, out_weight.shape[0]), BF16)],
@@ -468,9 +476,7 @@
     got = shift(send, CORE, 2, 1)
     (keep,) = call(keep_kernel, [((half, width), F32)], [rest, held_weight])
     own, *sends = call(add_kernel, split, [place, keep, got], scalars=1)
-    received = []
-    for step, part in enumerate(sends, 1):
-        received.append(shift(part, WIDE, wide, step))
+    received = across(sends, 1)
     chunk = [((deep, row_dev, width), BF16)]
     (summed,) = call(sum_kernel, chunk, [own, *received])
     mixed = lax.all_to_all(summed, DEEP, 0, 0, tiled=True)
@@ -487,9 +493,9 @@
         [place, near],
         scalars=1,
     )
-    parts = [shift(part, WIDE, wide, step) if step else part for step, part in enumerate(parts)]
+    parts = [parts[0]] + across(parts[1:], 1)
     low, send = call(sort_kernel, [((slots // 2, full), BF16)] * 2, parts)
-    lows, highs = around(low, shift(send, CORE, 2, 1))
+    lows, highs = around(low, shift(send, CORE, 2, 1), mirrored)
     weights = [norm_gain.reshape(ring, 1, width), gate_matrix[0], up_matrix[0]]
     sums = [((slots, hidden_units), F32)] * 2
     partial = call(own_kernel, sums, [place, lows[0], highs[0], *weights], scalars=1)
@@ -525,7 +531,7 @@
         [((share_slots, width), BF16)] * wide,
         [low, shift(high, CORE, 2, 1)],
     )
-    parts = [shift(part, WIDE, wide, -step) if step else part for step, part in enumerate(parts)]
+    parts = [parts[0]] + across(parts[1:], -1)
     (summed,) = call(spread_kernel, chunk, [pick, *parts])
     returned = lax.all_to_all(summed, DEEP, 0, 0, tiled=True)
     done = [((row_dev, width), BF16)]

time: 198 us -> 194 us (0.980)
  starting transfers between devices: 41.7 us -> 30.4 us
  waiting for transfers between devices: 92.8 us -> 101 us
    ppermute x0 -> x6, waiting for transfers between devices: none -> 60.6 us  [mirrored(): return lax.ppermute(value, (CONTEXT, CORE), pairs)]
    ppermute x30 -> x24, waiting for transfers between devices: 92.8 us -> 40.7 us  [shift(): lax.ppermute(value, axis, [(i, (i + step) % count) for i in range(count)])]
    ppermute x30 -> x24, starting transfers between devices: 41.7 us -> 26.7 us  [shift(): lax.ppermute(value, axis, [(i, (i + step) % count) for i in range(count)])]
    ppermute x0 -> x6, starting transfers between devices: none -> 3.63 us  [mirrored(): return lax.ppermute(value, (CONTEXT, CORE), pairs)]
    pallas_call x18 -> x17, Pallas kernels: 15.8 us -> 14.8 us  [call(): pl.pallas_call(kernel, out_shape=tuple((out(shape, dtype) for shape, dtyp...]
  transfers between devices with their start and end apart: 30 -> 30, of which waited for: 20 -> 21; matrix products, arithmetic and copies ran while one was open for 0% -> 0% of each run, Pallas kernels for 3% -> 3%
where the time goes in v7:
time: 194 us; the launch traced here: 193 us
  waiting for transfers between devices  101 us (52%)
  blocking collectives  45.9 us (24%)
  starting transfers between devices  30.4 us (16%)
  Pallas kernels  14.8 us (8%)
    ppermute x6, waiting for transfers between devices, mirrored(): return lax.ppermute(value, (CONTEXT, CORE), pairs)  60.6 us
    ppermute x24, waiting for transfers between devices, shift(): lax.ppermute(value, axis, [(i, (i + step) % count) for i in range(count)])  40.7 us
    ppermute x24, starting transfers between devices, shift(): lax.ppermute(value, axis, [(i, (i + step) % count) for i in range(count)])  26.7 us
    all_to_all x1, blocking collectives, local(): mixed = lax.all_to_all(summed, DEEP, 0, 0, tiled=True)  19.1 us
    pallas_call x17, Pallas kernels, call(): pl.pallas_call(kernel, out_shape=tuple((out(shape, dtype) for shape, dtyp...  14.8 us
    all_to_all x1, blocking collectives, local(): returned = lax.all_to_all(summed, DEEP, 0, 0, tiled=True)  14 us
    all_to_all x1, blocking collectives, local(): lax.all_to_all(payload, DEEP, 0, 0, tiled=True)  12.7 us
  transfers between devices with their start and end apart: 30, of which 21 were waited for; matrix products, arithmetic and copies ran while one was open for 0% of the time, Pallas kernels for 3%

profile of v7, /device:TPU:24, one launch (start us, length us, event | category | flops | bytes accessed | tf_op | source)
XLA Modules:
  0.0 192.7 jit_solution(4761782432020356691)
XLA Ops:
  0.0 3.8 %shard_map.154 = (bf16[144,512]{1,0:T(8,128)(2,1)S(1)}, bf16[144,512]{1,0:T(8,128)(2,1)S(1)}, bf16[256,1792]{1,0:T(8,128)(2,1)S(1)}) custom-call(s32[8]{0:T(128)S(1)} %compare_select_fusion.4.place, bf16[512,384]{1,0:T(8,128)(2,1)} %q_ref.1, bf16[2,128,512]{2,1,0:T(8,128)(2,1)} %kl_ref.1, bf16[2,512,128]{2,1,0:T(8,128)(2,1)} %vl_ref.1, ...), custom_call_target="tpu_custom_call" | custom-call | tf_op jit(solution)/shard_map/pallas_call | solution.py:354
  3.8 2.0 %collective-permute-start = (bf16[144,512]{1,0:T(8,128)(2,1)S(1)}, bf16[144,512]{1,0:T(8,128)(2,1)S(1)}, u32[]{:S(2)}, u32[]{:S(2)}) collective-permute-start(bf16[144,512]{1,0:T(8,128)(2,1)S(1)} %get-tuple-element.38.refs_0_), channel_id=1, source_target_pairs={{0,64},{64,128},{128,192},{192,0},{1,65},{65,129},{129,193},{193,1... | collective-permute-start | bytes 442376 | tf_op jit(solution)/shard_map/ppermute | solution.py:365
  5.9 0.7 collective-permute-start.2
  6.6 2.5 %collective-permute-start.3 = (bf16[144,512]{1,0:T(8,128)(2,1)S(1)}, bf16[144,512]{1,0:T(8,128)(2,1)S(1)}, u32[]{:S(2)}, u32[]{:S(2)}) collective-permute-start(bf16[144,512]{1,0:T(8,128)(2,1)S(1)} %get-tuple-element.39.refs_4_), channel_id=1, source_target_pairs={{0,64},{64,128},{128,192},{192,0},{1,65},{65,129},{129,193},{193,1... | collective-permute-start | bytes 442376 | tf_op jit(solution)/shard_map/ppermute | solution.py:365
  9.1 1.5 collective-permute-done.refs_1_
  10.6 1.8 collective-permute-start.1
  12.6 2.4 %collective-permute-done.2.refs_3_ = bf16[144,512]{1,0:T(8,128)(2,1)S(1)} collective-permute-done((bf16[144,512]{1,0:T(8,128)(2,1)S(1)}, bf16[144,512]{1,0:T(8,128)(2,1)S(1)}, u32[]{:S(2)}, u32[]{:S(2)}) %collective-permute-start.2) | collective-permute-done | bytes 147488 | tf_op jit(solution)/shard_map/ppermute | solution.py:365
  15.0 0.7 collective-permute-done.1.refs_2_
  15.8 2.9 %collective-permute-done.5.refs_6_ = bf16[144,512]{1,0:T(8,128)(2,1)S(1)} collective-permute-done((bf16[144,512]{1,0:T(8,128)(2,1)S(1)}, bf16[144,512]{1,0:T(8,128)(2,1)S(1)}, u32[]{:S(2)}, u32[]{:S(2)}) %collective-permute-start.5) | collective-permute-done | bytes 147488 | tf_op jit(solution)/shard_map/ppermute | solution.py:365
  18.7 1.3 shard_map.155
  20.6 2.0 %collective-permute-done.6.got_ref = bf16[256,1792]{1,0:T(8,128)(2,1)S(1)} collective-permute-done((bf16[256,1792]{1,0:T(8,128)(2,1)S(1)}, bf16[256,1792]{1,0:T(8,128)(2,1)S(1)}, u32[]{:S(2)}, u32[]{:S(2)}) %collective-permute-start.6) | collective-permute-done | bytes 917536 | tf_op jit(solution)/shard_map/ppermute | solution.py:365
  23.3 1.2 collective-permute-start.7
  24.5 2.7 %collective-permute-start.8 = (bf16[64,1792]{1,0:T(8,128)(2,1)S(1)}, bf16[64,1792]{1,0:T(8,128)(2,1)S(1)}, u32[]{:S(2)}, u32[]{:S(2)}) collective-permute-start(bf16[64,1792]{1,0:T(8,128)(2,1)S(1)} %get-tuple-element.45), channel_id=1, source_target_pairs={{0,32},{16,48},{32,0},{48,16},{1,33},{17,49},{33,1},{49,17},{2,34}... | collective-permute-start | bytes 688136 | tf_op jit(solution)/shard_map/ppermute | solution.py:365
  27.3 1.4 collective-permute-start.9
  28.7 3.7 %collective-permute-done.7.refs_0_ = bf16[64,1792]{1,0:T(8,128)(2,1)S(1)} collective-permute-done((bf16[64,1792]{1,0:T(8,128)(2,1)S(1)}, bf16[64,1792]{1,0:T(8,128)(2,1)S(1)}, u32[]{:S(2)}, u32[]{:S(2)}) %collective-permute-start.7) | collective-permute-done | bytes 229408 | tf_op jit(solution)/shard_map/ppermute | solution.py:365
  32.4 5.4 %collective-permute-done.8.refs_1_ = bf16[64,1792]{1,0:T(8,128)(2,1)S(1)} collective-permute-done((bf16[64,1792]{1,0:T(8,128)(2,1)S(1)}, bf16[64,1792]{1,0:T(8,128)(2,1)S(1)}, u32[]{:S(2)}, u32[]{:S(2)}) %collective-permute-start.8) | collective-permute-done | bytes 229408 | tf_op jit(solution)/shard_map/ppermute | solution.py:365
  37.9 19.1 %all_to_all.15.parts_ref = bf16[8,8,1792]{2,1,0:T(8,128)(2,1)S(1)} all-to-all(bf16[8,8,1792]{2,1,0:T(8,128)(2,1)S(1)} %shard_map.158), channel_id=1, replica_groups=mesh['context'=4,'x'=4,'z'=8,'core'=2] {'z'}, dimensions={0} | all-to-all | bytes 458752 | tf_op jit(solution)/shard_map/all_to_all | solution.py:482
  57.2 12.7 %all_to_all.16 = bf16[8,8,1920]{2,1,0:T(8,128)(2,1)S(1)} all-to-all(bf16[8,8,1920]{2,1,0:T(8,128)(2,1)S(1)} %get-tuple-element.47), channel_id=1, replica_groups=mesh['context'=4,'x'=4,'z'=8,'core'=2] {'z'}, dimensions={0} | all-to-all | bytes 491520 | tf_op jit(solution)/shard_map/all_to_all | solution.py:488
  69.9 1.4 shard_map.160
  71.4 1.7 collective-permute-start.10
  73.0 3.1 %collective-permute-start.11 = (bf16[48,1920]{1,0:T(8,128)(2,1)S(1)}, bf16[48,1920]{1,0:T(8,128)(2,1)S(1)}, u32[]{:S(2)}, u32[]{:S(2)}) collective-permute-start(bf16[48,1920]{1,0:T(8,128)(2,1)S(1)} %get-tuple-element.51), channel_id=1, source_target_pairs={{0,32},{16,48},{32,0},{48,16},{1,33},{17,49},{33,1},{49,17},{2,34}... | collective-permute-start | bytes 552968 | tf_op jit(solution)/shard_map/ppermute | solution.py:365
  76.7 3.3 %collective-permute-done.10.refs_1_ = bf16[48,1920]{1,0:T(8,128)(2,1)S(1)} collective-permute-done((bf16[48,1920]{1,0:T(8,128)(2,1)S(1)}, bf16[48,1920]{1,0:T(8,128)(2,1)S(1)}, u32[]{:S(2)}, u32[]{:S(2)}) %collective-permute-start.10) | collective-permute-done | bytes 184352 | tf_op jit(solution)/shard_map/ppermute | solution.py:365
  80.0 2.0 %collective-permute-done.11.refs_2_ = bf16[48,1920]{1,0:T(8,128)(2,1)S(1)} collective-permute-done((bf16[48,1920]{1,0:T(8,128)(2,1)S(1)}, bf16[48,1920]{1,0:T(8,128)(2,1)S(1)}, u32[]{:S(2)}, u32[]{:S(2)}) %collective-permute-start.11) | collective-permute-done | bytes 184352 | tf_op jit(solution)/shard_map/ppermute | solution.py:365
  82.3 1.9 collective-permute-start.16
  84.2 0.7 shard_map.165
  84.9 1.5 collective-permute-start.22
  87.0 0.9 collective-permute-start.25
  87.9 5.7 %collective-permute-done.14.low1 = bf16[96,1920]{1,0:T(8,128)(2,1)S(1)} collective-permute-done((bf16[96,1920]{1,0:T(8,128)(2,1)S(1)}, bf16[96,1920]{1,0:T(8,128)(2,1)S(1)}, u32[]{:S(2)}, u32[]{:S(2)}) %collective-permute-start.14) | collective-permute-done | bytes 368672 | tf_op jit(solution)/shard_map/ppermute | solution.py:456
  93.6 1.4 collective-permute-done.16.low3
  95.7 44.7 %collective-permute-done.15.high1 = bf16[96,1920]{1,0:T(8,128)(2,1)S(1)} collective-permute-done((bf16[96,1920]{1,0:T(8,128)(2,1)S(1)}, bf16[96,1920]{1,0:T(8,128)(2,1)S(1)}, u32[]{:S(2)}, u32[]{:S(2)}) %collective-permute-start.15) | collective-permute-done | bytes 368672 | tf_op jit(solution)/shard_map/ppermute | solution.py:456
  140.4 1.2 collective-permute-done.17.high3
  141.5 0.9 collective-permute-start.19
  142.4 1.1 shard_map.162
  143.5 1.5 shard_map.163
  145.0 6.5 %collective-permute-done.18.low2 = bf16[96,1920]{1,0:T(8,128)(2,1)S(1)} collective-permute-done((bf16[96,1920]{1,0:T(8,128)(2,1)S(1)}, bf16[96,1920]{1,0:T(8,128)(2,1)S(1)}, u32[]{:S(2)}, u32[]{:S(2)}) %collective-permute-start.18) | collective-permute-done | bytes 368672 | tf_op jit(solution)/shard_map/ppermute | solution.py:456
  151.4 1.2 collective-permute-done.19.high2
  152.6 1.1 shard_map.164.active0
  153.8 2.0 %collective-permute-start.21 = (bf16[192,256]{1,0:T(8,128)(2,1)S(1)}, bf16[192,256]{1,0:T(8,128)(2,1)S(1)}, u32[]{:S(2)}, u32[]{:S(2)}) collective-permute-start(bf16[192,256]{1,0:T(8,128)(2,1)S(1)} %shard_map.164.active0), channel_id=1, source_target_pairs={{0,192},{64,0},{128,64},{192,128},{1,193},{65,1},{129,65},{193,129... | collective-permute-start | bytes 294920 | tf_op jit(solution)/shard_map/ppermute | solution.py:365
  155.9 2.9 %collective-permute-done.20.active1 = bf16[192,256]{1,0:T(8,128)(2,1)S(1)} collective-permute-done((bf16[192,256]{1,0:T(8,128)(2,1)S(1)}, bf16[192,256]{1,0:T(8,128)(2,1)S(1)}, u32[]{:S(2)}, u32[]{:S(2)}) %collective-permute-start.20) | collective-permute-done | bytes 98336 | tf_op jit(solution)/shard_map/ppermute | solution.py:365
  158.7 2.0 %collective-permute-done.21.active3 = bf16[192,256]{1,0:T(8,128)(2,1)S(1)} collective-permute-done((bf16[192,256]{1,0:T(8,128)(2,1)S(1)}, bf16[192,256]{1,0:T(8,128)(2,1)S(1)}, u32[]{:S(2)}, u32[]{:S(2)}) %collective-permute-start.21) | collective-permute-done | bytes 98336 | tf_op jit(solution)/shard_map/ppermute | solution.py:365
  160.8 1.2 shard_map.166.sum_ref
  162.5 1.6 collective-permute-done.26.got_ref
  164.2 2.2 %collective-permute-start.27 = (bf16[48,1792]{1,0:T(8,128)(2,1)S(1)}, bf16[48,1792]{1,0:T(8,128)(2,1)S(1)}, u32[]{:S(2)}, u32[]{:S(2)}) collective-permute-start(bf16[48,1792]{1,0:T(8,128)(2,1)S(1)} %get-tuple-element.67), channel_id=1, source_target_pairs={{0,48},{16,0},{32,16},{48,32},{1,49},{17,1},{33,17},{49,33},{2,50}... | collective-permute-start | bytes 516104 | tf_op jit(solution)/shard_map/ppermute | solution.py:365
  166.4 1.0 collective-permute-start.28
  167.4 6.7 %collective-permute-done.27.refs_1_ = bf16[48,1792]{1,0:T(8,128)(2,1)S(1)} collective-permute-done((bf16[48,1792]{1,0:T(8,128)(2,1)S(1)}, bf16[48,1792]{1,0:T(8,128)(2,1)S(1)}, u32[]{:S(2)}, u32[]{:S(2)}) %collective-permute-start.27) | collective-permute-done | bytes 172064 | tf_op jit(solution)/shard_map/ppermute | solution.py:365
  174.1 1.1 collective-permute-done.28.refs_2_
  175.2 2.5 %collective-permute-done.29.refs_3_ = bf16[48,1792]{1,0:T(8,128)(2,1)S(1)} collective-permute-done((bf16[48,1792]{1,0:T(8,128)(2,1)S(1)}, bf16[48,1792]{1,0:T(8,128)(2,1)S(1)}, u32[]{:S(2)}, u32[]{:S(2)}) %collective-permute-start.29) | collective-permute-done | bytes 172064 | tf_op jit(solution)/shard_map/ppermute | solution.py:365
  178.0 14.0 %all_to_all.17.parts_ref = bf16[8,8,1792]{2,1,0:T(8,128)(2,1)S(1)} all-to-all(bf16[8,8,1792]{2,1,0:T(8,128)(2,1)S(1)} %shard_map.169), channel_id=1, replica_groups=mesh['context'=4,'x'=4,'z'=8,'core'=2] {'z'}, dimensions={0} | all-to-all | bytes 458752 | tf_op jit(solution)/shard_map/all_to_all | solution.py:536
  (47 shorter events, 5.6 us)
Async XLA Ops:
  3.8 6.8 %collective-permute-start = (bf16[144,512]{1,0:T(8,128)(2,1)S(1)}, bf16[144,512]{1,0:T(8,128)(2,1)S(1)}, u32[]{:S(2)}, u32[]{:S(2)}) collective-permute-start(bf16[144,512]{1,0:T(8,128)(2,1)S(1)} %get-tuple-element.38.refs_0_), channel_id=1, source_target_pairs={{0,64},{64,128},{128,192},{192,0},{1,65},{65,129},{129,193},{193,1... | collective-permute-start | bytes 442376 | tf_op jit(solution)/shard_map/ppermute | solution.py:365
  5.8 6.6 %collective-permute-start.4 = (bf16[144,512]{1,0:T(8,128)(2,1)S(1)}, bf16[144,512]{1,0:T(8,128)(2,1)S(1)}, u32[]{:S(2)}, u32[]{:S(2)}) collective-permute-start(bf16[144,512]{1,0:T(8,128)(2,1)S(1)} %get-tuple-element.39.refs_4_), channel_id=1, source_target_pairs={{0,192},{64,0},{128,64},{192,128},{1,193},{65,1},{129,65},{193,129... | collective-permute-start | bytes 442376 | tf_op jit(solution)/shard_map/ppermute | solution.py:365
  5.9 9.1 %collective-permute-start.2 = (bf16[144,512]{1,0:T(8,128)(2,1)S(1)}, bf16[144,512]{1,0:T(8,128)(2,1)S(1)}, u32[]{:S(2)}, u32[]{:S(2)}) collective-permute-start(bf16[144,512]{1,0:T(8,128)(2,1)S(1)} %get-tuple-element.38.refs_0_), channel_id=1, source_target_pairs={{0,192},{64,0},{128,64},{192,128},{1,193},{65,1},{129,65},{193,129... | collective-permute-start | bytes 442376 | tf_op jit(solution)/shard_map/ppermute | solution.py:365
  6.6 8.4 %collective-permute-start.3 = (bf16[144,512]{1,0:T(8,128)(2,1)S(1)}, bf16[144,512]{1,0:T(8,128)(2,1)S(1)}, u32[]{:S(2)}, u32[]{:S(2)}) collective-permute-start(bf16[144,512]{1,0:T(8,128)(2,1)S(1)} %get-tuple-element.39.refs_4_), channel_id=1, source_target_pairs={{0,64},{64,128},{128,192},{192,0},{1,65},{65,129},{129,193},{193,1... | collective-permute-start | bytes 442376 | tf_op jit(solution)/shard_map/ppermute | solution.py:365
  10.6 5.2 %collective-permute-start.1 = (bf16[144,512]{1,0:T(8,128)(2,1)S(1)}, bf16[144,512]{1,0:T(8,128)(2,1)S(1)}, u32[]{:S(2)}, u32[]{:S(2)}) collective-permute-start(bf16[144,512]{1,0:T(8,128)(2,1)S(1)} %collective-permute-done.refs_1_), channel_id=1, source_target_pairs={{0,64},{64,128},{128,192},{192,0},{1,65},{65,129},{129,193},{193,1... | collective-permute-start | bytes 442376 | tf_op jit(solution)/shard_map/ppermute | solution.py:365
  12.4 6.4 %collective-permute-start.5 = (bf16[144,512]{1,0:T(8,128)(2,1)S(1)}, bf16[144,512]{1,0:T(8,128)(2,1)S(1)}, u32[]{:S(2)}, u32[]{:S(2)}) collective-permute-start(bf16[144,512]{1,0:T(8,128)(2,1)S(1)} %collective-permute-done.4.refs_7_), channel_id=1, source_target_pairs={{0,192},{64,0},{128,64},{192,128},{1,193},{65,1},{129,65},{193,129... | collective-permute-start | bytes 442376 | tf_op jit(solution)/shard_map/ppermute | solution.py:365
  20.0 2.6 %collective-permute-start.6 = (bf16[256,1792]{1,0:T(8,128)(2,1)S(1)}, bf16[256,1792]{1,0:T(8,128)(2,1)S(1)}, u32[]{:S(2)}, u32[]{:S(2)}) collective-permute-start(bf16[256,1792]{1,0:T(8,128)(2,1)S(1)} %get-tuple-element.42.after_ref), channel_id=1, source_target_pairs={{0,1},{1,0},{2,3},{3,2},{4,5},{5,4},{6,7},{7,6},{8,9},{9,8},{10,11... | collective-permute-start | bytes 2752520 | tf_op jit(solution)/shard_map/ppermute | solution.py:365
  20.1 37.0 %copy-start.4 = (bf16[8,1792]{1,0:T(8,128)(2,1)S(1)}, bf16[8,1792]{1,0:T(8,128)(2,1)}, u32[]{:S(2)}) copy-start(bf16[8,1792]{1,0:T(8,128)(2,1)} %residual_ref.1) | copy-start | bytes 86020
  20.1 36.9 %copy-start.5 = (s32[8,8]{1,0:T(8,128)S(1)}, s32[8,8]{1,0:T(8,128)}, u32[]{:S(2)}) copy-start(s32[8,8]{1,0:T(8,128)} %ids_ref.1) | copy-start | bytes 772
  20.2 36.9 %copy-start.6 = (f32[8,8]{1,0:T(8,128)S(1)}, f32[8,8]{1,0:T(8,128)}, u32[]{:S(2)}) copy-start(f32[8,8]{1,0:T(8,128)} %weights_ref.1) | copy-start | bytes 772
  20.2 64.0 %copy-start.2 = (bf16[1,256,7168]{2,1,0:T(8,128)(2,1)S(1)}, bf16[1,256,7168]{2,1,0:T(8,128)(2,1)}, u32[]{:S(2)}) copy-start(bf16[1,256,7168]{2,1,0:T(8,128)(2,1)} %param.31) | copy-start | bytes 11010052
  23.3 9.1 %collective-permute-start.7 = (bf16[64,1792]{1,0:T(8,128)(2,1)S(1)}, bf16[64,1792]{1,0:T(8,128)(2,1)S(1)}, u32[]{:S(2)}, u32[]{:S(2)}) collective-permute-start(bf16[64,1792]{1,0:T(8,128)(2,1)S(1)} %get-tuple-element.44), channel_id=1, source_target_pairs={{0,16},{16,32},{32,48},{48,0},{1,17},{17,33},{33,49},{49,1},{2,18}... | collective-permute-start | bytes 688136 | tf_op jit(solution)/shard_map/ppermute | solution.py:365
  24.5 13.3 %collective-permute-start.8 = (bf16[64,1792]{1,0:T(8,128)(2,1)S(1)}, bf16[64,1792]{1,0:T(8,128)(2,1)S(1)}, u32[]{:S(2)}, u32[]{:S(2)}) collective-permute-start(bf16[64,1792]{1,0:T(8,128)(2,1)S(1)} %get-tuple-element.45), channel_id=1, source_target_pairs={{0,32},{16,48},{32,0},{48,16},{1,33},{17,49},{33,1},{49,17},{2,34}... | collective-permute-start | bytes 688136 | tf_op jit(solution)/shard_map/ppermute | solution.py:365
  27.3 10.5 %collective-permute-start.9 = (bf16[64,1792]{1,0:T(8,128)(2,1)S(1)}, bf16[64,1792]{1,0:T(8,128)(2,1)S(1)}, u32[]{:S(2)}, u32[]{:S(2)}) collective-permute-start(bf16[64,1792]{1,0:T(8,128)(2,1)S(1)} %get-tuple-element.46), channel_id=1, source_target_pairs={{0,48},{16,0},{32,16},{48,32},{1,49},{17,1},{33,17},{49,33},{2,50}... | collective-permute-start | bytes 688136 | tf_op jit(solution)/shard_map/ppermute | solution.py:365
  37.8 104.6 %copy-start.1 = (bf16[1,7168,256]{2,1,0:T(8,128)(2,1)S(1)}, bf16[1,7168,256]{2,1,0:T(8,128)(2,1)}, u32[]{:S(2)}) copy-start(bf16[1,7168,256]{2,1,0:T(8,128)(2,1)} %param.30) | copy-start | bytes 11010052
  37.9 104.5 %copy-start = (bf16[1,7168,256]{2,1,0:T(8,128)(2,1)S(1)}, bf16[1,7168,256]{2,1,0:T(8,128)(2,1)}, u32[]{:S(2)}) copy-start(bf16[1,7168,256]{2,1,0:T(8,128)(2,1)} %param.29) | copy-start | bytes 11010052
  37.9 104.5 %copy-start.3 = (f32[7168]{0:T(1024)S(1)}, f32[7168]{0:T(1024)}, u32[]{:S(2)}) copy-start(f32[7168]{0:T(1024)} %param.26) | copy-start | bytes 86020
  71.4 8.6 %collective-permute-start.10 = (bf16[48,1920]{1,0:T(8,128)(2,1)S(1)}, bf16[48,1920]{1,0:T(8,128)(2,1)S(1)}, u32[]{:S(2)}, u32[]{:S(2)}) collective-permute-start(bf16[48,1920]{1,0:T(8,128)(2,1)S(1)} %get-tuple-element.50), channel_id=1, source_target_pairs={{0,16},{16,32},{32,48},{48,0},{1,17},{17,33},{33,49},{49,1},{2,18}... | collective-permute-start | bytes 552968 | tf_op jit(solution)/shard_map/ppermute | solution.py:365
  73.0 8.9 %collective-permute-start.11 = (bf16[48,1920]{1,0:T(8,128)(2,1)S(1)}, bf16[48,1920]{1,0:T(8,128)(2,1)S(1)}, u32[]{:S(2)}, u32[]{:S(2)}) collective-permute-start(bf16[48,1920]{1,0:T(8,128)(2,1)S(1)} %get-tuple-element.51), channel_id=1, source_target_pairs={{0,32},{16,48},{32,0},{48,16},{1,33},{17,49},{33,1},{49,17},{2,34}... | collective-permute-start | bytes 552968 | tf_op jit(solution)/shard_map/ppermute | solution.py:365
  76.1 5.8 %collective-permute-start.12 = (bf16[48,1920]{1,0:T(8,128)(2,1)S(1)}, bf16[48,1920]{1,0:T(8,128)(2,1)S(1)}, u32[]{:S(2)}, u32[]{:S(2)}) collective-permute-start(bf16[48,1920]{1,0:T(8,128)(2,1)S(1)} %get-tuple-element.52), channel_id=1, source_target_pairs={{0,48},{16,0},{32,16},{48,32},{1,49},{17,1},{33,17},{49,33},{2,50}... | collective-permute-start | bytes 552968 | tf_op jit(solution)/shard_map/ppermute | solution.py:365
  82.0 5.0 %collective-permute-start.13 = (bf16[96,1920]{1,0:T(8,128)(2,1)S(1)}, bf16[96,1920]{1,0:T(8,128)(2,1)S(1)}, u32[]{:S(2)}, u32[]{:S(2)}) collective-permute-start(bf16[96,1920]{1,0:T(8,128)(2,1)S(1)} %get-tuple-element.54), channel_id=1, source_target_pairs={{0,1},{1,0},{2,3},{3,2},{4,5},{5,4},{6,7},{7,6},{8,9},{9,8},{10,11... | collective-permute-start | bytes 1105928 | tf_op jit(solution)/shard_map/ppermute | solution.py:365
  82.1 11.5 %collective-permute-start.14 = (bf16[96,1920]{1,0:T(8,128)(2,1)S(1)}, bf16[96,1920]{1,0:T(8,128)(2,1)S(1)}, u32[]{:S(2)}, u32[]{:S(2)}) collective-permute-start(bf16[96,1920]{1,0:T(8,128)(2,1)S(1)} %get-tuple-element.53.low_ref.low0), channel_id=1, source_target_pairs={{0,64},{1,193},{64,128},{65,1},{128,192},{129,65},{192,0},{193,129... | collective-permute-start | bytes 1105928 | tf_op jit(solution)/shard_map/ppermute | solution.py:456
  82.3 12.7 %collective-permute-start.16 = (bf16[96,1920]{1,0:T(8,128)(2,1)S(1)}, bf16[96,1920]{1,0:T(8,128)(2,1)S(1)}, u32[]{:S(2)}, u32[]{:S(2)}) collective-permute-start(bf16[96,1920]{1,0:T(8,128)(2,1)S(1)} %get-tuple-element.53.low_ref.low0), channel_id=1, source_target_pairs={{0,192},{1,65},{64,0},{65,129},{128,64},{129,193},{192,128},{193,1... | collective-permute-start | bytes 1105928 | tf_op jit(solution)/shard_map/ppermute | solution.py:456
  84.9 70.9 %collective-permute-start.22 = (bf16[256,1792]{1,0:T(8,128)(2,1)S(1)}, bf16[256,1792]{1,0:T(8,128)(2,1)S(1)}, u32[]{:S(2)}, u32[]{:S(2)}) collective-permute-start(bf16[256,1792]{1,0:T(8,128)(2,1)S(1)} %get-tuple-element.60), channel_id=1, source_target_pairs={{0,64},{64,128},{128,192},{192,0},{1,65},{65,129},{129,193},{193,1... | collective-permute-start | bytes 2752520 | tf_op jit(solution)/shard_map/ppermute | solution.py:365
  86.4 69.5 %collective-permute-start.23 = (bf16[256,1792]{1,0:T(8,128)(2,1)S(1)}, bf16[256,1792]{1,0:T(8,128)(2,1)S(1)}, u32[]{:S(2)}, u32[]{:S(2)}) collective-permute-start(bf16[256,1792]{1,0:T(8,128)(2,1)S(1)} %get-tuple-element.61), channel_id=1, source_target_pairs={{0,192},{64,0},{128,64},{192,128},{1,193},{65,1},{129,65},{193,129... | collective-permute-start | bytes 2752520 | tf_op jit(solution)/shard_map/ppermute | solution.py:365
  87.0 75.0 %collective-permute-start.25 = (bf16[256,1792]{1,0:T(8,128)(2,1)S(1)}, bf16[256,1792]{1,0:T(8,128)(2,1)S(1)}, u32[]{:S(2)}, u32[]{:S(2)}) collective-permute-start(bf16[256,1792]{1,0:T(8,128)(2,1)S(1)} %get-tuple-element.62), channel_id=1, source_target_pairs={{0,128},{64,192},{128,0},{192,64},{1,129},{65,193},{129,1},{193,65... | collective-permute-start | bytes 2752520 | tf_op jit(solution)/shard_map/ppermute | solution.py:365
  93.6 46.7 %collective-permute-start.15 = (bf16[96,1920]{1,0:T(8,128)(2,1)S(1)}, bf16[96,1920]{1,0:T(8,128)(2,1)S(1)}, u32[]{:S(2)}, u32[]{:S(2)}) collective-permute-start(bf16[96,1920]{1,0:T(8,128)(2,1)S(1)} %collective-permute-done.13.high_ref.high0), channel_id=1, source_target_pairs={{0,64},{1,193},{64,128},{65,1},{128,192},{129,65},{192,0},{193,129... | collective-permute-start | bytes 1105928 | tf_op jit(solution)/shard_map/ppermute | solution.py:456
  95.0 46.5 %collective-permute-start.17 = (bf16[96,1920]{1,0:T(8,128)(2,1)S(1)}, bf16[96,1920]{1,0:T(8,128)(2,1)S(1)}, u32[]{:S(2)}, u32[]{:S(2)}) collective-permute-start(bf16[96,1920]{1,0:T(8,128)(2,1)S(1)} %collective-permute-done.13.high_ref.high0), channel_id=1, source_target_pairs={{0,192},{1,65},{64,0},{65,129},{128,64},{129,193},{192,128},{193,1... | collective-permute-start | bytes 1105928 | tf_op jit(solution)/shard_map/ppermute | solution.py:456
  140.4 11.1 %collective-permute-start.18 = (bf16[96,1920]{1,0:T(8,128)(2,1)S(1)}, bf16[96,1920]{1,0:T(8,128)(2,1)S(1)}, u32[]{:S(2)}, u32[]{:S(2)}) collective-permute-start(bf16[96,1920]{1,0:T(8,128)(2,1)S(1)} %collective-permute-done.14.low1), channel_id=1, source_target_pairs={{0,64},{1,193},{64,128},{65,1},{128,192},{129,65},{192,0},{193,129... | collective-permute-start | bytes 1105928 | tf_op jit(solution)/shard_map/ppermute | solution.py:456
  141.5 11.1 %collective-permute-start.19 = (bf16[96,1920]{1,0:T(8,128)(2,1)S(1)}, bf16[96,1920]{1,0:T(8,128)(2,1)S(1)}, u32[]{:S(2)}, u32[]{:S(2)}) collective-permute-start(bf16[96,1920]{1,0:T(8,128)(2,1)S(1)} %collective-permute-done.17.high3), channel_id=1, source_target_pairs={{0,192},{1,65},{64,0},{65,129},{128,64},{129,193},{192,128},{193,1... | collective-permute-start | bytes 1105928 | tf_op jit(solution)/shard_map/ppermute | solution.py:456
  153.8 5.0 %collective-permute-start.20 = (bf16[192,256]{1,0:T(8,128)(2,1)S(1)}, bf16[192,256]{1,0:T(8,128)(2,1)S(1)}, u32[]{:S(2)}, u32[]{:S(2)}) collective-permute-start(bf16[192,256]{1,0:T(8,128)(2,1)S(1)} %shard_map.164.active0), channel_id=1, source_target_pairs={{0,64},{64,128},{128,192},{192,0},{1,65},{65,129},{129,193},{193,1... | collective-permute-start | bytes 294920 | tf_op jit(solution)/shard_map/ppermute | solution.py:365
  153.8 6.9 %collective-permute-start.21 = (bf16[192,256]{1,0:T(8,128)(2,1)S(1)}, bf16[192,256]{1,0:T(8,128)(2,1)S(1)}, u32[]{:S(2)}, u32[]{:S(2)}) collective-permute-start(bf16[192,256]{1,0:T(8,128)(2,1)S(1)} %shard_map.164.active0), channel_id=1, source_target_pairs={{0,192},{64,0},{128,64},{192,128},{1,193},{65,1},{129,65},{193,129... | collective-permute-start | bytes 294920 | tf_op jit(solution)/shard_map/ppermute | solution.py:365
  155.9 6.2 %collective-permute-start.24 = (bf16[192,256]{1,0:T(8,128)(2,1)S(1)}, bf16[192,256]{1,0:T(8,128)(2,1)S(1)}, u32[]{:S(2)}, u32[]{:S(2)}) collective-permute-start(bf16[192,256]{1,0:T(8,128)(2,1)S(1)} %shard_map.164.active0), channel_id=1, source_target_pairs={{0,128},{64,192},{128,0},{192,64},{1,129},{65,193},{129,1},{193,65... | collective-permute-start | bytes 294920 | tf_op jit(solution)/shard_map/ppermute | solution.py:365
  162.4 1.7 collective-permute-start.26
  164.2 9.9 %collective-permute-start.27 = (bf16[48,1792]{1,0:T(8,128)(2,1)S(1)}, bf16[48,1792]{1,0:T(8,128)(2,1)S(1)}, u32[]{:S(2)}, u32[]{:S(2)}) collective-permute-start(bf16[48,1792]{1,0:T(8,128)(2,1)S(1)} %get-tuple-element.67), channel_id=1, source_target_pairs={{0,48},{16,0},{32,16},{48,32},{1,49},{17,1},{33,17},{49,33},{2,50}... | collective-permute-start | bytes 516104 | tf_op jit(solution)/shard_map/ppermute | solution.py:365
  166.4 8.8 %collective-permute-start.28 = (bf16[48,1792]{1,0:T(8,128)(2,1)S(1)}, bf16[48,1792]{1,0:T(8,128)(2,1)S(1)}, u32[]{:S(2)}, u32[]{:S(2)}) collective-permute-start(bf16[48,1792]{1,0:T(8,128)(2,1)S(1)} %get-tuple-element.68), channel_id=1, source_target_pairs={{0,32},{16,48},{32,0},{48,16},{1,33},{17,49},{33,1},{49,17},{2,34}... | collective-permute-start | bytes 516104 | tf_op jit(solution)/shard_map/ppermute | solution.py:365
  167.4 10.3 %collective-permute-start.29 = (bf16[48,1792]{1,0:T(8,128)(2,1)S(1)}, bf16[48,1792]{1,0:T(8,128)(2,1)S(1)}, u32[]{:S(2)}, u32[]{:S(2)}) collective-permute-start(bf16[48,1792]{1,0:T(8,128)(2,1)S(1)} %get-tuple-element.69), channel_id=1, source_target_pairs={{0,16},{16,32},{32,48},{48,0},{1,17},{17,33},{33,49},{49,1},{2,18}... | collective-permute-start | bytes 516104 | tf_op jit(solution)/shard_map/ppermute | solution.py:365
